TPU v7x, 128 devices: a whole 4x4x4 slice. The times are simulated.
128 devices in a mesh: tm: 32 (over z, y, core), chan: 4 (over x).
Axes of the slice: x: 4, y: 4, z: 4, core: 2. Of those that a mesh axis runs over, the one named last changes fastest.
Arguments:
- coarse: bfloat16 [2, 98304, 4096], P(None, 'tm', 'chan'), may hold values from -6 to 6
- prototype: float32 [16, 1024], replicated, may hold values from -4 to 4
- req_block: int32 [4, 4], replicated, may hold values from 0 to 31, as said below
- req_start: int32 [4, 4], replicated, may hold values from 0 to 80, as said below
- req_frames: int32 [4, 4], replicated, may hold values from 1 to 81
- req_count: int32 [4], replicated, may hold values from 1 to 4, as said below
Outputs:
- spectra: bfloat16 [96, 4, 4, 2, 1024, 128], P('tm', 'chan')
Inputs may be any that keep to these rules, and one draw needn't show every extreme that they name: `req_block`: among the live slots of one owner at most 2 name blocks b with the same b // 8; in every draw some owner reaches 2. req_start + req_frames <= 81 in every slot; in every draw some live slot starts at hop 81 - 1 and some live slot spans all 81 frames. Slots q < req_count[c] of owner c are live, the others are empty; in every draw some owner has 4 live slots.
All inputs are finite; a program needn't handle non-finite values.
Results may differ from a plain program's by a relative error of at most 0.001.
Values may be sent and summed in bfloat16 or wider, within the bound.
No kernel may reach another device: no remote copies, remote signals or barrier semaphores. Data moves between devices by JAX's collectives and lax.ppermute only.
A program may use at most 256 MiB of HBM per device.

v0:
```python
import math

import jax
import jax.numpy as jnp
from jax import lax
from jax.sharding import PartitionSpec as P

BLOCKW = 128
NFINE = 1024
TAPS = 16
HOPS_DEV = 3
MAXREQ = 4
PAIR = 2


def build_table():
    index_line = jnp.arange(NFINE, dtype=jnp.int32)
    products = index_line[:, None] * index_line[None, :] % NFINE
    angles = products.astype(jnp.float32) * (2.0 * math.pi / NFINE)
    cosine = jnp.cos(angles) / math.sqrt(NFINE)
    sine = jnp.sin(angles) / math.sqrt(NFINE)
    upper = jnp.concatenate([cosine, sine], axis=1)
    lower = jnp.concatenate([-sine, cosine], axis=1)
    return jnp.concatenate([upper, lower], axis=0)


def shards(coarse, prototype, req_block, req_start, req_frames, req_count):
    owners = lax.axis_size("chan")
    column = lax.axis_index("chan")
    row_index = lax.axis_index("tm")
    time_devices = lax.axis_size("tm")
    per_column = coarse.shape[2] // BLOCKW
    coarse_data = coarse.reshape(2, HOPS_DEV, NFINE, per_column, BLOCKW)
    slot_ids = jnp.arange(MAXREQ, dtype=jnp.int32)
    is_live = slot_ids[None, :] < req_count[:, None]
    sources = req_block // per_column
    is_mine = is_live & (sources == column)
    ranking = jnp.cumsum(is_mine.astype(jnp.int32), axis=1) - 1
    pair_ids = jnp.arange(PAIR, dtype=jnp.int32)
    picked = is_mine[:, None, :] & (ranking[:, None, :] == pair_ids[None, :, None])
    local_ids = req_block - column * per_column
    block_ids = jnp.arange(per_column, dtype=jnp.int32)
    matches = picked[:, :, :, None] & (
        local_ids[:, None, :, None] == block_ids[None, None, None, :]
    )
    chooser = jnp.any(matches, axis=2).astype(jnp.bfloat16)
    outgoing = jnp.einsum(
        "dpb,xhkbc->dpxhkc", chooser, coarse_data, preferred_element_type=jnp.float32
    ).astype(jnp.bfloat16)
    incoming = lax.all_to_all(outgoing, "chan", split_axis=0, concat_axis=0, tiled=True)
    owner_ids = jnp.arange(owners, dtype=jnp.int32)
    row_pick = owner_ids == column
    my_block = jnp.sum(jnp.where(row_pick[:, None], req_block, 0), axis=0)
    my_start = jnp.sum(jnp.where(row_pick[:, None], req_start, 0), axis=0)
    my_frames = jnp.sum(jnp.where(row_pick[:, None], req_frames, 0), axis=0)
    my_count = jnp.sum(jnp.where(row_pick, req_count, 0))
    my_live = slot_ids < my_count
    my_source = my_block // per_column
    earlier = (
        my_live[:, None]
        & my_live[None, :]
        & (my_source[:, None] == my_source[None, :])
        & (slot_ids[None, :] < slot_ids[:, None])
    )
    my_rank = jnp.sum(earlier.astype(jnp.int32), axis=1)
    arrival = my_source * PAIR + my_rank
    taker = (
        my_live[:, None] & (arrival[:, None] == jnp.arange(owners * PAIR, dtype=jnp.int32)[None, :])
    ).astype(jnp.bfloat16)
    arrived = incoming.reshape(owners * PAIR, 2, HOPS_DEV, NFINE, BLOCKW)
    slots = jnp.einsum(
        "qs,sxhkc->qxhkc", taker, arrived, preferred_element_type=jnp.float32
    ).astype(jnp.bfloat16)
    hop_ids = row_index * HOPS_DEV + jnp.arange(HOPS_DEV, dtype=jnp.int32)
    active = (
        my_live[:, None]
        & (hop_ids[None, :] >= my_start[:, None])
        & (hop_ids[None, :] < (my_start + my_frames)[:, None])
    )
    table = build_table()
    widest = MAXREQ * BLOCKW
    share = widest // time_devices
    all_hops = HOPS_DEV * time_devices
    sending = slots.transpose(2, 1, 3, 0, 4).reshape(HOPS_DEV, 2, NFINE, widest)
    gathered_cols = lax.all_to_all(sending, "tm", split_axis=3, concat_axis=0, tiled=True)
    padding = jnp.zeros((TAPS - 1, 2, NFINE, share), jnp.bfloat16)
    extended = jnp.concatenate([gathered_cols, padding], axis=0)
    col_filtered = jnp.zeros((all_hops, 2, NFINE, share), jnp.float32)
    for tap_index in range(TAPS):
        weights = prototype[tap_index][None, None, :, None]
        col_filtered = col_filtered + weights * extended[tap_index : tap_index + all_hops].astype(
            jnp.float32
        )
    flat = col_filtered.transpose(1, 2, 0, 3).reshape(2 * NFINE, all_hops * share)
    result = jnp.dot(
        table, flat, precision=lax.Precision.HIGHEST, preferred_element_type=jnp.float32
    )
    result = result.reshape(2, NFINE, all_hops, share).transpose(2, 0, 1, 3).astype(jnp.bfloat16)
    returned = lax.all_to_all(result, "tm", split_axis=0, concat_axis=3, tiled=True)
    spectra = returned.reshape(HOPS_DEV, 2, NFINE, MAXREQ, BLOCKW).transpose(0, 3, 1, 2, 4)
    keep = active.T[:, :, None, None, None]
    spectra = jnp.where(keep, spectra, jnp.zeros_like(spectra))
    return spectra[:, None]


def solution(mesh):
    return jax.shard_map(
        shards,
        mesh=mesh,
        in_specs=(P(None, "tm", "chan"), P(), P(), P(), P(), P()),
        out_specs=P("tm", "chan", None, None, None, None),
        check_vma=False,
    )
```

profile of v0, /device:TPU:0, one launch (start us, length us, event | category | flops | bytes accessed | tf_op | source)
XLA Modules:
  0.0 602.9 jit_solution(15410880582212164777)
XLA Ops:
  0.0 0.8 select_reduce_fusion.1
  0.9 0.8 fusion.28
  1.6 0.2 reduce_window_sum.11
  1.8 7.8 %copy.43 = bf16[768,8,8,128]{3,2,1,0:T(8,128)(2,1)S(1)} copy(bf16[768,8,8,128]{3,1,2,0:T(8,128)(2,1)} %bitcast.79) | data formatting | bytes 25165824
  9.6 0.1 and_reduce_fusion
  9.7 6.6 %convolution_convert_fusion = bf16[4,2,2,3,1024,128]{5,0,4,3,2,1:T(4,128)(2,1)} fusion(bf16[2,3,1024,8,128,1]{4,3,2,1,0,5:T(8,128)(2,1)S(1)} %bitcast.72, pred[4,2,8,1,1,1]{2,1,0,5,4,3:T(4,128)(4,1)S(1)} %bitcast.97), kind=kOutput, calls=%fused_computation.7 | convolution fusion | flops 106954752 | bytes 25165888 | tf_op jit(solution)/shard_map/dpb,xhkbc->dpxhkc/dot_general | solution.py:47
  16.3 11.6 %copy.27 = bf16[4,2,2,3,1024,128]{5,4,3,2,1,0:T(8,128)(2,1)} copy(bf16[4,2,2,3,1024,128]{5,0,4,3,2,1:T(4,128)(2,1)} %convolution_convert_fusion) | data formatting | bytes 25165824 | tf_op jit(solution)/shard_map/convert_element_type | solution.py:49
  27.9 6.5 %all-to-all-start = ((bf16[4,2,2,3,1024,128]{5,4,3,2,1,0:T(8,128)(2,1)}), bf16[4,2,2,3,1024,128]{5,4,3,2,1,0:T(8,128)(2,1)}, u32[]{:S(2)}, u32[]{:S(2)}) async-start(bf16[4,2,2,3,1024,128]{5,4,3,2,1,0:T(8,128)(2,1)} %copy.27), calls=%async_computation | async-start | bytes 25165824 | tf_op jit(solution)/shard_map/all_to_all | solution.py:50
  34.4 0.6 select_reduce_fusion.3
  35.0 0.6 iota_compare_fusion.5
  35.7 0.2 convert_reduce_fusion
  35.9 137.4 %all-to-all-done = bf16[4,2,2,3,1024,128]{5,4,3,2,1,0:T(8,128)(2,1)} async-done(((bf16[4,2,2,3,1024,128]{5,4,3,2,1,0:T(8,128)(2,1)}), bf16[4,2,2,3,1024,128]{5,4,3,2,1,0:T(8,128)(2,1)}, u32[]{:S(2)}, u32[]{:S(2)}) %all-to-all-start) | async-done | bytes 12582944 | tf_op jit(solution)/shard_map/all_to_all | solution.py:50
  173.3 14.5 %convert_bitcast_fusion.1 = bf16[3,2,1024,4,128]{4,3,2,0,1:T(4,128)(2,1)} fusion(bf16[8,2,3,1024,128]{4,3,2,1,0:T(8,128)(2,1)} %bitcast.7, s32[4]{0:T(128)S(1)} %multiply_add_fusion, pred[4]{0:T(512)(128)(4,1)S(1)} %iota_compare_fusion.5), kind=kOutput, calls=%fused_computation.22 | convolution fusion | flops 53477440 | bytes 18874388 | tf_op jit(solution)/shard_map/qs,sxhkc->qxhkc/dot_general | solution.py:71
  187.8 17.6 %copy.42 = bf16[3,2,1024,4,128]{2,1,0,4,3:T(2,128)(2,1)} copy(bf16[3,2,1024,4,128]{4,3,2,0,1:T(4,128)(2,1)} %convert_bitcast_fusion.1) | data formatting | bytes 12582912 | tf_op jit(solution)/shard_map/reshape | solution.py:84
  205.4 9.1 %all-to-all-start.1 = ((bf16[3,2,1024,512]{2,1,0,3:T(2,128)(2,1)}), bf16[3,2,1024,512]{2,1,0,3:T(2,128)(2,1)}, u32[]{:S(2)}, u32[]{:S(2)}) async-start(bf16[3,2,1024,512]{2,1,0,3:T(2,128)(2,1)} %bitcast.74), calls=%async_computation.1 | async-start | bytes 12582912 | tf_op jit(solution)/shard_map/all_to_all | solution.py:85
  214.6 15.5 %fusion.16 = f32[1024,1024]{1,0:T(8,128)S(1)} fusion(), kind=kLoop, calls=%fused_computation.34 | loop fusion | flops 16777216 | bytes 4194304 | tf_op jit(solution)/shard_map/neg | solution.py:23
  230.1 16.6 %sine_multiply_fusion = (f32[1024,1024]{1,0:T(8,128)S(1)}, f32[1024,1024]{1,0:T(8,128)S(1)}) fusion(), kind=kLoop, calls=%fused_computation.29 | loop fusion | flops 16777216 | bytes 8388608 | tf_op jit(solution)/shard_map/div | solution.py:21
  246.7 15.5 %maximum_maximum_fusion = f32[2048,2048]{1,0:T(8,128)} fusion(f32[1024,1024]{1,0:T(8,128)S(1)} %get-tuple-element.28, f32[1024,1024]{1,0:T(8,128)S(1)} %fusion.16, f32[1024,1024]{1,0:T(8,128)S(1)} %get-tuple-element.27), kind=kLoop, calls=%fused_computation | loop fusion | flops 12582912 | bytes 29360128 | tf_op jit(solution)/shard_map/concatenate | solution.py:24
  262.3 29.7 %all-to-all-done.1 = bf16[3,2,1024,512]{2,1,0,3:T(2,128)(2,1)} async-done(((bf16[3,2,1024,512]{2,1,0,3:T(2,128)(2,1)}), bf16[3,2,1024,512]{2,1,0,3:T(2,128)(2,1)}, u32[]{:S(2)}, u32[]{:S(2)}) %all-to-all-start.1) | async-done | bytes 6291488 | tf_op jit(solution)/shard_map/all_to_all | solution.py:85
  291.9 4.8 copy.30
  296.7 3.4 copy.31
  300.1 48.5 %add_bitcast_fusion = f32[2,1024,96,16]{1,3,0,2:T(8,128)} fusion(bf16[96,2,1024,16]{2,3,1,0:T(8,128)(2,1)} %bitcast.77, f32[1024]{0:T(1024)S(1)} %bitcast.95, f32[1024]{0:T(1024)S(1)} %bitcast.96, f32[1024]{0:T(1024)S(1)} %bitcast.82, f32[1024]{0:T(1024)S(1)} %bitcast.83, f32[1024]{0:T(1024)S(1)} %bitcast.84, f32[1024]{0:T(1024)S(1)} %bitcast.85, ...), kind=kLoop, calls=%fused_computation.6 | loop fusion | flops 147849216 | bytes 18939904 | tf_op jit(solution)/shard_map/transpose | solution.py:94
  348.7 22.3 %copy.32 = f32[2,1024,96,16]{1,0,3,2:T(2,128)} copy(f32[2,1024,96,16]{1,3,0,2:T(8,128)} %add_bitcast_fusion) | data formatting | bytes 25165824 | tf_op jit(solution)/shard_map/transpose | solution.py:94
  371.0 15.3 %copy.44 = f32[192,8,2,1024]{3,1,2,0:T(8,128)} copy(f32[192,8,2,1024]{3,2,1,0:T(2,128)} %bitcast.73) | data formatting | bytes 25165824
  386.3 112.1 %convert_bitcast_fusion = bf16[96,2,1024,16]{2,0,3,1:T(8,128)(2,1)S(1)} fusion(f32[2,1024,2048,1]{2,1,3,0:T(8,128)} %bitcast.78, f32[96,16,2048]{2,1,0:T(8,128)} %bitcast.80), kind=kOutput, calls=%fused_computation.10 | convolution fusion | flops 77312557056 | bytes 35651584 | tf_op jit(solution)/shard_map/dot_general | solution.py:95
  498.4 6.2 %copy.34 = bf16[96,2,1024,16]{2,3,1,0:T(8,128)(2,1)} copy(bf16[96,2,1024,16]{2,0,3,1:T(8,128)(2,1)S(1)} %convert_bitcast_fusion) | data formatting | bytes 12582912 | tf_op jit(solution)/shard_map/convert_element_type | solution.py:98
  504.6 4.9 all-to-all-start.2
  509.6 0.1 compare_and_fusion.1
  509.7 77.8 %all-to-all-done.2 = bf16[96,2,1024,16]{2,3,1,0:T(8,128)(2,1)} async-done(((bf16[96,2,1024,16]{2,3,1,0:T(8,128)(2,1)}), bf16[96,2,1024,16]{2,3,1,0:T(8,128)(2,1)}, u32[]{:S(2)}, u32[]{:S(2)}) %all-to-all-start.2) | async-done | bytes 6291488 | tf_op jit(solution)/shard_map/all_to_all | solution.py:99
  587.5 3.5 copy.35
  591.0 3.1 fusion.5
  594.1 8.6 %copy.36 = bf16[3,1,4,2,1024,128]{5,4,3,2,1,0:T(8,128)(2,1)} copy(bf16[3,1,4,2,1024,128]{4,5,2,3,0,1:T(8,128)(2,1)} %fusion.5) | data formatting | bytes 12582912 | tf_op jit(solution)/shard_map/broadcast_in_dim | solution.py:103
  (13 shorter events, 0.2 us)
Async XLA Ops:
  27.9 6.5 %copy-start.1 = (s32[4]{0:T(128)S(1)}, s32[4]{0:T(128)}, u32[]{:S(2)}) copy-start(s32[4]{0:T(128)} %param.11) | copy-start | bytes 52
  27.9 145.4 %all-to-all-start = ((bf16[4,2,2,3,1024,128]{5,4,3,2,1,0:T(8,128)(2,1)}), bf16[4,2,2,3,1024,128]{5,4,3,2,1,0:T(8,128)(2,1)}, u32[]{:S(2)}, u32[]{:S(2)}) async-start(bf16[4,2,2,3,1024,128]{5,4,3,2,1,0:T(8,128)(2,1)} %copy.27), calls=%async_computation | async-start | bytes 25165824 | tf_op jit(solution)/shard_map/all_to_all | solution.py:50
  187.8 26.8 %copy-start = (f32[16,1024]{1,0:T(8,128)S(1)}, f32[16,1024]{1,0:T(8,128)}, u32[]{:S(2)}) copy-start(f32[16,1024]{1,0:T(8,128)} %param.7) | copy-start | bytes 196612
  205.4 86.5 %all-to-all-start.1 = ((bf16[3,2,1024,512]{2,1,0,3:T(2,128)(2,1)}), bf16[3,2,1024,512]{2,1,0,3:T(2,128)(2,1)}, u32[]{:S(2)}, u32[]{:S(2)}) async-start(bf16[3,2,1024,512]{2,1,0,3:T(2,128)(2,1)} %bitcast.74), calls=%async_computation.1 | async-start | bytes 12582912 | tf_op jit(solution)/shard_map/all_to_all | solution.py:85
  504.6 82.8 %all-to-all-start.2 = ((bf16[96,2,1024,16]{2,3,1,0:T(8,128)(2,1)}), bf16[96,2,1024,16]{2,3,1,0:T(8,128)(2,1)}, u32[]{:S(2)}, u32[]{:S(2)}) async-start(bf16[96,2,1024,16]{2,3,1,0:T(8,128)(2,1)} %copy.34), calls=%async_computation.2 | async-start | bytes 12582912 | tf_op jit(solution)/shard_map/all_to_all | solution.py:99
where the time goes:
time: 611 us; the launch traced here: 603 us
  waiting for transfers between devices  245 us (40%)
  matrix products  133 us (22%)
  other arithmetic  103 us (17%)
  local copies, waits for them, and re-layouts  101 us (17%)
  starting transfers between devices  20.5 us (3%)
    all_to_all x1, waiting for transfers between devices, shards(): lax.all_to_all(outgoing, 'chan', split_axis=0, concat_axis=0, tiled=True)  137 us
    dot_general x1, matrix products, shards(): jnp.dot(table, flat, precision=lax.Precision.HIGHEST, preferred_element_t...  112 us
    all_to_all x1, waiting for transfers between devices, shards(): lax.all_to_all(result, 'tm', split_axis=0, concat_axis=3, tiled=True)  77.8 us
    transpose x1, other arithmetic, shards(): col_filtered.transpose(1, 2, 0, 3).reshape(2 * NFINE, all_hops * share)  48.5 us
    all_to_all x1, waiting for transfers between devices, shards(): lax.all_to_all(sending, 'tm', split_axis=3, concat_axis=0, tiled=True)  29.7 us
    unnamed x6, local copies, waits for them, and re-layouts  23.1 us
    transpose x1, local copies, waits for them, and re-layouts, shards(): col_filtered.transpose(1, 2, 0, 3).reshape(2 * NFINE, all_hops * share)  22.3 us
    reshape x1, local copies, waits for them, and re-layouts, shards(): sending = slots.transpose(2, 1, 3, 0, 4).reshape(HOPS_DEV, 2, NFINE, widest)  17.6 us
  transfers between devices with their start and end apart: 3, of which 3 were waited for; matrix products, arithmetic and copies ran while one was open for 8% of the time, Pallas kernels for 0%

commit v1 on v0

v1 whole, which is shorter than its diff:
```python
import math

import jax
import jax.numpy as jnp
import ml_dtypes
import numpy as np
from jax import lax
from jax.experimental import pallas as pl
from jax.experimental.pallas import tpu as pltpu
from jax.sharding import PartitionSpec as P

BLOCKW = 128
NFINE = 1024
TAPS = 16
HOPS_DEV = 3
MAXREQ = 4
PAIR = 2
TM = 32
OWNERS = 4
BPC = 8
HOPS = 96
SHARE = BLOCKW // TM
ROWS = 2 * SHARE
RADIX = 8
LANES = 128
FRAMES = 84
GROUP = 12


def pick_matrix():
    pick = np.zeros((2 * BLOCKW, 2 * BLOCKW), np.float32)
    for device in range(TM):
        for part in range(2):
            for column in range(SHARE):
                pick[device * ROWS + part * SHARE + column, part * BLOCKW + device * SHARE + column] = 1
    return pick.astype(ml_dtypes.bfloat16)


def dft_tables():
    k2 = np.arange(LANES)[None, :, None]
    m = np.arange(RADIX)[:, None, None] + RADIX * np.arange(LANES)[None, None, :]
    angles = (k2 * m % NFINE) * (2.0 * math.pi / NFINE)
    table = np.concatenate([np.cos(angles), np.sin(angles)], axis=2) / math.sqrt(NFINE)
    high = table.astype(np.float32).astype(ml_dtypes.bfloat16)
    low = (table - high.astype(np.float64)).astype(np.float32).astype(ml_dtypes.bfloat16)
    return np.concatenate([high, high], axis=1), low


def pack_kernel(block_ref, count_ref, column_ref, x_ref, pick_ref, out_ref):
    for hop in range(HOPS_DEV):
        rows = pl.ds(hop * NFINE, NFINE)
        both = jnp.concatenate([x_ref[0, rows, :], x_ref[1, rows, :]], axis=1)
        turned = lax.dot_general(
            pick_ref[...], both, (((1,), (1,)), ((), ())), preferred_element_type=jnp.float32
        )
        out_ref[:, 0, 0, hop] = turned.reshape(TM, ROWS, NFINE).astype(jnp.bfloat16)


def wanted_block(owner, rank, block_ref, count_ref, column_ref):
    seen = jnp.int32(0)
    chosen = jnp.int32(0)
    for slot in range(MAXREQ):
        block = block_ref[owner, slot]
        mine = (slot < count_ref[owner]) & (block // BPC == column_ref[0])
        chosen = jnp.where(mine & (seen == rank), block % BPC, chosen)
        seen = seen + mine.astype(jnp.int32)
    return chosen


def pack(coarse, pick, req_block, req_count, column):
    return pl.pallas_call(
        pack_kernel,
        out_shape=jax.ShapeDtypeStruct((TM, OWNERS, PAIR, HOPS_DEV, ROWS, NFINE), jnp.bfloat16),
        grid_spec=pltpu.PrefetchScalarGridSpec(
            num_scalar_prefetch=3,
            grid=(OWNERS, PAIR),
            in_specs=[
                pl.BlockSpec(
                    (2, HOPS_DEV * NFINE, BLOCKW),
                    lambda c, r, *refs: (0, 0, wanted_block(c, r, *refs)),
                ),
                pl.BlockSpec((2 * BLOCKW, 2 * BLOCKW), lambda c, r, *refs: (0, 0)),
            ],
            out_specs=pl.BlockSpec(
                (TM, 1, 1, HOPS_DEV, ROWS, NFINE), lambda c, r, *refs: (0, c, r, 0, 0, 0)
            ),
        ),
        name="pack",
    )(req_block, req_count, column, coarse, pick)


def turn(value, sign):
    return pltpu.roll(value, SHARE, value.ndim - 2) * sign


def dft4(a, b, c, d, sign):
    s02, d02, s13, d13 = a + c, a - c, b + d, turn(b - d, sign)
    return s02 + s13, d02 + d13, s02 - s13, d02 - d13


def dft8(x, sign):
    half = math.sqrt(0.5)
    low = [x[i] + x[i + 4] for i in range(4)]
    high = [x[i] - x[i + 4] for i in range(4)]
    high[1] = (high[1] + turn(high[1], sign)) * half
    high[2] = turn(high[2], sign)
    high[3] = (turn(high[3], sign) - high[3]) * half
    even, odd = dft4(*low, sign), dft4(*high, sign)
    return [pair for both in zip(even, odd) for pair in both]


def filter_kernel(block_ref, count_ref, column_ref, x_ref, proto_ref, tall_ref, low_ref, out_ref, wide_ref, fir_ref, split_ref):
    sign = jnp.where(lax.broadcasted_iota(jnp.int32, (ROWS, LANES), 0) < SHARE, 1.0, -1.0)
    wide_ref[HOPS:, :, :] = jnp.zeros((FRAMES + TAPS - 1 - HOPS, ROWS, LANES), jnp.float32)
    for tile in range(RADIX):
        lanes = pl.ds(tile * LANES, LANES)
        wide_ref[:HOPS] = x_ref[:, 0, 0, :, :, lanes].astype(jnp.float32).reshape(HOPS, ROWS, LANES)
        weights = [jnp.broadcast_to(proto_ref[tap, lanes].reshape(1, LANES), (ROWS, LANES)) for tap in range(TAPS)]

        def fir(step, carry):
            first = step * GROUP
            samples = wide_ref[pl.ds(first, GROUP + TAPS - 1)]
            total = samples[:GROUP] * weights[0]
            for tap in range(1, TAPS):
                total = total + samples[tap : tap + GROUP] * weights[tap]
            fir_ref[pl.ds(first, GROUP), :, lanes] = total
            return carry

        lax.fori_loop(0, FRAMES // GROUP, fir, 0)

    def butterflies(step, carry):
        first = step * 2
        parts = [fir_ref[pl.ds(first, 2), :, tile * LANES : (tile + 1) * LANES] for tile in range(RADIX)]
        rows = pl.ds(pl.multiple_of(first * ROWS, 2 * ROWS), 2 * ROWS)
        for m1, value in enumerate(dft8(parts, sign)):
            value = value.reshape(2 * ROWS, LANES)
            high = value.astype(jnp.bfloat16)
            split_ref[m1, rows, :LANES] = high
            split_ref[m1, rows, LANES:] = (value - high.astype(jnp.float32)).astype(jnp.bfloat16)
        return carry

    lax.fori_loop(0, FRAMES // 2, butterflies, 0)
    for m1 in range(RADIX):
        both = split_ref[m1]
        product = jnp.dot(both, tall_ref[m1], preferred_element_type=jnp.float32)
        product = product + jnp.dot(both[:, :LANES], low_ref[m1], preferred_element_type=jnp.float32)
        cosines = product[:, :LANES].reshape(FRAMES, ROWS, LANES)
        sines = product[:, LANES:].reshape(FRAMES, ROWS, LANES)
        result = (cosines + turn(sines, sign)).astype(jnp.bfloat16)
        out_ref[: FRAMES // HOPS_DEV, :, 0, :, m1 * LANES : (m1 + 1) * LANES] = result.reshape(
            FRAMES // HOPS_DEV, HOPS_DEV, ROWS, LANES
        )


def arrival(slot, block_ref, count_ref, column_ref):
    owner = column_ref[0]
    source = block_ref[owner, slot] // BPC
    rank = jnp.int32(0)
    for other in range(MAXREQ - 1):
        same = (other < slot) & (block_ref[owner, other] // BPC == source)
        rank = rank + same.astype(jnp.int32)
    return source, jnp.minimum(rank, PAIR - 1)


def filter_and_transform(arrived, prototype, tall, low, req_block, req_count, column):
    def arrived_map(q, *refs):
        source, rank = arrival(q, *refs)
        return (0, source, rank, 0, 0, 0)

    return pl.pallas_call(
        filter_kernel,
        out_shape=jax.ShapeDtypeStruct((TM, HOPS_DEV, MAXREQ, ROWS, NFINE), jnp.bfloat16),
        grid_spec=pltpu.PrefetchScalarGridSpec(
            num_scalar_prefetch=3,
            grid=(MAXREQ,),
            in_specs=[
                pl.BlockSpec((TM, 1, 1, HOPS_DEV, ROWS, NFINE), arrived_map),
                pl.BlockSpec((TAPS, NFINE), lambda q, *refs: (0, 0)),
                pl.BlockSpec((RADIX, 2 * LANES, 2 * LANES), lambda q, *refs: (0, 0, 0)),
                pl.BlockSpec((RADIX, LANES, 2 * LANES), lambda q, *refs: (0, 0, 0)),
            ],
            out_specs=pl.BlockSpec(
                (TM, HOPS_DEV, 1, ROWS, NFINE), lambda q, *refs: (0, 0, q, 0, 0)
            ),
            scratch_shapes=[
                pltpu.VMEM((FRAMES + TAPS - 1, ROWS, LANES), jnp.float32),
                pltpu.VMEM((FRAMES, ROWS, NFINE), jnp.float32),
                pltpu.VMEM((RADIX, FRAMES * ROWS, 2 * LANES), jnp.bfloat16),
            ],
        ),
        name="filter",
    )(req_block, req_count, column, arrived, prototype, tall, low)


def unpack_kernel(start_ref, frames_ref, count_ref, place_ref, y_ref, pick_ref, out_ref, turned_ref):
    slot = pl.program_id(1)
    owner = place_ref[0]
    hop = place_ref[1] * HOPS_DEV + pl.program_id(0)
    begin = start_ref[owner, slot]
    active = (slot < count_ref[owner]) & (hop >= begin) & (hop < begin + frames_ref[owner, slot])

    @pl.when(active)
    def _():
        rows = y_ref[:, 0, 0].astype(jnp.float32).reshape(TM * ROWS, NFINE).astype(jnp.bfloat16)
        for m1 in range(RADIX):
            columns = lax.dot_general(
                rows[:, m1 * LANES : (m1 + 1) * LANES],
                pick_ref[...],
                (((0,), (0,)), ((), ())),
                preferred_element_type=jnp.float32,
            )
            for part in range(2):
                turned_ref[part, pl.ds(m1, LANES, stride=RADIX), :] = columns[:, part * LANES : (part + 1) * LANES]
        out_ref[0, 0, 0] = turned_ref[...].astype(jnp.bfloat16)

    @pl.when(jnp.logical_not(active))
    def _():
        out_ref[...] = jnp.zeros_like(out_ref)


def unpack(returned, pick, req_start, req_frames, req_count, place):
    return pl.pallas_call(
        unpack_kernel,
        out_shape=jax.ShapeDtypeStruct((HOPS_DEV, 1, MAXREQ, 2, NFINE, BLOCKW), jnp.bfloat16),
        grid_spec=pltpu.PrefetchScalarGridSpec(
            num_scalar_prefetch=4,
            grid=(HOPS_DEV, MAXREQ),
            in_specs=[
                pl.BlockSpec((TM, 1, 1, ROWS, NFINE), lambda h, q, *refs: (0, h, q, 0, 0)),
                pl.BlockSpec((2 * BLOCKW, 2 * BLOCKW), lambda h, q, *refs: (0, 0)),
            ],
            out_specs=pl.BlockSpec(
                (1, 1, 1, 2, NFINE, BLOCKW), lambda h, q, *refs: (h, 0, q, 0, 0, 0)
            ),
            scratch_shapes=[pltpu.VMEM((2, NFINE, BLOCKW), jnp.float32)],
        ),
        name="unpack",
    )(req_start, req_frames, req_count, place, returned, pick)


def shards(coarse, prototype, req_block, req_start, req_frames, req_count):
    column = lax.axis_index("chan").astype(jnp.int32)
    place = jnp.stack([column, lax.axis_index("tm").astype(jnp.int32)])
    pick = jnp.asarray(pick_matrix())
    tall, low = (jnp.asarray(table) for table in dft_tables())
    outgoing = pack(coarse, pick, req_block, req_count, place)
    outgoing = outgoing.reshape(TM * OWNERS, PAIR, HOPS_DEV, ROWS, NFINE)
    arrived = lax.all_to_all(outgoing, ("tm", "chan"), split_axis=0, concat_axis=0, tiled=True)
    arrived = arrived.reshape(TM, OWNERS, PAIR, HOPS_DEV, ROWS, NFINE)
    result = filter_and_transform(arrived, prototype, tall, low, req_block, req_count, place)
    returned = lax.all_to_all(result, "tm", split_axis=0, concat_axis=0, tiled=True)
    return unpack(returned, pick, req_start, req_frames, req_count, place)


def solution(mesh):
    return jax.shard_map(
        shards,
        mesh=mesh,
        in_specs=(P(None, "tm", "chan"), P(), P(), P(), P(), P()),
        out_specs=P("tm", "chan", None, None, None, None),
        check_vma=False,
    )
```

time: 611 us -> 289 us (0.47)
  waiting for transfers between devices: 245 us -> 0 us
  blocking collectives: 0 us -> 231 us
  matrix products: 133 us -> 0 us
  other arithmetic: 103 us -> 0.59 us
  local copies, waits for them, and re-layouts: 101 us -> 0 us
  Pallas kernels: 0 us -> 55 us
  starting transfers between devices: 20.5 us -> 0 us
    all_to_all x3 -> x0, waiting for transfers between devices: 245 us -> none  [the longest x1 137 us: shards(): lax.all_to_all(outgoing, 'chan', split_axis=0, concat_axis=0, tiled=True)]
    all_to_all x0 -> x2, blocking collectives: none -> 231 us  [the longest x1 153 us: shards(): lax.all_to_all(outgoing, ('tm', 'chan'), split_axis=0, concat_axis=0, til...]
    dot_general x3 -> x0, matrix products: 133 us -> none  [the longest x1 112 us: shards(): jnp.dot(table, flat, precision=lax.Precision.HIGHEST, preferred_element_t...]
    pallas_call x0 -> x3, Pallas kernels: none -> 55 us  [the longest x1 29.8 us: filter_and_transform(): pl.pallas_call(filter_kernel, out_shape=jax.ShapeDtypeStruct((TM, HOPS_DE...]
    transpose x1 -> x0, other arithmetic: 48.5 us -> none  [shards(): col_filtered.transpose(1, 2, 0, 3).reshape(2 * NFINE, all_hops * share)]
    unnamed x6 -> x0, local copies, waits for them, and re-layouts: 23.1 us -> none
    transpose x1 -> x0, local copies, waits for them, and re-layouts: 22.3 us -> none  [shards(): col_filtered.transpose(1, 2, 0, 3).reshape(2 * NFINE, all_hops * share)]
    all_to_all x3 -> x0, starting transfers between devices: 20.5 us -> none  [the longest x1 9.11 us: shards(): lax.all_to_all(sending, 'tm', split_axis=3, concat_axis=0, tiled=True)]
  transfers between devices with their start and end apart: 3 -> 0, of which waited for: 3 -> 0; matrix products, arithmetic and copies ran while one was open for 8% -> 0% of each run, Pallas kernels for 0% -> 0%
where the time goes in v1:
time: 289 us; the launch traced here: 287 us
  blocking collectives  231 us (80%)
  Pallas kernels  55 us (19%)
    all_to_all x1, blocking collectives, shards(): lax.all_to_all(outgoing, ('tm', 'chan'), split_axis=0, concat_axis=0, til...  153 us
    all_to_all x1, blocking collectives, shards(): lax.all_to_all(result, 'tm', split_axis=0, concat_axis=0, tiled=True)  78.4 us
    pallas_call x1, Pallas kernels, filter_and_transform(): pl.pallas_call(filter_kernel, out_shape=jax.ShapeDtypeStruct((TM, HOPS_DE...  29.8 us
    pallas_call x1, Pallas kernels, pack(): pl.pallas_call(pack_kernel, out_shape=jax.ShapeDtypeStruct((TM, OWNERS, P...  14.2 us
    pallas_call x1, Pallas kernels, unpack(): pl.pallas_call(unpack_kernel, out_shape=jax.ShapeDtypeStruct((HOPS_DEV, 1...  11 us

profile of v1, /device:TPU:0, one launch (start us, length us, event | category | flops | bytes accessed | tf_op | source)
XLA Modules:
  0.0 286.7 jit_solution(840191796328976033)
XLA Ops:
  0.0 0.6 pad_add_fusion.column_ref.place_ref
  0.6 14.2 %pack.1 = bf16[32,4,2,3,8,1024]{5,4,3,2,1,0:T(8,128)(2,1)} custom-call(s32[4,4]{1,0:T(4,128)} %block_ref.3, s32[4]{0:T(128)} %count_ref.5, s32[2]{0:T(128)} %pad_add_fusion.column_ref.place_ref, bf16[2,3072,1024]{2,1,0:T(8,128)(2,1)} %x_ref.1, bf16[256,256]{1,0:T(8,128)(2,1)} %constant.15.clone.pick_ref), custom_call_target="tpu_custom_call" | custom-call | tf_op jit(solution)/shard_map/pack/pallas_call | solution.py:71
  14.8 152.7 %all_to_all.10 = bf16[128,2,3,8,1024]{4,3,2,1,0:T(8,128)(2,1)} all-to-all(bf16[128,2,3,8,1024]{4,3,2,1,0:T(8,128)(2,1)} %bitcast.4), channel_id=1, replica_groups=mesh['tm'=32,'chan'=4] {'tm','chan'}, dimensions={0} | all-to-all | bytes 25165824 | tf_op jit(solution)/shard_map/all_to_all | solution.py:248
  167.5 29.8 %filter.1 = bf16[32,3,4,8,1024]{4,3,2,1,0:T(8,128)(2,1)} custom-call(s32[4,4]{1,0:T(4,128)} %block_ref.3, s32[4]{0:T(128)} %count_ref.5, s32[2]{0:T(128)} %pad_add_fusion.column_ref.place_ref, bf16[32,4,2,3,8,1024]{5,4,3,2,1,0:T(8,128)(2,1)} %bitcast.5, f32[16,1024]{1,0:T(8,128)} %proto_ref.1, bf16[8,256,256]{2,1,0:T(8,128)(2,1)} %constant.16.clone.tall_ref, ...), custom_call_target="tpu_custom_call" | custom-call | tf_op jit(solution)/shard_map/filter/pallas_call | solution.py:170
  197.4 78.4 %all_to_all.11.y_ref = bf16[32,3,4,8,1024]{4,3,2,1,0:T(8,128)(2,1)} all-to-all(bf16[32,3,4,8,1024]{4,3,2,1,0:T(8,128)(2,1)} %filter.1), channel_id=1, replica_groups=mesh['tm'=32,'chan'=4] {'tm'}, dimensions={0} | all-to-all | bytes 12582912 | tf_op jit(solution)/shard_map/all_to_all | solution.py:251
  275.7 11.0 %unpack.1 = bf16[3,1,4,2,1024,128]{5,4,3,2,1,0:T(8,128)(2,1)} custom-call(s32[4,4]{1,0:T(4,128)} %start_ref.1, s32[4,4]{1,0:T(4,128)} %frames_ref.1, s32[4]{0:T(128)} %count_ref.5, s32[2]{0:T(128)} %pad_add_fusion.column_ref.place_ref, bf16[32,3,4,8,1024]{4,3,2,1,0:T(8,128)(2,1)} %all_to_all.11.y_ref, bf16[256,256]{1,0:T(8,128)(2,1)} %constant.15.clone.pick_ref), custom_call_target="tpu_custom_call" | custom-call | tf_op jit(solution)/shard_map/unpack/pallas_call | solution.py:222

commit v2 on v1

v2 whole, which is shorter than its diff:
```python
import math

import jax
import jax.numpy as jnp
import ml_dtypes
import numpy as np
from jax import lax
from jax.experimental import pallas as pl
from jax.experimental.pallas import tpu as pltpu
from jax.sharding import PartitionSpec as P

BLOCKW = 128
NFINE = 1024
TAPS = 16
HOPS_DEV = 3
MAXREQ = 4
PAIR = 2
TM = 32
OWNERS = 4
BPC = 8
HOPS = 96
HALF = BLOCKW // 2
SHARE = HALF // TM
ROWS = 8
RADIX = 8
LANES = 128
FRAMES = 84
GROUP = 12


def late_pick():
    pick = np.zeros((TM, 2, PAIR, SHARE, PAIR, 2, BLOCKW), np.float32)
    for device, part, rank, column in np.ndindex(TM, 2, PAIR, SHARE):
        pick[device, part, rank, column, rank, part, HALF + device * SHARE + column] = 1
    return pick.reshape(TM * ROWS, PAIR * 2 * BLOCKW).astype(ml_dtypes.bfloat16)


def early_pick():
    pick = np.zeros((TM, 2, 2, SHARE, 2, 2, HALF), np.float32)
    for device, part, slot, column in np.ndindex(TM, 2, 2, SHARE):
        pick[device, part, slot, column, slot, part, device * SHARE + column] = 1
    return pick.reshape(TM * ROWS, 2 * BLOCKW).astype(ml_dtypes.bfloat16)


def lower_half():
    pick = np.zeros((2, BLOCKW, 2, HALF), np.float32)
    for part, column in np.ndindex(2, HALF):
        pick[part, column, part, column] = 1
    return pick.reshape(2 * BLOCKW, BLOCKW).astype(ml_dtypes.bfloat16)


def dft_tables():
    k2 = np.arange(LANES)[None, :, None]
    m = np.arange(RADIX)[:, None, None] + RADIX * np.arange(LANES)[None, None, :]
    angles = (k2 * m % NFINE) * (2.0 * math.pi / NFINE)
    table = np.concatenate([np.cos(angles), np.sin(angles)], axis=2) / math.sqrt(NFINE)
    high = table.astype(np.float32).astype(ml_dtypes.bfloat16)
    low = (table - high.astype(np.float64)).astype(np.float32).astype(ml_dtypes.bfloat16)
    return high, low


def wanted_block(shift, rank, block_ref, count_ref, place_ref):
    owner = (place_ref[0] + shift) % OWNERS
    seen = jnp.int32(0)
    chosen = jnp.int32(0)
    for slot in range(MAXREQ):
        block = block_ref[owner, slot]
        mine = (slot < count_ref[owner]) & (block // BPC == place_ref[0])
        chosen = jnp.where(mine & (seen == rank), block % BPC, chosen)
        seen = seen + mine.astype(jnp.int32)
    return chosen


def pack_early_kernel(block_ref, count_ref, place_ref, x_ref, lower_ref, *out_refs):
    def write(out_ref):
        for hop in range(HOPS_DEV):
            rows = pl.ds(hop * NFINE, NFINE)
            both = jnp.concatenate([x_ref[0, rows, :], x_ref[1, rows, :]], axis=1)
            out_ref[0, hop] = jnp.dot(both, lower_ref[...], preferred_element_type=jnp.float32).astype(jnp.bfloat16)

    for shift, out_ref in enumerate(out_refs):
        pl.when(pl.program_id(0) == shift)(lambda out_ref=out_ref: write(out_ref))


def pack_early(coarse, lower, req_block, req_count, place):
    def out_map(own, d, r):
        return (jnp.where(d < own, 0, jnp.where(d > own, PAIR - 1, r)), 0, 0, 0)

    return pl.pallas_call(
        pack_early_kernel,
        out_shape=[jax.ShapeDtypeStruct((PAIR, HOPS_DEV, NFINE, BLOCKW), jnp.bfloat16)] * OWNERS,
        grid_spec=pltpu.PrefetchScalarGridSpec(
            num_scalar_prefetch=3,
            grid=(OWNERS, PAIR),
            in_specs=[
                pl.BlockSpec(
                    (2, HOPS_DEV * NFINE, BLOCKW),
                    lambda d, r, *refs: (0, 0, wanted_block(d, r, *refs)),
                ),
                pl.BlockSpec((2 * BLOCKW, BLOCKW), lambda d, r, *refs: (0, 0)),
            ],
            out_specs=[
                pl.BlockSpec(
                    (1, HOPS_DEV, NFINE, BLOCKW), lambda d, r, *refs, own=own: out_map(own, d, r)
                )
                for own in range(OWNERS)
            ],
        ),
        name="pack_early",
    )(req_block, req_count, place, coarse, lower)


def pack_late_kernel(block_ref, count_ref, place_ref, x0_ref, x1_ref, pick_ref, out_ref):
    for hop in range(HOPS_DEV):
        rows = pl.ds(hop * NFINE, NFINE)
        wide = jnp.concatenate([x0_ref[0, rows, :], x0_ref[1, rows, :], x1_ref[0, rows, :], x1_ref[1, rows, :]], axis=1)
        turned = lax.dot_general(
            pick_ref[...], wide, (((1,), (1,)), ((), ())), preferred_element_type=jnp.float32
        )
        out_ref[:, 0, hop] = turned.reshape(TM, ROWS, NFINE).astype(jnp.bfloat16)


def pack_late(coarse, pick, req_block, req_count, place):
    def block_spec(rank):
        return pl.BlockSpec(
            (2, HOPS_DEV * NFINE, BLOCKW), lambda d, *refs: (0, 0, wanted_block(d, rank, *refs))
        )

    return pl.pallas_call(
        pack_late_kernel,
        out_shape=jax.ShapeDtypeStruct((TM, OWNERS, HOPS_DEV, ROWS, NFINE), jnp.bfloat16),
        grid_spec=pltpu.PrefetchScalarGridSpec(
            num_scalar_prefetch=3,
            grid=(OWNERS,),
            in_specs=[
                block_spec(0),
                block_spec(1),
                pl.BlockSpec((TM * ROWS, PAIR * 2 * BLOCKW), lambda d, *refs: (0, 0)),
            ],
            out_specs=pl.BlockSpec(
                (TM, 1, HOPS_DEV, ROWS, NFINE), lambda d, *refs: (0, d, 0, 0, 0)
            ),
        ),
        name="pack_late",
    )(req_block, req_count, place, coarse, coarse, pick)


def arrival(slot, block_ref, place_ref):
    owner = place_ref[0]
    source = block_ref[owner, slot] // BPC
    rank = jnp.int32(0)
    for other in range(slot):
        rank = rank + (block_ref[owner, other] // BPC == source).astype(jnp.int32)
    return (owner - source + OWNERS) % OWNERS, jnp.minimum(rank, PAIR - 1)


def choose_kernel(block_ref, place_ref, a0, a1, a2, a3, pick_ref, out_ref, held_ref, sem):
    pair, hop = pl.program_id(0), pl.program_id(1)

    @pl.when((pair == 0) & (hop == 0))
    def _():
        for slot in range(MAXREQ):
            shift, rank = arrival(slot, block_ref, place_ref)
            for own, ref in enumerate((a0, a1, a2, a3)):

                @pl.when(shift == own)
                def _():
                    pltpu.make_async_copy(ref.at[rank], held_ref.at[slot], sem.at[slot]).start()

    @pl.when(hop == 0)
    def _():
        for slot in range(2):
            at = pair * 2 + slot
            pltpu.make_async_copy(a0.at[0], held_ref.at[at], sem.at[at]).wait()

    both = jnp.concatenate([held_ref[pair * 2, hop], held_ref[pair * 2 + 1, hop]], axis=1)
    turned = lax.dot_general(
        pick_ref[...], both, (((1,), (1,)), ((), ())), preferred_element_type=jnp.float32
    )
    out_ref[:, 0, 0] = turned.reshape(TM, ROWS, NFINE).astype(jnp.bfloat16)


def choose(arrived, pick, req_block, place):
    return pl.pallas_call(
        choose_kernel,
        out_shape=jax.ShapeDtypeStruct((TM, MAXREQ // 2, HOPS_DEV, ROWS, NFINE), jnp.bfloat16),
        grid_spec=pltpu.PrefetchScalarGridSpec(
            num_scalar_prefetch=2,
            grid=(MAXREQ // 2, HOPS_DEV),
            in_specs=[pl.BlockSpec(memory_space=pl.ANY)] * OWNERS
            + [pl.BlockSpec((TM * ROWS, 2 * BLOCKW), lambda p, h, *refs: (0, 0))],
            out_specs=pl.BlockSpec(
                (TM, 1, 1, ROWS, NFINE), lambda p, h, *refs: (0, p, h, 0, 0)
            ),
            scratch_shapes=[
                pltpu.VMEM((MAXREQ, HOPS_DEV, NFINE, BLOCKW), jnp.bfloat16),
                pltpu.SemaphoreType.DMA((MAXREQ,)),
            ],
        ),
        name="choose",
    )(req_block, place, *arrived, pick)


def turn(value, sign):
    return pltpu.roll(value, ROWS // 2, value.ndim - 2) * sign


def dft4(a, b, c, d, sign):
    s02, d02, s13, d13 = a + c, a - c, b + d, turn(b - d, sign)
    return s02 + s13, d02 + d13, s02 - s13, d02 - d13


def dft8(x, sign):
    half = math.sqrt(0.5)
    low = [x[i] + x[i + 4] for i in range(4)]
    high = [x[i] - x[i + 4] for i in range(4)]
    high[1] = (high[1] + turn(high[1], sign)) * half
    high[2] = turn(high[2], sign)
    high[3] = (turn(high[3], sign) - high[3]) * half
    even, odd = dft4(*low, sign), dft4(*high, sign)
    return [pair for both in zip(even, odd) for pair in both]


def transform(load, proto_ref, high_ref, low_ref, out_ref, wide_ref, fir_ref, split_ref):
    sign = jnp.where(lax.broadcasted_iota(jnp.int32, (ROWS, LANES), 0) < ROWS // 2, 1.0, -1.0)
    wide_ref[HOPS:, :, :] = jnp.zeros((FRAMES + TAPS - 1 - HOPS, ROWS, LANES), jnp.float32)
    def taps(tile, carry):
        lanes = pl.ds(pl.multiple_of(tile * LANES, LANES), LANES)
        wide_ref[:HOPS] = load(lanes)
        weights = [jnp.broadcast_to(proto_ref[tap, lanes].reshape(1, LANES), (ROWS, LANES)) for tap in range(TAPS)]

        def fir(step, inner):
            first = step * GROUP
            samples = wide_ref[pl.ds(first, GROUP + TAPS - 1)]
            total = samples[:GROUP] * weights[0]
            for tap in range(1, TAPS):
                total = total + samples[tap : tap + GROUP] * weights[tap]
            fir_ref[pl.ds(first, GROUP), :, lanes] = total
            return inner

        return lax.fori_loop(0, FRAMES // GROUP, fir, carry)

    lax.fori_loop(0, RADIX, taps, 0)

    def butterflies(step, carry):
        first = step * 2
        parts = [fir_ref[pl.ds(first, 2), :, tile * LANES : (tile + 1) * LANES] for tile in range(RADIX)]
        rows = pl.ds(pl.multiple_of(first * ROWS, 2 * ROWS), 2 * ROWS)
        for m1, value in enumerate(dft8(parts, sign)):
            value = value.reshape(2 * ROWS, LANES)
            high = value.astype(jnp.bfloat16)
            split_ref[m1, rows, :LANES] = high
            split_ref[m1, rows, LANES:] = (value - high.astype(jnp.float32)).astype(jnp.bfloat16)
        return carry

    lax.fori_loop(0, FRAMES // 2, butterflies, 0)
    for m1 in range(RADIX):
        both = split_ref[m1]
        high = high_ref[m1]
        product = jnp.dot(both, jnp.concatenate([high, high], axis=0), preferred_element_type=jnp.float32)
        product = product + jnp.dot(both[:, :LANES], low_ref[m1], preferred_element_type=jnp.float32)
        cosines = product[:, :LANES].reshape(FRAMES, ROWS, LANES)
        sines = product[:, LANES:].reshape(FRAMES, ROWS, LANES)
        result = (cosines + turn(sines, sign)).astype(jnp.bfloat16)
        out_ref[: FRAMES // HOPS_DEV, :, 0, :, m1 * LANES : (m1 + 1) * LANES] = result.reshape(
            FRAMES // HOPS_DEV, HOPS_DEV, ROWS, LANES
        )


def early_kernel(x_ref, *refs):
    def load(lanes):
        return x_ref[:, 0, :, :, lanes].astype(jnp.float32).reshape(HOPS, ROWS, LANES)

    transform(load, *refs)


def late_kernel(block_ref, place_ref, a0, a1, a2, a3, proto_ref, high_ref, low_ref, out_ref, wide_ref, fir_ref, split_ref, held_ref, sem):
    pair = pl.program_id(0)

    @pl.when(pair == 0)
    def _():
        for slot in range(MAXREQ):
            shift, _ = arrival(slot, block_ref, place_ref)
            for own, ref in enumerate((a0.at[:, 0], a1, a2, a3)):

                @pl.when(shift == own)
                def _():
                    pltpu.make_async_copy(ref, held_ref.at[slot], sem.at[slot]).start()

    for slot in range(2):
        at = pair * 2 + slot
        pltpu.make_async_copy(a1, held_ref.at[at], sem.at[at]).wait()

    ranks = [arrival(slot, block_ref, place_ref)[1] for slot in range(MAXREQ)]
    first_rank = jnp.where(pair == 0, ranks[0], ranks[2])
    second_rank = jnp.where(pair == 0, ranks[1], ranks[3])
    is_second = (lax.broadcasted_iota(jnp.int32, (HOPS, ROWS, LANES), 1) // SHARE) % 2 == 1

    def load(lanes):
        first = held_ref[pair * 2, :, :, :, lanes].astype(jnp.float32).reshape(HOPS, ROWS, LANES)
        second = held_ref[pair * 2 + 1, :, :, :, lanes].astype(jnp.float32).reshape(HOPS, ROWS, LANES)
        first = jnp.where(first_rank == 0, first, pltpu.roll(first, ROWS - SHARE, 1))
        second = jnp.where(second_rank == 1, second, pltpu.roll(second, SHARE, 1))
        return jnp.where(is_second, second, first)

    transform(load, proto_ref, high_ref, low_ref, out_ref, wide_ref, fir_ref, split_ref)


def table_specs():
    return [
        pl.BlockSpec((TAPS, NFINE), lambda p, *refs: (0, 0)),
        pl.BlockSpec((RADIX, LANES, 2 * LANES), lambda p, *refs: (0, 0, 0)),
        pl.BlockSpec((RADIX, LANES, 2 * LANES), lambda p, *refs: (0, 0, 0)),
    ]


RESULT = jax.ShapeDtypeStruct((TM, HOPS_DEV, MAXREQ // 2, ROWS, NFINE), jnp.bfloat16)


def result_spec():
    return pl.BlockSpec((TM, HOPS_DEV, 1, ROWS, NFINE), lambda p, *refs: (0, 0, p, 0, 0))


def work_space():
    return [
        pltpu.VMEM((FRAMES + TAPS - 1, ROWS, LANES), jnp.float32),
        pltpu.VMEM((FRAMES, ROWS, NFINE), jnp.float32),
        pltpu.VMEM((RADIX, FRAMES * ROWS, 2 * LANES), jnp.bfloat16),
    ]


def filter_early(gathered, tables):
    return pl.pallas_call(
        early_kernel,
        out_shape=RESULT,
        grid=(MAXREQ // 2,),
        in_specs=[
            pl.BlockSpec((TM, 1, HOPS_DEV, ROWS, NFINE), lambda p: (0, p, 0, 0, 0)),
            *table_specs(),
        ],
        out_specs=result_spec(),
        scratch_shapes=work_space(),
        name="filter_early",
    )(gathered, *tables)


def filter_late(arrived, tables, req_block, place):
    return pl.pallas_call(
        late_kernel,
        out_shape=RESULT,
        grid_spec=pltpu.PrefetchScalarGridSpec(
            num_scalar_prefetch=2,
            grid=(MAXREQ // 2,),
            in_specs=[pl.BlockSpec(memory_space=pl.ANY)] * OWNERS + table_specs(),
            out_specs=result_spec(),
            scratch_shapes=work_space()
            + [
                pltpu.VMEM((MAXREQ, TM, HOPS_DEV, ROWS, NFINE), jnp.bfloat16),
                pltpu.SemaphoreType.DMA((MAXREQ,)),
            ],
        ),
        name="filter_late",
    )(req_block, place, *arrived, *tables)


def final_pick(slot):
    shape = (2 * TM * ROWS, 2 * BLOCKW)
    row, column = (lax.broadcasted_iota(jnp.int32, shape, dim) for dim in range(2))
    place = (row // ROWS) * SHARE + row % SHARE + BLOCKW * ((row // 4) % 2)
    return jnp.where((place == column) & ((row // 2) % 2 == slot), 1.0, 0.0).astype(jnp.bfloat16)


def unpack_kernel(start_ref, frames_ref, count_ref, place_ref, early_ref, late_ref, out_ref, turned_ref, pick_ref):
    slot = pl.program_id(1)

    @pl.when((slot == 0) & (pl.program_id(0) == 0))
    def _():
        for which in range(2):
            pick_ref[which] = final_pick(which)

    owner = place_ref[0]
    hop = place_ref[1] * HOPS_DEV + pl.program_id(0)
    begin = start_ref[owner, slot]
    active = (slot < count_ref[owner]) & (hop >= begin) & (hop < begin + frames_ref[owner, slot])

    @pl.when(active)
    def _():
        rows = jnp.concatenate([early_ref[:, 0, 0], late_ref[:, 0, 0]], axis=0)
        rows = rows.astype(jnp.float32).reshape(2 * TM * ROWS, NFINE).astype(jnp.bfloat16)
        for m1 in range(RADIX):
            columns = lax.dot_general(
                rows[:, m1 * LANES : (m1 + 1) * LANES],
                pick_ref[slot % 2],
                (((0,), (0,)), ((), ())),
                preferred_element_type=jnp.float32,
            )
            for part in range(2):
                turned_ref[part, pl.ds(m1, LANES, stride=RADIX), :] = columns[:, part * LANES : (part + 1) * LANES]
        out_ref[0, 0, 0] = turned_ref[...].astype(jnp.bfloat16)

    @pl.when(jnp.logical_not(active))
    def _():
        out_ref[...] = jnp.zeros_like(out_ref)


def unpack(early, late, req_start, req_frames, req_count, place):
    back_spec = pl.BlockSpec((TM, 1, 1, ROWS, NFINE), lambda h, q, *refs: (0, h, q // 2, 0, 0))
    return pl.pallas_call(
        unpack_kernel,
        out_shape=jax.ShapeDtypeStruct((HOPS_DEV, 1, MAXREQ, 2, NFINE, BLOCKW), jnp.bfloat16),
        grid_spec=pltpu.PrefetchScalarGridSpec(
            num_scalar_prefetch=4,
            grid=(HOPS_DEV, MAXREQ),
            in_specs=[
                back_spec,
                back_spec,
            ],
            out_specs=pl.BlockSpec(
                (1, 1, 1, 2, NFINE, BLOCKW), lambda h, q, *refs: (h, 0, q, 0, 0, 0)
            ),
            scratch_shapes=[
                pltpu.VMEM((2, NFINE, BLOCKW), jnp.float32),
                pltpu.VMEM((2, 2 * TM * ROWS, 2 * BLOCKW), jnp.bfloat16),
            ],
        ),
        name="unpack",
    )(req_start, req_frames, req_count, place, early, late)


def over_tm(array):
    return lax.all_to_all(array, "tm", split_axis=0, concat_axis=0, tiled=True)


def along_chan(arrays):
    return [arrays[0]] + [
        lax.ppermute(arrays[d], "chan", [(s, (s + d) % OWNERS) for s in range(OWNERS)])
        for d in range(1, OWNERS)
    ]


def shards(coarse, prototype, req_block, req_start, req_frames, req_count):
    column = lax.axis_index("chan").astype(jnp.int32)
    place = jnp.stack([column, lax.axis_index("tm").astype(jnp.int32)])
    tables = (prototype, *(jnp.asarray(table) for table in dft_tables()))
    late = pack_late(coarse, jnp.asarray(late_pick()), req_block, req_count, place)
    early = pack_early(coarse, jnp.asarray(lower_half()), req_block, req_count, place)
    late = over_tm(late)
    early = choose(along_chan(early), jnp.asarray(early_pick()), req_block, place)
    late, early = lax.optimization_barrier((late, early))
    early = over_tm(early)
    late = along_chan([late] + [late[:, d] for d in range(1, OWNERS)])
    early = filter_early(early, tables)
    _, *late = lax.optimization_barrier((early, *late))
    early = over_tm(early)
    late = over_tm(filter_late(late, tables, req_block, place))
    return unpack(early, late, req_start, req_frames, req_count, place)


def solution(mesh):
    return jax.shard_map(
        shards,
        mesh=mesh,
        in_specs=(P(None, "tm", "chan"), P(), P(), P(), P(), P()),
        out_specs=P("tm", "chan", None, None, None, None),
        check_vma=False,
    )
```

time: 289 us -> 319 us (1.10)
  blocking collectives: 231 us -> 90.9 us
  waiting for transfers between devices: 0 us -> 116 us
  starting transfers between devices: 0 us -> 27.3 us
  Pallas kernels: 55 us -> 74.1 us
  local copies, waits for them, and re-layouts: 0 us -> 7.43 us
    all_to_all x2, blocking collectives: 231 us -> 90.9 us  [over_tm(): return lax.all_to_all(array, 'tm', split_axis=0, concat_axis=0, tiled=True)]
    ppermute x0 -> x6, waiting for transfers between devices: none -> 84 us  [along_chan(): lax.ppermute(arrays[d], 'chan', [(s, (s + d) % OWNERS) for s in range(OWN...]
    all_to_all x0 -> x2, waiting for transfers between devices: none -> 32.1 us  [over_tm(): return lax.all_to_all(array, 'tm', split_axis=0, concat_axis=0, tiled=True)]
    pallas_call x2 -> x5, Pallas kernels: 44 us -> 62.7 us  [the longest x1 18.9 us: filter_late(): pl.pallas_call(late_kernel, out_shape=RESULT, grid_spec=pltpu.PrefetchSca...]
    all_to_all x0 -> x2, starting transfers between devices: none -> 15.8 us  [over_tm(): return lax.all_to_all(array, 'tm', split_axis=0, concat_axis=0, tiled=True)]
    ppermute x0 -> x6, starting transfers between devices: none -> 11.5 us  [along_chan(): lax.ppermute(arrays[d], 'chan', [(s, (s + d) % OWNERS) for s in range(OWN...]
    squeeze x0 -> x1, local copies, waits for them, and re-layouts: none -> 4.62 us  [shards(): late = along_chan([late] + [late[:, d] for d in range(1, OWNERS)])]
  transfers between devices with their start and end apart: 0 -> 8, of which waited for: 0 -> 5; matrix products, arithmetic and copies ran while one was open for 0% -> 1% of each run, Pallas kernels for 0% -> 11%
where the time goes in v2:
time: 319 us; the launch traced here: 317 us
  waiting for transfers between devices  116 us (36%)
  blocking collectives  90.9 us (28%)
  Pallas kernels  74.1 us (23%)
  starting transfers between devices  27.3 us (9%)
  local copies, waits for them, and re-layouts  7.43 us (2%)
    all_to_all x2, blocking collectives, over_tm(): return lax.all_to_all(array, 'tm', split_axis=0, concat_axis=0, tiled=True)  90.9 us
    ppermute x6, waiting for transfers between devices, along_chan(): lax.ppermute(arrays[d], 'chan', [(s, (s + d) % OWNERS) for s in range(OWN...  84 us
    all_to_all x2, waiting for transfers between devices, over_tm(): return lax.all_to_all(array, 'tm', split_axis=0, concat_axis=0, tiled=True)  32.1 us
    pallas_call x1, Pallas kernels, filter_late(): pl.pallas_call(late_kernel, out_shape=RESULT, grid_spec=pltpu.PrefetchSca...  18.9 us
    all_to_all x2, starting transfers between devices, over_tm(): return lax.all_to_all(array, 'tm', split_axis=0, concat_axis=0, tiled=True)  15.8 us
    pallas_call x1, Pallas kernels, filter_early(): pl.pallas_call(early_kernel, out_shape=RESULT, grid=(MAXREQ // 2,), in_sp...  15.7 us
    ppermute x6, starting transfers between devices, along_chan(): lax.ppermute(arrays[d], 'chan', [(s, (s + d) % OWNERS) for s in range(OWN...  11.5 us
    pallas_call x1, Pallas kernels, unpack(): pl.pallas_call(unpack_kernel, out_shape=jax.ShapeDtypeStruct((HOPS_DEV, 1...  11.4 us
  transfers between devices with their start and end apart: 8, of which 5 were waited for; matrix products, arithmetic and copies ran while one was open for 1% of the time, Pallas kernels for 11%

profile of v2, /device:TPU:0, one launch (start us, length us, event | category | flops | bytes accessed | tf_op | source)
XLA Modules:
  0.0 316.5 jit_solution(13601288953101645233)
XLA Ops:
  0.0 0.6 pad_add_fusion.place_ref
  0.6 10.4 %pack_late.1 = bf16[32,4,3,8,1024]{4,3,2,1,0:T(8,128)(2,1)} custom-call(s32[4,4]{1,0:T(4,128)} %block_ref.7, s32[4]{0:T(128)} %count_ref.5, s32[2]{0:T(128)} %pad_add_fusion.place_ref, bf16[2,3072,1024]{2,1,0:T(8,128)(2,1)} %x_ref.1, bf16[2,3072,1024]{2,1,0:T(8,128)(2,1)} %x_ref.1, bf16[256,512]{1,0:T(8,128)(2,1)} %constant.21.clone.pick_ref), custom_call_target="tpu_custom_call" | custom-call | tf_op jit(solution)/shard_map/pack_late/pallas_call | solution.py:129
  11.0 8.5 %all-to-all-start = ((bf16[32,4,3,8,1024]{4,3,2,1,0:T(8,128)(2,1)}), bf16[32,4,3,8,1024]{4,3,2,1,0:T(8,128)(2,1)}, u32[]{:S(2)}, u32[]{:S(2)}) async-start(bf16[32,4,3,8,1024]{4,3,2,1,0:T(8,128)(2,1)} %pack_late.1), calls=%async_computation | async-start | bytes 12582912 | tf_op jit(solution)/shard_map/all_to_all | solution.py:431
  19.5 10.7 %pack_early.1 = (bf16[2,3,1024,128]{3,2,1,0:T(8,128)(2,1)}, bf16[2,3,1024,128]{3,2,1,0:T(8,128)(2,1)}, bf16[2,3,1024,128]{3,2,1,0:T(8,128)(2,1)}, bf16[2,3,1024,128]{3,2,1,0:T(8,128)(2,1)}) custom-call(s32[4,4]{1,0:T(4,128)} %block_ref.7, s32[4]{0:T(128)} %count_ref.5, s32[2]{0:T(128)} %pad_add_fusion.place_ref, bf16[2,3072,1024]{2,1,0:T(8,128)(2,1)} %x_ref.1, ...), custom_call_target="tpu_custom_call" | custom-call | tf_op jit(solution)/shard_map/pack_early/pallas_call | solution.py:89
  30.3 2.2 collective-permute-start
  32.4 2.0 collective-permute-start.1
  34.4 2.3 collective-permute-start.2
  36.7 31.5 %collective-permute-done.a1 = bf16[2,3,1024,128]{3,2,1,0:T(8,128)(2,1)S(1)} collective-permute-done((bf16[2,3,1024,128]{3,2,1,0:T(8,128)(2,1)}, bf16[2,3,1024,128]{3,2,1,0:T(8,128)(2,1)S(1)}, u32[]{:S(2)}, u32[]{:S(2)}) %collective-permute-start) | collective-permute-done | bytes 1572896 | tf_op jit(solution)/shard_map/ppermute | solution.py:436
  68.2 0.0 copy-start.2
  68.2 34.6 %collective-permute-done.1.a2 = bf16[2,3,1024,128]{3,2,1,0:T(8,128)(2,1)S(1)} collective-permute-done((bf16[2,3,1024,128]{3,2,1,0:T(8,128)(2,1)}, bf16[2,3,1024,128]{3,2,1,0:T(8,128)(2,1)S(1)}, u32[]{:S(2)}, u32[]{:S(2)}) %collective-permute-start.1) | collective-permute-done | bytes 1572896 | tf_op jit(solution)/shard_map/ppermute | solution.py:436
  102.8 0.0 collective-permute-done.2.a3
  102.8 0.0 copy-done.2
  102.8 1.1 copy-done.3
  104.0 6.9 %choose.1 = bf16[32,2,3,8,1024]{4,3,2,1,0:T(8,128)(2,1)} custom-call(s32[4,4]{1,0:T(4,128)} %block_ref.7, s32[2]{0:T(128)} %pad_add_fusion.place_ref, bf16[2,3,1024,128]{3,2,1,0:T(8,128)(2,1)} %get-tuple-element.15.a0, bf16[2,3,1024,128]{3,2,1,0:T(8,128)(2,1)} %copy-done.2, bf16[2,3,1024,128]{3,2,1,0:T(8,128)(2,1)} %copy-done.3, ...), custom_call_target="tpu_custom_call" | custom-call | tf_op jit(solution)/shard_map/choose/pallas_call | solution.py:184
  110.9 0.0 all-to-all-done.a0
  110.9 7.3 %all-to-all-start.1 = ((bf16[32,2,3,8,1024]{4,3,2,1,0:T(8,128)(2,1)}), bf16[32,2,3,8,1024]{4,3,2,1,0:T(8,128)(2,1)S(1)}, u32[]{:S(2)}, u32[]{:S(2)}) async-start(bf16[32,2,3,8,1024]{4,3,2,1,0:T(8,128)(2,1)} %choose.1), calls=%async_computation.1 | async-start | bytes 6291456 | tf_op jit(solution)/shard_map/all_to_all | solution.py:431
  118.2 4.6 %slice_bitcast_fusion = (bf16[32,3,8,1024]{3,2,1,0:T(8,128)(2,1)}, bf16[32,3,8,1024]{3,2,1,0:T(8,128)(2,1)}, bf16[32,3,8,1024]{3,2,1,0:T(8,128)(2,1)}) fusion(bf16[32,4,3,8,1024]{4,3,2,1,0:T(8,128)(2,1)} %all-to-all-done.a0), kind=kLoop, calls=%fused_computation | loop fusion | bytes 9437184 | tf_op jit(solution)/shard_map/squeeze | solution.py:451
  122.8 0.4 collective-permute-start.3
  123.1 2.4 collective-permute-start.4
  125.5 2.3 collective-permute-start.5
  127.9 32.1 %all-to-all-done.1.x_ref = bf16[32,2,3,8,1024]{4,3,2,1,0:T(8,128)(2,1)S(1)} async-done(((bf16[32,2,3,8,1024]{4,3,2,1,0:T(8,128)(2,1)}), bf16[32,2,3,8,1024]{4,3,2,1,0:T(8,128)(2,1)S(1)}, u32[]{:S(2)}, u32[]{:S(2)}) %all-to-all-start.1) | async-done | bytes 3145760 | tf_op jit(solution)/shard_map/all_to_all | solution.py:431
  159.9 1.7 copy-done
  161.6 15.7 %filter_early.1 = bf16[32,3,2,8,1024]{4,3,2,1,0:T(8,128)(2,1)} custom-call(bf16[32,2,3,8,1024]{4,3,2,1,0:T(8,128)(2,1)} %copy-done, f32[16,1024]{1,0:T(8,128)} %proto_ref.1, bf16[8,128,256]{2,1,0:T(8,128)(2,1)} %constant.19.clone.refs_1_.high_ref, bf16[8,128,256]{2,1,0:T(8,128)(2,1)} %constant.20.clone.refs_2_.low_ref), custom_call_target="tpu_custom_call" | custom-call | tf_op jit(solution)/shard_map/filter_early/pallas_call | solution.py:333
  177.3 17.3 %collective-permute-done.3.a1 = bf16[32,3,8,1024]{3,2,1,0:T(8,128)(2,1)} collective-permute-done((bf16[32,3,8,1024]{3,2,1,0:T(8,128)(2,1)}, bf16[32,3,8,1024]{3,2,1,0:T(8,128)(2,1)}, u32[]{:S(2)}, u32[]{:S(2)}) %collective-permute-start.3) | collective-permute-done | bytes 1572896 | tf_op jit(solution)/shard_map/ppermute | solution.py:436
  194.6 0.0 collective-permute-done.4.a2
  194.6 0.6 collective-permute-done.5.a3
  195.2 18.9 %filter_late.1 = bf16[32,3,2,8,1024]{4,3,2,1,0:T(8,128)(2,1)} custom-call(s32[4,4]{1,0:T(4,128)} %block_ref.7, s32[2]{0:T(128)} %pad_add_fusion.place_ref, bf16[32,4,3,8,1024]{4,3,2,1,0:T(8,128)(2,1)} %all-to-all-done.a0, bf16[32,3,8,1024]{3,2,1,0:T(8,128)(2,1)} %collective-permute-done.3.a1, bf16[32,3,8,1024]{3,2,1,0:T(8,128)(2,1)} %collective-permute-done.4.a2, ...), custom_call_target="tpu_custom_call" | custom-call | tf_op jit(solution)/shard_map/filter_late/pallas_call | solution.py:348
  214.1 0.0 copy-start.1
  214.2 47.4 %all_to_all.20.late_ref = bf16[32,3,2,8,1024]{4,3,2,1,0:T(8,128)(2,1)} all-to-all(bf16[32,3,2,8,1024]{4,3,2,1,0:T(8,128)(2,1)} %filter_late.1), channel_id=1, replica_groups=mesh['tm'=32,'chan'=4] {'tm'}, dimensions={0} | all-to-all | bytes 6291456 | tf_op jit(solution)/shard_map/all_to_all | solution.py:431
  261.6 0.0 copy-done.1
  261.6 43.5 %all_to_all.21.early_ref = bf16[32,3,2,8,1024]{4,3,2,1,0:T(8,128)(2,1)} all-to-all(bf16[32,3,2,8,1024]{4,3,2,1,0:T(8,128)(2,1)S(1)} %copy-done.1), channel_id=1, replica_groups=mesh['tm'=32,'chan'=4] {'tm'}, dimensions={0} | all-to-all | bytes 6291456 | tf_op jit(solution)/shard_map/all_to_all | solution.py:431
  305.1 11.4 %unpack.1 = bf16[3,1,4,2,1024,128]{5,4,3,2,1,0:T(8,128)(2,1)} custom-call(s32[4,4]{1,0:T(4,128)} %start_ref.1, s32[4,4]{1,0:T(4,128)} %frames_ref.1, s32[4]{0:T(128)} %count_ref.5, s32[2]{0:T(128)} %pad_add_fusion.place_ref, bf16[32,3,2,8,1024]{4,3,2,1,0:T(8,128)(2,1)} %all_to_all.21.early_ref, bf16[32,3,2,8,1024]{4,3,2,1,0:T(8,128)(2,1)} %all_to_all.20.late_ref), custom_call_target="tpu_custom_call" | custom-call | tf_op jit(solution)/shard_map/unpack/pallas_call | solution.py:408
  (2 shorter events, 0.0 us)
Async XLA Ops:
  11.0 99.9 %all-to-all-start = ((bf16[32,4,3,8,1024]{4,3,2,1,0:T(8,128)(2,1)}), bf16[32,4,3,8,1024]{4,3,2,1,0:T(8,128)(2,1)}, u32[]{:S(2)}, u32[]{:S(2)}) async-start(bf16[32,4,3,8,1024]{4,3,2,1,0:T(8,128)(2,1)} %pack_late.1), calls=%async_computation | async-start | bytes 12582912 | tf_op jit(solution)/shard_map/all_to_all | solution.py:431
  30.3 37.9 %collective-permute-start = (bf16[2,3,1024,128]{3,2,1,0:T(8,128)(2,1)}, bf16[2,3,1024,128]{3,2,1,0:T(8,128)(2,1)S(1)}, u32[]{:S(2)}, u32[]{:S(2)}) collective-permute-start(bf16[2,3,1024,128]{3,2,1,0:T(8,128)(2,1)} %get-tuple-element.16), channel_id=1, source_target_pairs={{0,1},{1,2},{2,3},{3,0},{4,5},{5,6},{6,7},{7,4},{8,9},{9,10},{10,1... | collective-permute-start | bytes 4718600 | tf_op jit(solution)/shard_map/ppermute | solution.py:436
  32.4 70.4 %collective-permute-start.1 = (bf16[2,3,1024,128]{3,2,1,0:T(8,128)(2,1)}, bf16[2,3,1024,128]{3,2,1,0:T(8,128)(2,1)S(1)}, u32[]{:S(2)}, u32[]{:S(2)}) collective-permute-start(bf16[2,3,1024,128]{3,2,1,0:T(8,128)(2,1)} %get-tuple-element.17), channel_id=1, source_target_pairs={{0,2},{1,3},{2,0},{3,1},{4,6},{5,7},{6,4},{7,5},{8,10},{9,11},{10,... | collective-permute-start | bytes 4718600 | tf_op jit(solution)/shard_map/ppermute | solution.py:436
  34.4 68.4 %collective-permute-start.2 = (bf16[2,3,1024,128]{3,2,1,0:T(8,128)(2,1)}, bf16[2,3,1024,128]{3,2,1,0:T(8,128)(2,1)}, u32[]{:S(2)}, u32[]{:S(2)}) collective-permute-start(bf16[2,3,1024,128]{3,2,1,0:T(8,128)(2,1)} %get-tuple-element.18), channel_id=1, source_target_pairs={{0,3},{1,0},{2,1},{3,2},{4,7},{5,4},{6,5},{7,6},{8,11},{9,8},{10,9... | collective-permute-start | bytes 4718600 | tf_op jit(solution)/shard_map/ppermute | solution.py:436
  68.2 34.6 %copy-start.2 = (bf16[2,3,1024,128]{3,2,1,0:T(8,128)(2,1)}, bf16[2,3,1024,128]{3,2,1,0:T(8,128)(2,1)S(1)}, u32[]{:S(2)}) copy-start(bf16[2,3,1024,128]{3,2,1,0:T(8,128)(2,1)S(1)} %collective-permute-done.a1) | copy-start | bytes 4718596
  102.8 1.1 copy-start.3
  110.9 49.0 %all-to-all-start.1 = ((bf16[32,2,3,8,1024]{4,3,2,1,0:T(8,128)(2,1)}), bf16[32,2,3,8,1024]{4,3,2,1,0:T(8,128)(2,1)S(1)}, u32[]{:S(2)}, u32[]{:S(2)}) async-start(bf16[32,2,3,8,1024]{4,3,2,1,0:T(8,128)(2,1)} %choose.1), calls=%async_computation.1 | async-start | bytes 6291456 | tf_op jit(solution)/shard_map/all_to_all | solution.py:431
  122.8 71.8 %collective-permute-start.3 = (bf16[32,3,8,1024]{3,2,1,0:T(8,128)(2,1)}, bf16[32,3,8,1024]{3,2,1,0:T(8,128)(2,1)}, u32[]{:S(2)}, u32[]{:S(2)}) collective-permute-start(bf16[32,3,8,1024]{3,2,1,0:T(8,128)(2,1)} %get-tuple-element.27), channel_id=1, source_target_pairs={{0,1},{1,2},{2,3},{3,0},{4,5},{5,6},{6,7},{7,4},{8,9},{9,10},{10,1... | collective-permute-start | bytes 4718600 | tf_op jit(solution)/shard_map/ppermute | solution.py:436
  123.1 71.4 %collective-permute-start.4 = (bf16[32,3,8,1024]{3,2,1,0:T(8,128)(2,1)}, bf16[32,3,8,1024]{3,2,1,0:T(8,128)(2,1)}, u32[]{:S(2)}, u32[]{:S(2)}) collective-permute-start(bf16[32,3,8,1024]{3,2,1,0:T(8,128)(2,1)} %get-tuple-element.26), channel_id=1, source_target_pairs={{0,2},{1,3},{2,0},{3,1},{4,6},{5,7},{6,4},{7,5},{8,10},{9,11},{10,... | collective-permute-start | bytes 4718600 | tf_op jit(solution)/shard_map/ppermute | solution.py:436
  125.5 69.7 %collective-permute-start.5 = (bf16[32,3,8,1024]{3,2,1,0:T(8,128)(2,1)}, bf16[32,3,8,1024]{3,2,1,0:T(8,128)(2,1)}, u32[]{:S(2)}, u32[]{:S(2)}) collective-permute-start(bf16[32,3,8,1024]{3,2,1,0:T(8,128)(2,1)} %get-tuple-element.25), channel_id=1, source_target_pairs={{0,3},{1,0},{2,1},{3,2},{4,7},{5,4},{6,5},{7,6},{8,11},{9,8},{10,9... | collective-permute-start | bytes 4718600 | tf_op jit(solution)/shard_map/ppermute | solution.py:436
  159.9 1.7 copy-start
  214.1 47.5 %copy-start.1 = (bf16[32,3,2,8,1024]{4,3,2,1,0:T(8,128)(2,1)S(1)}, bf16[32,3,2,8,1024]{4,3,2,1,0:T(8,128)(2,1)}, u32[]{:S(2)}) copy-start(bf16[32,3,2,8,1024]{4,3,2,1,0:T(8,128)(2,1)} %filter_early.1) | copy-start | bytes 9437188

commit v3 on v2

--- a/solution.py
+++ b/solution.py
@@ -42,13 +42,6 @@
     return pick.reshape(TM * ROWS, 2 * BLOCKW).astype(ml_dtypes.bfloat16)
 
 
-def lower_half():
-    pick = np.zeros((2, BLOCKW, 2, HALF), np.float32)
-    for part, column in np.ndindex(2, HALF):
-        pick[part, column, part, column] = 1
-    return pick.reshape(2 * BLOCKW, BLOCKW).astype(ml_dtypes.bfloat16)
-
-
 def dft_tables():
     k2 = np.arange(LANES)[None, :, None]
     m = np.arange(RADIX)[:, None, None] + RADIX * np.arange(LANES)[None, None, :]
@@ -71,18 +64,17 @@
     return chosen
 
 
-def pack_early_kernel(block_ref, count_ref, place_ref, x_ref, lower_ref, *out_refs):
+def pack_early_kernel(block_ref, count_ref, place_ref, x_ref, *out_refs):
     def write(out_ref):
         for hop in range(HOPS_DEV):
             rows = pl.ds(hop * NFINE, NFINE)
-            both = jnp.concatenate([x_ref[0, rows, :], x_ref[1, rows, :]], axis=1)
-            out_ref[0, hop] = jnp.dot(both, lower_ref[...], preferred_element_type=jnp.float32).astype(jnp.bfloat16)
+            out_ref[0, hop] = jnp.concatenate([x_ref[0, rows, :HALF], x_ref[1, rows, :HALF]], axis=1)
 
     for shift, out_ref in enumerate(out_refs):
         pl.when(pl.program_id(0) == shift)(lambda out_ref=out_ref: write(out_ref))
 
 
-def pack_early(coarse, lower, req_block, req_count, place):
+def pack_early(coarse, req_block, req_count, place):
     def out_map(own, d, r):
         return (jnp.where(d < own, 0, jnp.where(d > own, PAIR - 1, r)), 0, 0, 0)
 
@@ -97,7 +89,6 @@
                     (2, HOPS_DEV * NFINE, BLOCKW),
                     lambda d, r, *refs: (0, 0, wanted_block(d, r, *refs)),
                 ),
-                pl.BlockSpec((2 * BLOCKW, BLOCKW), lambda d, r, *refs: (0, 0)),
             ],
             out_specs=[
                 pl.BlockSpec(
@@ -107,23 +98,21 @@
             ],
         ),
         name="pack_early",
-    )(req_block, req_count, place, coarse, lower)
+    )(req_block, req_count, place, coarse)
 
 
 def pack_late_kernel(block_ref, count_ref, place_ref, x0_ref, x1_ref, pick_ref, out_ref):
-    for hop in range(HOPS_DEV):
-        rows = pl.ds(hop * NFINE, NFINE)
-        wide = jnp.concatenate([x0_ref[0, rows, :], x0_ref[1, rows, :], x1_ref[0, rows, :], x1_ref[1, rows, :]], axis=1)
-        turned = lax.dot_general(
-            pick_ref[...], wide, (((1,), (1,)), ((), ())), preferred_element_type=jnp.float32
-        )
-        out_ref[:, 0, hop] = turned.reshape(TM, ROWS, NFINE).astype(jnp.bfloat16)
+    wide = jnp.concatenate([x0_ref[0], x0_ref[1], x1_ref[0], x1_ref[1]], axis=1)
+    turned = lax.dot_general(
+        pick_ref[...], wide, (((1,), (1,)), ((), ())), preferred_element_type=jnp.float32
+    )
+    out_ref[:, 0, 0] = turned.reshape(TM, ROWS, NFINE).astype(jnp.bfloat16)
 
 
 def pack_late(coarse, pick, req_block, req_count, place):
     def block_spec(rank):
         return pl.BlockSpec(
-            (2, HOPS_DEV * NFINE, BLOCKW), lambda d, *refs: (0, 0, wanted_block(d, rank, *refs))
+            (2, NFINE, BLOCKW), lambda d, h, *refs: (0, h, wanted_block(d, rank, *refs))
         )
 
     return pl.pallas_call(
@@ -131,14 +120,14 @@
         out_shape=jax.ShapeDtypeStruct((TM, OWNERS, HOPS_DEV, ROWS, NFINE), jnp.bfloat16),
         grid_spec=pltpu.PrefetchScalarGridSpec(
             num_scalar_prefetch=3,
-            grid=(OWNERS,),
+            grid=(OWNERS, HOPS_DEV),
             in_specs=[
                 block_spec(0),
                 block_spec(1),
-                pl.BlockSpec((TM * ROWS, PAIR * 2 * BLOCKW), lambda d, *refs: (0, 0)),
+                pl.BlockSpec((TM * ROWS, PAIR * 2 * BLOCKW), lambda d, h, *refs: (0, 0)),
             ],
             out_specs=pl.BlockSpec(
-                (TM, 1, HOPS_DEV, ROWS, NFINE), lambda d, *refs: (0, d, 0, 0, 0)
+                (TM, 1, 1, ROWS, NFINE), lambda d, h, *refs: (0, d, h, 0, 0)
             ),
         ),
         name="pack_late",
@@ -314,6 +303,7 @@
     ]
 
 
+COST = pl.CostEstimate(flops=18_000_000_000, transcendentals=0, bytes_accessed=2 * MAXREQ * HOPS * 4 * NFINE * 2)
 RESULT = jax.ShapeDtypeStruct((TM, HOPS_DEV, MAXREQ // 2, ROWS, NFINE), jnp.bfloat16)
 
 
@@ -340,6 +330,7 @@
         ],
         out_specs=result_spec(),
         scratch_shapes=work_space(),
+        cost_estimate=COST,
         name="filter_early",
     )(gathered, *tables)
 
@@ -359,6 +350,7 @@
                 pltpu.SemaphoreType.DMA((MAXREQ,)),
             ],
         ),
+        cost_estimate=COST,
         name="filter_late",
     )(req_block, place, *arrived, *tables)
 
@@ -387,15 +379,14 @@
     def _():
         rows = jnp.concatenate([early_ref[:, 0, 0], late_ref[:, 0, 0]], axis=0)
         rows = rows.astype(jnp.float32).reshape(2 * TM * ROWS, NFINE).astype(jnp.bfloat16)
+        columns = lax.dot_general(
+            rows, pick_ref[slot % 2], (((0,), (0,)), ((), ())), preferred_element_type=jnp.float32
+        )
         for m1 in range(RADIX):
-            columns = lax.dot_general(
-                rows[:, m1 * LANES : (m1 + 1) * LANES],
-                pick_ref[slot % 2],
-                (((0,), (0,)), ((), ())),
-                preferred_element_type=jnp.float32,
-            )
             for part in range(2):
-                turned_ref[part, pl.ds(m1, LANES, stride=RADIX), :] = columns[:, part * LANES : (part + 1) * LANES]
+                turned_ref[part, pl.ds(m1, LANES, stride=RADIX), :] = columns[
+                    m1 * LANES : (m1 + 1) * LANES, part * BLOCKW : (part + 1) * BLOCKW
+                ]
         out_ref[0, 0, 0] = turned_ref[...].astype(jnp.bfloat16)
 
     @pl.when(jnp.logical_not(active))
@@ -443,7 +434,7 @@
     place = jnp.stack([column, lax.axis_index("tm").astype(jnp.int32)])
     tables = (prototype, *(jnp.asarray(table) for table in dft_tables()))
     late = pack_late(coarse, jnp.asarray(late_pick()), req_block, req_count, place)
-    early = pack_early(coarse, jnp.asarray(lower_half()), req_block, req_count, place)
+    early = pack_early(coarse, req_block, req_count, place)
     late = over_tm(late)
     early = choose(along_chan(early), jnp.asarray(early_pick()), req_block, place)
     late, early = lax.optimization_barrier((late, early))
@@ -451,8 +442,8 @@
     late = along_chan([late] + [late[:, d] for d in range(1, OWNERS)])
     early = filter_early(early, tables)
     _, *late = lax.optimization_barrier((early, *late))
-    early = over_tm(early)
-    late = over_tm(filter_late(late, tables, req_block, place))
+    early, late = lax.optimization_barrier((over_tm(early), filter_late(late, tables, req_block, place)))
+    late = over_tm(late)
     return unpack(early, late, req_start, req_frames, req_count, place)
 
 

time: 319 us -> 286 us (0.90)
  blocking collectives: 90.9 us -> 44.6 us
  waiting for transfers between devices: 116 us -> 124 us
  Pallas kernels: 74.1 us -> 78.4 us
    all_to_all x2 -> x1, blocking collectives: 90.9 us -> 44.6 us  [over_tm(): return lax.all_to_all(array, 'tm', split_axis=0, concat_axis=0, tiled=True)]
    all_to_all x2 -> x3, waiting for transfers between devices: 32.1 us -> 42.7 us  [over_tm(): return lax.all_to_all(array, 'tm', split_axis=0, concat_axis=0, tiled=True)]
    all_to_all x2 -> x3, starting transfers between devices: 15.8 us -> 19.9 us  [over_tm(): return lax.all_to_all(array, 'tm', split_axis=0, concat_axis=0, tiled=True)]
    pallas_call x1, Pallas kernels: 10.4 us -> 14.4 us  [pack_late(): pl.pallas_call(pack_late_kernel, out_shape=jax.ShapeDtypeStruct((TM, OWNE...]
  transfers between devices with their start and end apart: 8 -> 9, of which waited for: 5 -> 6; matrix products, arithmetic and copies ran while one was open for 1% -> 2% of each run, Pallas kernels for 11% -> 18%
where the time goes in v3:
time: 286 us; the launch traced here: 284 us
  waiting for transfers between devices  124 us (43%)
  Pallas kernels  78.4 us (27%)
  blocking collectives  44.6 us (16%)
  starting transfers between devices  29.2 us (10%)
  local copies, waits for them, and re-layouts  7.44 us (3%)
    ppermute x6, waiting for transfers between devices, along_chan(): lax.ppermute(arrays[d], 'chan', [(s, (s + d) % OWNERS) for s in range(OWN...  81.4 us
    all_to_all x1, blocking collectives, over_tm(): return lax.all_to_all(array, 'tm', split_axis=0, concat_axis=0, tiled=True)  44.6 us
    all_to_all x3, waiting for transfers between devices, over_tm(): return lax.all_to_all(array, 'tm', split_axis=0, concat_axis=0, tiled=True)  42.7 us
    all_to_all x3, starting transfers between devices, over_tm(): return lax.all_to_all(array, 'tm', split_axis=0, concat_axis=0, tiled=True)  19.9 us
    pallas_call x1, Pallas kernels, filter_late(): pl.pallas_call(late_kernel, out_shape=RESULT, grid_spec=pltpu.PrefetchSca...  18.7 us
    pallas_call x1, Pallas kernels, filter_early(): pl.pallas_call(early_kernel, out_shape=RESULT, grid=(MAXREQ // 2,), in_sp...  15.7 us
    pallas_call x1, Pallas kernels, pack_late(): pl.pallas_call(pack_late_kernel, out_shape=jax.ShapeDtypeStruct((TM, OWNE...  14.4 us
    pallas_call x1, Pallas kernels, unpack(): pl.pallas_call(unpack_kernel, out_shape=jax.ShapeDtypeStruct((HOPS_DEV, 1...  12.7 us
  transfers between devices with their start and end apart: 9, of which 6 were waited for; matrix products, arithmetic and copies ran while one was open for 2% of the time, Pallas kernels for 18%

profile of v3, /device:TPU:0, one launch (start us, length us, event | category | flops | bytes accessed | tf_op | source)
XLA Modules:
  0.0 284.4 jit_solution(13807888283312665745)
XLA Ops:
  0.0 0.6 pad_add_fusion.place_ref
  0.6 14.4 %pack_late.1 = bf16[32,4,3,8,1024]{4,3,2,1,0:T(8,128)(2,1)} custom-call(s32[4,4]{1,0:T(4,128)} %block_ref.7, s32[4]{0:T(128)} %count_ref.5, s32[2]{0:T(128)} %pad_add_fusion.place_ref, bf16[2,3072,1024]{2,1,0:T(8,128)(2,1)} %x_ref.1, bf16[2,3072,1024]{2,1,0:T(8,128)(2,1)} %x_ref.1, bf16[256,512]{1,0:T(8,128)(2,1)} %constant.19.clone.pick_ref), custom_call_target="tpu_custom_call" | custom-call | tf_op jit(solution)/shard_map/pack_late/pallas_call | solution.py:118
  14.9 8.5 %all-to-all-start = ((bf16[32,4,3,8,1024]{4,3,2,1,0:T(8,128)(2,1)}), bf16[32,4,3,8,1024]{4,3,2,1,0:T(8,128)(2,1)}, u32[]{:S(2)}, u32[]{:S(2)}) async-start(bf16[32,4,3,8,1024]{4,3,2,1,0:T(8,128)(2,1)} %pack_late.1), calls=%async_computation | async-start | bytes 12582912 | tf_op jit(solution)/shard_map/all_to_all | solution.py:422
  23.5 10.0 %pack_early.1 = (bf16[2,3,1024,128]{3,2,1,0:T(8,128)(2,1)}, bf16[2,3,1024,128]{3,2,1,0:T(8,128)(2,1)}, bf16[2,3,1024,128]{3,2,1,0:T(8,128)(2,1)}, bf16[2,3,1024,128]{3,2,1,0:T(8,128)(2,1)}) custom-call(s32[4,4]{1,0:T(4,128)} %block_ref.7, s32[4]{0:T(128)} %count_ref.5, s32[2]{0:T(128)} %pad_add_fusion.place_ref, bf16[2,3072,1024]{2,1,0:T(8,128)(2,1)} %x_ref.1), custom_call_target="tpu_custom_call" | custom-call | tf_op jit(solution)/shard_map/pack_early/pallas_call | solution.py:81
  33.5 0.7 collective-permute-start
  34.2 4.1 %collective-permute-start.1 = (bf16[2,3,1024,128]{3,2,1,0:T(8,128)(2,1)}, bf16[2,3,1024,128]{3,2,1,0:T(8,128)(2,1)S(1)}, u32[]{:S(2)}, u32[]{:S(2)}) collective-permute-start(bf16[2,3,1024,128]{3,2,1,0:T(8,128)(2,1)} %get-tuple-element.19), channel_id=1, source_target_pairs={{0,2},{1,3},{2,0},{3,1},{4,6},{5,7},{6,4},{7,5},{8,10},{9,11},{10,... | collective-permute-start | bytes 4718600 | tf_op jit(solution)/shard_map/ppermute | solution.py:427
  38.3 0.8 collective-permute-start.2
  39.1 32.7 %collective-permute-done.a1 = bf16[2,3,1024,128]{3,2,1,0:T(8,128)(2,1)S(1)} collective-permute-done((bf16[2,3,1024,128]{3,2,1,0:T(8,128)(2,1)}, bf16[2,3,1024,128]{3,2,1,0:T(8,128)(2,1)S(1)}, u32[]{:S(2)}, u32[]{:S(2)}) %collective-permute-start) | collective-permute-done | bytes 1572896 | tf_op jit(solution)/shard_map/ppermute | solution.py:427
  71.8 0.0 copy-start.2
  71.8 34.9 %collective-permute-done.1.a2 = bf16[2,3,1024,128]{3,2,1,0:T(8,128)(2,1)S(1)} collective-permute-done((bf16[2,3,1024,128]{3,2,1,0:T(8,128)(2,1)}, bf16[2,3,1024,128]{3,2,1,0:T(8,128)(2,1)S(1)}, u32[]{:S(2)}, u32[]{:S(2)}) %collective-permute-start.1) | collective-permute-done | bytes 1572896 | tf_op jit(solution)/shard_map/ppermute | solution.py:427
  106.7 0.0 collective-permute-done.2.a3
  106.7 0.0 copy-done.2
  106.7 1.1 copy-done.3
  107.9 6.9 %choose.1 = bf16[32,2,3,8,1024]{4,3,2,1,0:T(8,128)(2,1)} custom-call(s32[4,4]{1,0:T(4,128)} %block_ref.7, s32[2]{0:T(128)} %pad_add_fusion.place_ref, bf16[2,3,1024,128]{3,2,1,0:T(8,128)(2,1)} %get-tuple-element.17.a0, bf16[2,3,1024,128]{3,2,1,0:T(8,128)(2,1)} %copy-done.2, bf16[2,3,1024,128]{3,2,1,0:T(8,128)(2,1)} %copy-done.3, ...), custom_call_target="tpu_custom_call" | custom-call | tf_op jit(solution)/shard_map/choose/pallas_call | solution.py:173
  114.8 0.0 all-to-all-done.a0
  114.8 7.3 %all-to-all-start.1 = ((bf16[32,2,3,8,1024]{4,3,2,1,0:T(8,128)(2,1)}), bf16[32,2,3,8,1024]{4,3,2,1,0:T(8,128)(2,1)S(1)}, u32[]{:S(2)}, u32[]{:S(2)}) async-start(bf16[32,2,3,8,1024]{4,3,2,1,0:T(8,128)(2,1)} %choose.1), calls=%async_computation.1 | async-start | bytes 6291456 | tf_op jit(solution)/shard_map/all_to_all | solution.py:422
  122.1 4.6 %slice_bitcast_fusion = (bf16[32,3,8,1024]{3,2,1,0:T(8,128)(2,1)}, bf16[32,3,8,1024]{3,2,1,0:T(8,128)(2,1)}, bf16[32,3,8,1024]{3,2,1,0:T(8,128)(2,1)}) fusion(bf16[32,4,3,8,1024]{4,3,2,1,0:T(8,128)(2,1)} %all-to-all-done.a0), kind=kLoop, calls=%fused_computation | loop fusion | bytes 9437184 | tf_op jit(solution)/shard_map/squeeze | solution.py:442
  126.7 0.1 collective-permute-start.3
  126.8 2.4 collective-permute-start.4
  129.2 1.2 collective-permute-start.5
  130.4 33.5 %all-to-all-done.1.x_ref = bf16[32,2,3,8,1024]{4,3,2,1,0:T(8,128)(2,1)S(1)} async-done(((bf16[32,2,3,8,1024]{4,3,2,1,0:T(8,128)(2,1)}), bf16[32,2,3,8,1024]{4,3,2,1,0:T(8,128)(2,1)S(1)}, u32[]{:S(2)}, u32[]{:S(2)}) %all-to-all-start.1) | async-done | bytes 3145760 | tf_op jit(solution)/shard_map/all_to_all | solution.py:422
  163.9 1.7 copy-done.1
  165.5 15.7 %filter_early.1 = bf16[32,3,2,8,1024]{4,3,2,1,0:T(8,128)(2,1)} custom-call(bf16[32,2,3,8,1024]{4,3,2,1,0:T(8,128)(2,1)} %copy-done.1, f32[16,1024]{1,0:T(8,128)} %proto_ref.1, bf16[8,128,256]{2,1,0:T(8,128)(2,1)} %constant.17.clone.refs_1_.high_ref, bf16[8,128,256]{2,1,0:T(8,128)(2,1)} %constant.18.clone.refs_2_.low_ref), custom_call_target="tpu_custom_call" | custom-call | flops 17999998976 | bytes 6291456 | tf_op jit(solution)/shard_map/filter_early/pallas_call | solution.py:323
  181.2 4.1 %all-to-all-start.2 = ((bf16[32,3,2,8,1024]{4,3,2,1,0:T(8,128)(2,1)}), bf16[32,3,2,8,1024]{4,3,2,1,0:T(8,128)(2,1)S(1)}, u32[]{:S(2)}, u32[]{:S(2)}) async-start(bf16[32,3,2,8,1024]{4,3,2,1,0:T(8,128)(2,1)} %filter_early.1), calls=%async_computation.2 | async-start | bytes 6291456 | tf_op jit(solution)/shard_map/all_to_all | solution.py:422
  185.3 13.2 %collective-permute-done.3.a1 = bf16[32,3,8,1024]{3,2,1,0:T(8,128)(2,1)} collective-permute-done((bf16[32,3,8,1024]{3,2,1,0:T(8,128)(2,1)}, bf16[32,3,8,1024]{3,2,1,0:T(8,128)(2,1)}, u32[]{:S(2)}, u32[]{:S(2)}) %collective-permute-start.3) | collective-permute-done | bytes 1572896 | tf_op jit(solution)/shard_map/ppermute | solution.py:427
  198.5 0.0 collective-permute-done.4.a2
  198.5 0.6 collective-permute-done.5.a3
  199.1 18.7 %filter_late.1 = bf16[32,3,2,8,1024]{4,3,2,1,0:T(8,128)(2,1)} custom-call(s32[4,4]{1,0:T(4,128)} %block_ref.7, s32[2]{0:T(128)} %pad_add_fusion.place_ref, bf16[32,4,3,8,1024]{4,3,2,1,0:T(8,128)(2,1)} %all-to-all-done.a0, bf16[32,3,8,1024]{3,2,1,0:T(8,128)(2,1)} %collective-permute-done.3.a1, bf16[32,3,8,1024]{3,2,1,0:T(8,128)(2,1)} %collective-permute-done.4.a2, ...), custom_call_target="tpu_custom_call" | custom-call | flops 17999998976 | bytes 6291456 | tf_op jit(solution)/shard_map/filter_late/pallas_call | solution.py:339
  217.9 9.2 %all-to-all-done.2.early_ref = bf16[32,3,2,8,1024]{4,3,2,1,0:T(8,128)(2,1)S(1)} async-done(((bf16[32,3,2,8,1024]{4,3,2,1,0:T(8,128)(2,1)}), bf16[32,3,2,8,1024]{4,3,2,1,0:T(8,128)(2,1)S(1)}, u32[]{:S(2)}, u32[]{:S(2)}) %all-to-all-start.2) | async-done | bytes 3145760 | tf_op jit(solution)/shard_map/all_to_all | solution.py:422
  227.1 44.6 %all_to_all.20.late_ref = bf16[32,3,2,8,1024]{4,3,2,1,0:T(8,128)(2,1)} all-to-all(bf16[32,3,2,8,1024]{4,3,2,1,0:T(8,128)(2,1)} %filter_late.1), channel_id=1, replica_groups=mesh['tm'=32,'chan'=4] {'tm'}, dimensions={0} | all-to-all | bytes 6291456 | tf_op jit(solution)/shard_map/all_to_all | solution.py:422
  271.7 0.0 copy-done
  271.7 12.7 %unpack.1 = bf16[3,1,4,2,1024,128]{5,4,3,2,1,0:T(8,128)(2,1)} custom-call(s32[4,4]{1,0:T(4,128)} %start_ref.1, s32[4,4]{1,0:T(4,128)} %frames_ref.1, s32[4]{0:T(128)} %count_ref.5, s32[2]{0:T(128)} %pad_add_fusion.place_ref, bf16[32,3,2,8,1024]{4,3,2,1,0:T(8,128)(2,1)} %copy-done, bf16[32,3,2,8,1024]{4,3,2,1,0:T(8,128)(2,1)} %all_to_all.20.late_ref), custom_call_target="tpu_custom_call" | custom-call | tf_op jit(solution)/shard_map/unpack/pallas_call | solution.py:399
  (3 shorter events, 0.0 us)
Async XLA Ops:
  14.9 99.9 %all-to-all-start = ((bf16[32,4,3,8,1024]{4,3,2,1,0:T(8,128)(2,1)}), bf16[32,4,3,8,1024]{4,3,2,1,0:T(8,128)(2,1)}, u32[]{:S(2)}, u32[]{:S(2)}) async-start(bf16[32,4,3,8,1024]{4,3,2,1,0:T(8,128)(2,1)} %pack_late.1), calls=%async_computation | async-start | bytes 12582912 | tf_op jit(solution)/shard_map/all_to_all | solution.py:422
  33.5 38.3 %collective-permute-start = (bf16[2,3,1024,128]{3,2,1,0:T(8,128)(2,1)}, bf16[2,3,1024,128]{3,2,1,0:T(8,128)(2,1)S(1)}, u32[]{:S(2)}, u32[]{:S(2)}) collective-permute-start(bf16[2,3,1024,128]{3,2,1,0:T(8,128)(2,1)} %get-tuple-element.18), channel_id=1, source_target_pairs={{0,1},{1,2},{2,3},{3,0},{4,5},{5,6},{6,7},{7,4},{8,9},{9,10},{10,1... | collective-permute-start | bytes 4718600 | tf_op jit(solution)/shard_map/ppermute | solution.py:427
  34.2 72.5 %collective-permute-start.1 = (bf16[2,3,1024,128]{3,2,1,0:T(8,128)(2,1)}, bf16[2,3,1024,128]{3,2,1,0:T(8,128)(2,1)S(1)}, u32[]{:S(2)}, u32[]{:S(2)}) collective-permute-start(bf16[2,3,1024,128]{3,2,1,0:T(8,128)(2,1)} %get-tuple-element.19), channel_id=1, source_target_pairs={{0,2},{1,3},{2,0},{3,1},{4,6},{5,7},{6,4},{7,5},{8,10},{9,11},{10,... | collective-permute-start | bytes 4718600 | tf_op jit(solution)/shard_map/ppermute | solution.py:427
  38.3 68.4 %collective-permute-start.2 = (bf16[2,3,1024,128]{3,2,1,0:T(8,128)(2,1)}, bf16[2,3,1024,128]{3,2,1,0:T(8,128)(2,1)}, u32[]{:S(2)}, u32[]{:S(2)}) collective-permute-start(bf16[2,3,1024,128]{3,2,1,0:T(8,128)(2,1)} %get-tuple-element.20), channel_id=1, source_target_pairs={{0,3},{1,0},{2,1},{3,2},{4,7},{5,4},{6,5},{7,6},{8,11},{9,8},{10,9... | collective-permute-start | bytes 4718600 | tf_op jit(solution)/shard_map/ppermute | solution.py:427
  71.8 34.9 %copy-start.2 = (bf16[2,3,1024,128]{3,2,1,0:T(8,128)(2,1)}, bf16[2,3,1024,128]{3,2,1,0:T(8,128)(2,1)S(1)}, u32[]{:S(2)}) copy-start(bf16[2,3,1024,128]{3,2,1,0:T(8,128)(2,1)S(1)} %collective-permute-done.a1) | copy-start | bytes 4718596
  106.7 1.2 copy-start.3
  114.8 49.0 %all-to-all-start.1 = ((bf16[32,2,3,8,1024]{4,3,2,1,0:T(8,128)(2,1)}), bf16[32,2,3,8,1024]{4,3,2,1,0:T(8,128)(2,1)S(1)}, u32[]{:S(2)}, u32[]{:S(2)}) async-start(bf16[32,2,3,8,1024]{4,3,2,1,0:T(8,128)(2,1)} %choose.1), calls=%async_computation.1 | async-start | bytes 6291456 | tf_op jit(solution)/shard_map/all_to_all | solution.py:422
  126.7 71.8 %collective-permute-start.3 = (bf16[32,3,8,1024]{3,2,1,0:T(8,128)(2,1)}, bf16[32,3,8,1024]{3,2,1,0:T(8,128)(2,1)}, u32[]{:S(2)}, u32[]{:S(2)}) collective-permute-start(bf16[32,3,8,1024]{3,2,1,0:T(8,128)(2,1)} %get-tuple-element.31), channel_id=1, source_target_pairs={{0,1},{1,2},{2,3},{3,0},{4,5},{5,6},{6,7},{7,4},{8,9},{9,10},{10,1... | collective-permute-start | bytes 4718600 | tf_op jit(solution)/shard_map/ppermute | solution.py:427
  126.8 71.7 %collective-permute-start.4 = (bf16[32,3,8,1024]{3,2,1,0:T(8,128)(2,1)}, bf16[32,3,8,1024]{3,2,1,0:T(8,128)(2,1)}, u32[]{:S(2)}, u32[]{:S(2)}) collective-permute-start(bf16[32,3,8,1024]{3,2,1,0:T(8,128)(2,1)} %get-tuple-element.30), channel_id=1, source_target_pairs={{0,2},{1,3},{2,0},{3,1},{4,6},{5,7},{6,4},{7,5},{8,10},{9,11},{10,... | collective-permute-start | bytes 4718600 | tf_op jit(solution)/shard_map/ppermute | solution.py:427
  129.2 69.9 %collective-permute-start.5 = (bf16[32,3,8,1024]{3,2,1,0:T(8,128)(2,1)}, bf16[32,3,8,1024]{3,2,1,0:T(8,128)(2,1)}, u32[]{:S(2)}, u32[]{:S(2)}) collective-permute-start(bf16[32,3,8,1024]{3,2,1,0:T(8,128)(2,1)} %get-tuple-element.29), channel_id=1, source_target_pairs={{0,3},{1,0},{2,1},{3,2},{4,7},{5,4},{6,5},{7,6},{8,11},{9,8},{10,9... | collective-permute-start | bytes 4718600 | tf_op jit(solution)/shard_map/ppermute | solution.py:427
  163.9 1.7 copy-start.1
  181.2 45.8 %all-to-all-start.2 = ((bf16[32,3,2,8,1024]{4,3,2,1,0:T(8,128)(2,1)}), bf16[32,3,2,8,1024]{4,3,2,1,0:T(8,128)(2,1)S(1)}, u32[]{:S(2)}, u32[]{:S(2)}) async-start(bf16[32,3,2,8,1024]{4,3,2,1,0:T(8,128)(2,1)} %filter_early.1), calls=%async_computation.2 | async-start | bytes 6291456 | tf_op jit(solution)/shard_map/all_to_all | solution.py:422
  227.1 44.6 %copy-start = (bf16[32,3,2,8,1024]{4,3,2,1,0:T(8,128)(2,1)}, bf16[32,3,2,8,1024]{4,3,2,1,0:T(8,128)(2,1)S(1)}, u32[]{:S(2)}) copy-start(bf16[32,3,2,8,1024]{4,3,2,1,0:T(8,128)(2,1)S(1)} %all-to-all-done.2.early_ref) | copy-start | bytes 9437188

commit v4 on v3

v4 whole, which is shorter than its diff:
```python
import math

import jax
import jax.numpy as jnp
import ml_dtypes
import numpy as np
from jax import lax
from jax.experimental import pallas as pl
from jax.experimental.pallas import tpu as pltpu
from jax.sharding import PartitionSpec as P

BLOCKW = 128
NFINE = 1024
TAPS = 16
HOPS_DEV = 3
MAXREQ = 4
PAIR = 2
TM = 32
OWNERS = 4
BPC = 8
HOPS = 96
HALF = BLOCKW // 2
SHARE = HALF // TM
ROWS = 8
RADIX = 8
LANES = 128
FRAMES = 84
GROUP = 21


def late_pick():
    pick = np.zeros((TM, 2, PAIR, SHARE, PAIR, 2, BLOCKW), np.float32)
    for device, part, rank, column in np.ndindex(TM, 2, PAIR, SHARE):
        pick[device, part, rank, column, rank, part, HALF + device * SHARE + column] = 1
    return pick.reshape(TM * ROWS, PAIR * 2 * BLOCKW).astype(ml_dtypes.bfloat16)


def early_pick():
    pick = np.zeros((TM, 2, 2, SHARE, 2, 2, HALF), np.float32)
    for device, part, slot, column in np.ndindex(TM, 2, 2, SHARE):
        pick[device, part, slot, column, slot, part, device * SHARE + column] = 1
    return pick.reshape(TM * ROWS, 2 * BLOCKW).astype(ml_dtypes.bfloat16)


def dft_tables():
    k2 = np.arange(LANES)[None, :, None]
    m = np.arange(RADIX)[:, None, None] + RADIX * np.arange(LANES)[None, None, :]
    angles = (k2 * m % NFINE) * (2.0 * math.pi / NFINE)
    table = np.concatenate([np.cos(angles), np.sin(angles)], axis=2) / math.sqrt(NFINE)
    high = table.astype(np.float32).astype(ml_dtypes.bfloat16)
    low = (table - high.astype(np.float64)).astype(np.float32).astype(ml_dtypes.bfloat16)
    return high, low


def wanted_block(shift, rank, block_ref, count_ref, place_ref):
    owner = (place_ref[0] + shift) % OWNERS
    seen = jnp.int32(0)
    chosen = jnp.int32(0)
    for slot in range(MAXREQ):
        block = block_ref[owner, slot]
        mine = (slot < count_ref[owner]) & (block // BPC == place_ref[0])
        chosen = jnp.where(mine & (seen == rank), block % BPC, chosen)
        seen = seen + mine.astype(jnp.int32)
    return seen > rank, chosen


def pack_kernel(block_ref, count_ref, place_ref, x_ref, pick_ref, *refs):
    late_ref, *early_refs = refs[: 1 + OWNERS]
    block_buf, late_buf, early_buf, block_sem, late_sem, early_sem = refs[1 + OWNERS :]
    wanted = [[wanted_block(d, r, block_ref, count_ref, place_ref) for r in range(PAIR)] for d in range(OWNERS)]

    def block_copy(d, r):
        columns = pl.ds(pl.multiple_of(wanted[d][r][1] * BLOCKW, BLOCKW), BLOCKW)
        return pltpu.make_async_copy(x_ref.at[:, :, columns], block_buf.at[d, r], block_sem.at[d, r])

    def late_copy(d):
        return pltpu.make_async_copy(late_buf.at[d], late_ref.at[:, d], late_sem.at[d])

    def early_copy(d, r):
        return pltpu.make_async_copy(early_buf.at[d, r], early_refs[d].at[r], early_sem.at[d, r])

    order = [(d, r) for d in (1, 2, 3, 0) for r in range(PAIR)]
    for d, r in order:
        pl.when(wanted[d][r][0])(lambda d=d, r=r: block_copy(d, r).start())
    for d, r in order:
        if r == 0:
            pl.when(wanted[d][0][0])(lambda d=d: block_copy(d, 0).wait())
            continue

        @pl.when(wanted[d][0][0] & jnp.logical_not(wanted[d][1][0]))
        def _():
            block_buf[d, 1] = jnp.zeros((2, HOPS_DEV * NFINE, BLOCKW), jnp.bfloat16)

        pl.when(wanted[d][1][0])(lambda d=d: block_copy(d, 1).wait())
        for rank in range(PAIR):

            @pl.when(wanted[d][rank][0])
            def _():
                early_buf[d, rank] = jnp.concatenate(
                    [block_buf[d, rank, 0, :, :HALF], block_buf[d, rank, 1, :, :HALF]], axis=1
                ).reshape(HOPS_DEV, NFINE, BLOCKW)
                early_copy(d, rank).start()

        @pl.when(wanted[d][0][0])
        def _():
            def one_hop(hop, carry):
                rows = pl.ds(pl.multiple_of(hop * NFINE, NFINE), NFINE)
                wide = jnp.concatenate([block_buf[d, i // 2, i % 2, rows] for i in range(2 * PAIR)], axis=1)
                turned = lax.dot_general(
                    pick_ref[...], wide, (((1,), (1,)), ((), ())), preferred_element_type=jnp.float32
                )
                late_buf[d, :, hop] = turned.reshape(TM, ROWS, NFINE).astype(jnp.bfloat16)
                return carry

            lax.fori_loop(0, HOPS_DEV, one_hop, 0)
            late_copy(d).start()

    for d, r in order:
        pl.when(wanted[d][r][0])(lambda d=d, r=r: early_copy(d, r).wait())
        if r == 0:
            pl.when(wanted[d][0][0])(lambda d=d: late_copy(d).wait())


def pack(coarse, pick, req_block, req_count, place):
    anywhere = pl.BlockSpec(memory_space=pl.ANY)
    early = jax.ShapeDtypeStruct((PAIR, HOPS_DEV, NFINE, BLOCKW), jnp.bfloat16)
    return pl.pallas_call(
        pack_kernel,
        out_shape=[jax.ShapeDtypeStruct((TM, OWNERS, HOPS_DEV, ROWS, NFINE), jnp.bfloat16)] + [early] * OWNERS,
        grid_spec=pltpu.PrefetchScalarGridSpec(
            num_scalar_prefetch=3,
            grid=(1,),
            in_specs=[anywhere, pl.BlockSpec((TM * ROWS, PAIR * 2 * BLOCKW), lambda i, *refs: (0, 0))],
            out_specs=[anywhere] * (1 + OWNERS),
            scratch_shapes=[
                pltpu.VMEM((OWNERS, PAIR, 2, HOPS_DEV * NFINE, BLOCKW), jnp.bfloat16),
                pltpu.VMEM((OWNERS, TM, HOPS_DEV, ROWS, NFINE), jnp.bfloat16),
                pltpu.VMEM((OWNERS, PAIR, HOPS_DEV, NFINE, BLOCKW), jnp.bfloat16),
                pltpu.SemaphoreType.DMA((OWNERS, PAIR)),
                pltpu.SemaphoreType.DMA((OWNERS,)),
                pltpu.SemaphoreType.DMA((OWNERS, PAIR)),
            ],
        ),
        name="pack",
    )(req_block, req_count, place, coarse, pick)


def arrival(slot, block_ref, count_ref, place_ref):
    owner = place_ref[0]
    slot = jnp.where(slot < count_ref[owner], slot, 0)
    source = block_ref[owner, slot] // BPC
    rank = jnp.int32(0)
    for other in range(MAXREQ - 1):
        same = (other < slot) & (block_ref[owner, other] // BPC == source)
        rank = rank + same.astype(jnp.int32)
    return (owner - source + OWNERS) % OWNERS, jnp.minimum(rank, PAIR - 1)


def choose_kernel(block_ref, count_ref, place_ref, a0, a1, a2, a3, pick_ref, out_ref, held_ref, out_buf, held_sem, out_sem):
    for slot in range(MAXREQ):
        shift, rank = arrival(slot, block_ref, count_ref, place_ref)
        for own, ref in enumerate((a0, a1, a2, a3)):

            @pl.when(shift == own)
            def _():
                pltpu.make_async_copy(ref.at[rank], held_ref.at[slot], held_sem.at[slot]).start()

    def out_copy(pair, hop):
        return pltpu.make_async_copy(out_buf.at[pair, hop], out_ref.at[:, pair, hop], out_sem.at[pair, hop])

    for pair in range(MAXREQ // 2):
        for slot in (2 * pair, 2 * pair + 1):
            pltpu.make_async_copy(a0.at[0], held_ref.at[slot], held_sem.at[slot]).wait()
        for hop in range(HOPS_DEV):
            both = jnp.concatenate([held_ref[pair * 2, hop], held_ref[pair * 2 + 1, hop]], axis=1)
            turned = lax.dot_general(
                pick_ref[...], both, (((1,), (1,)), ((), ())), preferred_element_type=jnp.float32
            )
            out_buf[pair, hop] = turned.reshape(TM, ROWS, NFINE).astype(jnp.bfloat16)
            out_copy(pair, hop).start()
    for pair in range(MAXREQ // 2):
        for hop in range(HOPS_DEV):
            out_copy(pair, hop).wait()


def choose(arrived, pick, req_block, req_count, place):
    anywhere = pl.BlockSpec(memory_space=pl.ANY)
    return pl.pallas_call(
        choose_kernel,
        out_shape=jax.ShapeDtypeStruct((TM, MAXREQ // 2, HOPS_DEV, ROWS, NFINE), jnp.bfloat16),
        grid_spec=pltpu.PrefetchScalarGridSpec(
            num_scalar_prefetch=3,
            grid=(1,),
            in_specs=[anywhere] * OWNERS + [pl.BlockSpec((TM * ROWS, 2 * BLOCKW), lambda i, *refs: (0, 0))],
            out_specs=anywhere,
            scratch_shapes=[
                pltpu.VMEM((MAXREQ, HOPS_DEV, NFINE, BLOCKW), jnp.bfloat16),
                pltpu.VMEM((MAXREQ // 2, HOPS_DEV, TM, ROWS, NFINE), jnp.bfloat16),
                pltpu.SemaphoreType.DMA((MAXREQ,)),
                pltpu.SemaphoreType.DMA((MAXREQ // 2, HOPS_DEV)),
            ],
        ),
        name="choose",
    )(req_block, req_count, place, *arrived, pick)


def turn(value, sign):
    return pltpu.roll(value, ROWS // 2, value.ndim - 2) * sign


def dft4(a, b, c, d, sign):
    s02, d02, s13, d13 = a + c, a - c, b + d, turn(b - d, sign)
    return s02 + s13, d02 + d13, s02 - s13, d02 - d13


def dft8(x, sign):
    half = math.sqrt(0.5)
    low = [x[i] + x[i + 4] for i in range(4)]
    high = [x[i] - x[i + 4] for i in range(4)]
    high[1] = (high[1] + turn(high[1], sign)) * half
    high[2] = turn(high[2], sign)
    high[3] = (turn(high[3], sign) - high[3]) * half
    even, odd = dft4(*low, sign), dft4(*high, sign)
    return [pair for both in zip(even, odd) for pair in both]


def transform(load, proto_ref, high_ref, low_ref, out_ref, wide_ref, fir_ref, split_ref):
    sign = jnp.where(lax.broadcasted_iota(jnp.int32, (ROWS, LANES), 0) < ROWS // 2, 1.0, -1.0)
    wide_ref[HOPS:, :, :] = jnp.zeros((FRAMES + TAPS - 1 - HOPS, ROWS, LANES), jnp.float32)
    def taps(tile, carry):
        lanes = pl.ds(pl.multiple_of(tile * LANES, LANES), LANES)
        wide_ref[:HOPS] = load(lanes)
        weights = [jnp.broadcast_to(proto_ref[tap, lanes].reshape(1, LANES), (ROWS, LANES)) for tap in range(TAPS)]

        def fir(step, inner):
            first = step * GROUP
            samples = wide_ref[pl.ds(first, GROUP + TAPS - 1)]
            total = samples[:GROUP] * weights[0]
            for tap in range(1, TAPS):
                total = total + samples[tap : tap + GROUP] * weights[tap]
            fir_ref[pl.ds(first, GROUP), :, lanes] = total
            return inner

        return lax.fori_loop(0, FRAMES // GROUP, fir, carry)

    lax.fori_loop(0, RADIX, taps, 0)

    def butterflies(step, carry):
        first = step * 2
        parts = [fir_ref[pl.ds(first, 2), :, tile * LANES : (tile + 1) * LANES] for tile in range(RADIX)]
        rows = pl.ds(pl.multiple_of(first * ROWS, 2 * ROWS), 2 * ROWS)
        for m1, value in enumerate(dft8(parts, sign)):
            value = value.reshape(2 * ROWS, LANES)
            high = value.astype(jnp.bfloat16)
            split_ref[m1, rows, :LANES] = high
            split_ref[m1, rows, LANES : 2 * LANES] = (value - high.astype(jnp.float32)).astype(jnp.bfloat16)
            split_ref[m1, rows, 2 * LANES :] = high
        return carry

    lax.fori_loop(0, FRAMES // 2, butterflies, 0)
    for m1 in range(RADIX):
        high = high_ref[m1]
        product = jnp.dot(
            split_ref[m1], jnp.concatenate([high, high, low_ref[m1]], axis=0), preferred_element_type=jnp.float32
        )
        cosines = product[:, :LANES].reshape(FRAMES, ROWS, LANES)
        sines = product[:, LANES:].reshape(FRAMES, ROWS, LANES)
        result = (cosines + turn(sines, sign)).astype(jnp.bfloat16)
        out_ref[: FRAMES // HOPS_DEV, :, 0, :, m1 * LANES : (m1 + 1) * LANES] = result.reshape(
            FRAMES // HOPS_DEV, HOPS_DEV, ROWS, LANES
        )


def early_kernel(x_ref, *refs):
    def load(lanes):
        return x_ref[:, 0, :, :, lanes].astype(jnp.float32).reshape(HOPS, ROWS, LANES)

    transform(load, *refs)


def late_kernel(block_ref, count_ref, place_ref, a0, a1, a2, a3, proto_ref, high_ref, low_ref, out_ref, wide_ref, fir_ref, split_ref, held_ref, sem):
    pair = pl.program_id(0)

    @pl.when(pair == 0)
    def _():
        for slot in range(MAXREQ):
            shift, _ = arrival(slot, block_ref, count_ref, place_ref)
            for own, ref in enumerate((a0.at[:, 0], a1, a2, a3)):

                @pl.when(shift == own)
                def _():
                    pltpu.make_async_copy(ref, held_ref.at[slot], sem.at[slot]).start()

    for slot in range(2):
        at = pair * 2 + slot
        pltpu.make_async_copy(a1, held_ref.at[at], sem.at[at]).wait()

    ranks = [arrival(slot, block_ref, count_ref, place_ref)[1] for slot in range(MAXREQ)]
    first_rank = jnp.where(pair == 0, ranks[0], ranks[2])
    second_rank = jnp.where(pair == 0, ranks[1], ranks[3])
    is_second = (lax.broadcasted_iota(jnp.int32, (HOPS, ROWS, LANES), 1) // SHARE) % 2 == 1

    def load(lanes):
        first = held_ref[pair * 2, :, :, :, lanes].astype(jnp.float32).reshape(HOPS, ROWS, LANES)
        second = held_ref[pair * 2 + 1, :, :, :, lanes].astype(jnp.float32).reshape(HOPS, ROWS, LANES)
        first = jnp.where(first_rank == 0, first, pltpu.roll(first, ROWS - SHARE, 1))
        second = jnp.where(second_rank == 1, second, pltpu.roll(second, SHARE, 1))
        return jnp.where(is_second, second, first)

    transform(load, proto_ref, high_ref, low_ref, out_ref, wide_ref, fir_ref, split_ref)


def table_specs():
    return [
        pl.BlockSpec((TAPS, NFINE), lambda p, *refs: (0, 0)),
        pl.BlockSpec((RADIX, LANES, 2 * LANES), lambda p, *refs: (0, 0, 0)),
        pl.BlockSpec((RADIX, LANES, 2 * LANES), lambda p, *refs: (0, 0, 0)),
    ]


COST = pl.CostEstimate(flops=18_000_000_000, transcendentals=0, bytes_accessed=2 * MAXREQ * HOPS * 4 * NFINE * 2)
RESULT = jax.ShapeDtypeStruct((TM, HOPS_DEV, MAXREQ // 2, ROWS, NFINE), jnp.bfloat16)


def result_spec():
    return pl.BlockSpec((TM, HOPS_DEV, 1, ROWS, NFINE), lambda p, *refs: (0, 0, p, 0, 0))


def work_space():
    return [
        pltpu.VMEM((FRAMES + TAPS - 1, ROWS, LANES), jnp.float32),
        pltpu.VMEM((FRAMES, ROWS, NFINE), jnp.float32),
        pltpu.VMEM((RADIX, FRAMES * ROWS, 3 * LANES), jnp.bfloat16),
    ]


def filter_early(gathered, tables):
    return pl.pallas_call(
        early_kernel,
        out_shape=RESULT,
        grid=(MAXREQ // 2,),
        in_specs=[
            pl.BlockSpec((TM, 1, HOPS_DEV, ROWS, NFINE), lambda p: (0, p, 0, 0, 0)),
            *table_specs(),
        ],
        out_specs=result_spec(),
        scratch_shapes=work_space(),
        cost_estimate=COST,
        name="filter_early",
    )(gathered, *tables)


def filter_late(arrived, tables, req_block, req_count, place):
    return pl.pallas_call(
        late_kernel,
        out_shape=RESULT,
        grid_spec=pltpu.PrefetchScalarGridSpec(
            num_scalar_prefetch=3,
            grid=(MAXREQ // 2,),
            in_specs=[pl.BlockSpec(memory_space=pl.ANY)] * OWNERS + table_specs(),
            out_specs=result_spec(),
            scratch_shapes=work_space()
            + [
                pltpu.VMEM((MAXREQ, TM, HOPS_DEV, ROWS, NFINE), jnp.bfloat16),
                pltpu.SemaphoreType.DMA((MAXREQ,)),
            ],
        ),
        cost_estimate=COST,
        name="filter_late",
    )(req_block, req_count, place, *arrived, *tables)


def final_pick(slot):
    shape = (2 * TM * ROWS, 2 * BLOCKW)
    row, column = (lax.broadcasted_iota(jnp.int32, shape, dim) for dim in range(2))
    place = (row // ROWS) * SHARE + row % SHARE + BLOCKW * ((row // 4) % 2)
    return jnp.where((place == column) & ((row // 2) % 2 == slot), 1.0, 0.0).astype(jnp.bfloat16)


def unpack_kernel(start_ref, frames_ref, count_ref, place_ref, early_ref, late_ref, out_ref, back_buf, rows_ref, turned_ref, pick_ref, sem):
    owner = place_ref[0]
    step = pl.program_id(0)

    def is_active(hop, slot):
        frame = place_ref[1] * HOPS_DEV + hop
        begin = start_ref[owner, slot]
        return (slot < count_ref[owner]) & (frame >= begin) & (frame < begin + frames_ref[owner, slot])

    def back_copies(hop, pair):
        at = hop * (MAXREQ // 2) + pair
        return [
            pltpu.make_async_copy(ref.at[:, hop, pair], back_buf.at[at, half], sem.at[at, half])
            for half, ref in enumerate((early_ref, late_ref))
        ]

    @pl.when(step == 0)
    def _():
        for hop in range(HOPS_DEV):
            for pair in range(MAXREQ // 2):

                @pl.when(is_active(hop, 2 * pair) | is_active(hop, 2 * pair + 1))
                def _():
                    for copy in back_copies(hop, pair):
                        copy.start()

        for which in range(2):
            pick_ref[which] = final_pick(which)

    hop, pair = step // (MAXREQ // 2), step % (MAXREQ // 2)
    active = [is_active(hop, 2 * pair + which) for which in range(2)]

    @pl.when(active[0] | active[1])
    def _():
        for copy in back_copies(hop, pair):
            copy.wait()
        rows_ref[...] = back_buf[step].astype(jnp.float32).reshape(2 * TM * ROWS, NFINE).astype(jnp.bfloat16)

    for which in range(2):

        @pl.when(active[which])
        def _():
            columns = lax.dot_general(
                rows_ref[...], pick_ref[which], (((0,), (0,)), ((), ())), preferred_element_type=jnp.float32
            )
            for m1 in range(RADIX):
                for part in range(2):
                    turned_ref[part, pl.ds(m1, LANES, stride=RADIX), :] = columns[
                        m1 * LANES : (m1 + 1) * LANES, part * BLOCKW : (part + 1) * BLOCKW
                    ]
            out_ref[0, 0, which] = turned_ref[...].astype(jnp.bfloat16)

        @pl.when(jnp.logical_not(active[which]))
        def _():
            out_ref[0, 0, which] = jnp.zeros((2, NFINE, BLOCKW), jnp.bfloat16)


def unpack(early, late, req_start, req_frames, req_count, place):
    anywhere = pl.BlockSpec(memory_space=pl.ANY)
    steps = HOPS_DEV * MAXREQ // 2
    return pl.pallas_call(
        unpack_kernel,
        out_shape=jax.ShapeDtypeStruct((HOPS_DEV, 1, MAXREQ, 2, NFINE, BLOCKW), jnp.bfloat16),
        grid_spec=pltpu.PrefetchScalarGridSpec(
            num_scalar_prefetch=4,
            grid=(steps,),
            in_specs=[anywhere, anywhere],
            out_specs=pl.BlockSpec(
                (1, 1, 2, 2, NFINE, BLOCKW),
                lambda i, *refs: (i // (MAXREQ // 2), 0, i % (MAXREQ // 2), 0, 0, 0),
            ),
            scratch_shapes=[
                pltpu.VMEM((steps, 2, TM, ROWS, NFINE), jnp.bfloat16),
                pltpu.VMEM((2 * TM * ROWS, NFINE), jnp.bfloat16),
                pltpu.VMEM((2, NFINE, BLOCKW), jnp.float32),
                pltpu.VMEM((2, 2 * TM * ROWS, 2 * BLOCKW), jnp.bfloat16),
                pltpu.SemaphoreType.DMA((steps, 2)),
            ],
        ),
        name="unpack",
    )(req_start, req_frames, req_count, place, early, late)


def over_tm(array):
    return lax.all_to_all(array, "tm", split_axis=0, concat_axis=0, tiled=True)


def along_chan(arrays):
    return [arrays[0]] + [
        lax.ppermute(arrays[d], "chan", [(s, (s + d) % OWNERS) for s in range(OWNERS)])
        for d in range(1, OWNERS)
    ]


def shards(coarse, prototype, req_block, req_start, req_frames, req_count):
    column = lax.axis_index("chan").astype(jnp.int32)
    place = jnp.stack([column, lax.axis_index("tm").astype(jnp.int32)])
    tables = (prototype, *(jnp.asarray(table) for table in dft_tables()))
    late, *early = pack(coarse, jnp.asarray(late_pick()), req_block, req_count, place)
    late = over_tm(late)
    early = choose(along_chan(early), jnp.asarray(early_pick()), req_block, req_count, place)
    late, early = lax.optimization_barrier((late, early))
    early = over_tm(early)
    late = along_chan([late] + [late[:, d] for d in range(1, OWNERS)])
    early = filter_early(early, tables)
    _, *late = lax.optimization_barrier((early, *late))
    early, late = lax.optimization_barrier((over_tm(early), filter_late(late, tables, req_block, req_count, place)))
    late = over_tm(late)
    return unpack(early, late, req_start, req_frames, req_count, place)


def solution(mesh):
    return jax.shard_map(
        shards,
        mesh=mesh,
        in_specs=(P(None, "tm", "chan"), P(), P(), P(), P(), P()),
        out_specs=P("tm", "chan", None, None, None, None),
        check_vma=False,
    )
```

time: 286 us -> 264 us (0.923)
  Pallas kernels: 78.4 us -> 52.4 us
    pallas_call x2 -> x1, Pallas kernels: 24.3 us -> 8.8 us  [pack(): pl.pallas_call(pack_kernel, out_shape=[jax.ShapeDtypeStruct((TM, OWNERS,...]
    pallas_call x1, Pallas kernels: 12.7 us -> 4.81 us  [unpack(): pl.pallas_call(unpack_kernel, out_shape=jax.ShapeDtypeStruct((HOPS_DEV, 1...]
  transfers between devices with their start and end apart: 9 -> 9, of which waited for: 6 -> 6; matrix products, arithmetic and copies ran while one was open for 2% -> 2% of each run, Pallas kernels for 18% -> 15%
where the time goes in v4:
time: 264 us; the launch traced here: 260 us
  waiting for transfers between devices  126 us (48%)
  Pallas kernels  52.4 us (20%)
  blocking collectives  44.6 us (17%)
  starting transfers between devices  29.5 us (11%)
  local copies, waits for them, and re-layouts  7.44 us (3%)
    ppermute x6, waiting for transfers between devices, along_chan(): lax.ppermute(arrays[d], 'chan', [(s, (s + d) % OWNERS) for s in range(OWN...  82.5 us
    all_to_all x1, blocking collectives, over_tm(): return lax.all_to_all(array, 'tm', split_axis=0, concat_axis=0, tiled=True)  44.6 us
    all_to_all x3, waiting for transfers between devices, over_tm(): return lax.all_to_all(array, 'tm', split_axis=0, concat_axis=0, tiled=True)  43.1 us
    all_to_all x3, starting transfers between devices, over_tm(): return lax.all_to_all(array, 'tm', split_axis=0, concat_axis=0, tiled=True)  20.1 us
    pallas_call x1, Pallas kernels, filter_late(): pl.pallas_call(late_kernel, out_shape=RESULT, grid_spec=pltpu.PrefetchSca...  18.3 us
    pallas_call x1, Pallas kernels, filter_early(): pl.pallas_call(early_kernel, out_shape=RESULT, grid=(MAXREQ // 2,), in_sp...  15.3 us
    ppermute x6, starting transfers between devices, along_chan(): lax.ppermute(arrays[d], 'chan', [(s, (s + d) % OWNERS) for s in range(OWN...  9.45 us
    pallas_call x1, Pallas kernels, pack(): pl.pallas_call(pack_kernel, out_shape=[jax.ShapeDtypeStruct((TM, OWNERS,...  8.8 us
  transfers between devices with their start and end apart: 9, of which 6 were waited for; matrix products, arithmetic and copies ran while one was open for 2% of the time, Pallas kernels for 15%

profile of v4, /device:TPU:0, one launch (start us, length us, event | category | flops | bytes accessed | tf_op | source)
XLA Modules:
  0.0 260.3 jit_solution(14111346440684411465)
XLA Ops:
  0.0 0.6 pad_add_fusion.place_ref
  0.6 8.8 %pack.1 = (bf16[32,4,3,8,1024]{4,3,2,1,0:T(8,128)(2,1)}, bf16[2,3,1024,128]{3,2,1,0:T(8,128)(2,1)}, bf16[2,3,1024,128]{3,2,1,0:T(8,128)(2,1)}, bf16[2,3,1024,128...) custom-call(s32[4,4]{1,0:T(4,128)} %block_ref.5, s32[4]{0:T(128)} %count_ref.7, s32[2]{0:T(128)} %pad_add_fusion.place_ref, ...), custom_call_target="tpu_custom_call" | custom-call | tf_op jit(solution)/shard_map/pack/pallas_call | solution.py:127
  9.4 8.6 %all-to-all-start = ((bf16[32,4,3,8,1024]{4,3,2,1,0:T(8,128)(2,1)}), bf16[32,4,3,8,1024]{4,3,2,1,0:T(8,128)(2,1)}, u32[]{:S(2)}, u32[]{:S(2)}) async-start(bf16[32,4,3,8,1024]{4,3,2,1,0:T(8,128)(2,1)} %get-tuple-element.18), calls=%async_computation | async-start | bytes 12582912 | tf_op jit(solution)/shard_map/all_to_all | solution.py:464
  17.9 0.1 collective-permute-start
  18.0 6.1 %collective-permute-start.1 = (bf16[2,3,1024,128]{3,2,1,0:T(8,128)(2,1)}, bf16[2,3,1024,128]{3,2,1,0:T(8,128)(2,1)S(1)}, u32[]{:S(2)}, u32[]{:S(2)}) collective-permute-start(bf16[2,3,1024,128]{3,2,1,0:T(8,128)(2,1)} %get-tuple-element.21), channel_id=1, source_target_pairs={{0,2},{1,3},{2,0},{3,1},{4,6},{5,7},{6,4},{7,5},{8,10},{9,11},{10,... | collective-permute-start | bytes 4718600 | tf_op jit(solution)/shard_map/ppermute | solution.py:469
  24.2 0.0 collective-permute-start.2
  24.2 33.5 %collective-permute-done.a1 = bf16[2,3,1024,128]{3,2,1,0:T(8,128)(2,1)S(1)} collective-permute-done((bf16[2,3,1024,128]{3,2,1,0:T(8,128)(2,1)}, bf16[2,3,1024,128]{3,2,1,0:T(8,128)(2,1)S(1)}, u32[]{:S(2)}, u32[]{:S(2)}) %collective-permute-start) | collective-permute-done | bytes 1572896 | tf_op jit(solution)/shard_map/ppermute | solution.py:469
  57.7 0.0 copy-start.2
  57.7 34.9 %collective-permute-done.1.a2 = bf16[2,3,1024,128]{3,2,1,0:T(8,128)(2,1)S(1)} collective-permute-done((bf16[2,3,1024,128]{3,2,1,0:T(8,128)(2,1)}, bf16[2,3,1024,128]{3,2,1,0:T(8,128)(2,1)S(1)}, u32[]{:S(2)}, u32[]{:S(2)}) %collective-permute-start.1) | collective-permute-done | bytes 1572896 | tf_op jit(solution)/shard_map/ppermute | solution.py:469
  92.6 0.0 copy-start.3
  92.6 0.0 collective-permute-done.2.a3
  92.6 0.0 copy-done.2
  92.6 1.1 copy-done.3
  93.7 5.2 %choose.1 = bf16[32,2,3,8,1024]{4,3,2,1,0:T(8,128)(2,1)} custom-call(s32[4,4]{1,0:T(4,128)} %block_ref.5, s32[4]{0:T(128)} %count_ref.7, s32[2]{0:T(128)} %pad_add_fusion.place_ref, bf16[2,3,1024,128]{3,2,1,0:T(8,128)(2,1)} %get-tuple-element.19.a0, bf16[2,3,1024,128]{3,2,1,0:T(8,128)(2,1)} %copy-done.2, bf16[2,3,1024,128]{3,2,1,0:T(8,128)(2,1)} %copy-done.3, ...), custom_call_target="tpu_custom_call" | custom-call | tf_op jit(solution)/shard_map/choose/pallas_call | solution.py:188
  98.9 0.0 all-to-all-done.a0
  98.9 7.3 %all-to-all-start.1 = ((bf16[32,2,3,8,1024]{4,3,2,1,0:T(8,128)(2,1)}), bf16[32,2,3,8,1024]{4,3,2,1,0:T(8,128)(2,1)S(1)}, u32[]{:S(2)}, u32[]{:S(2)}) async-start(bf16[32,2,3,8,1024]{4,3,2,1,0:T(8,128)(2,1)} %choose.1), calls=%async_computation.1 | async-start | bytes 6291456 | tf_op jit(solution)/shard_map/all_to_all | solution.py:464
  106.2 4.6 %slice_bitcast_fusion = (bf16[32,3,8,1024]{3,2,1,0:T(8,128)(2,1)}, bf16[32,3,8,1024]{3,2,1,0:T(8,128)(2,1)}, bf16[32,3,8,1024]{3,2,1,0:T(8,128)(2,1)}) fusion(bf16[32,4,3,8,1024]{4,3,2,1,0:T(8,128)(2,1)} %all-to-all-done.a0), kind=kLoop, calls=%fused_computation | loop fusion | bytes 9437184 | tf_op jit(solution)/shard_map/squeeze | solution.py:483
  110.8 0.0 collective-permute-start.3
  110.8 2.6 collective-permute-start.4
  113.4 0.7 collective-permute-start.5
  114.0 33.9 %all-to-all-done.1.x_ref = bf16[32,2,3,8,1024]{4,3,2,1,0:T(8,128)(2,1)S(1)} async-done(((bf16[32,2,3,8,1024]{4,3,2,1,0:T(8,128)(2,1)}), bf16[32,2,3,8,1024]{4,3,2,1,0:T(8,128)(2,1)S(1)}, u32[]{:S(2)}, u32[]{:S(2)}) %all-to-all-start.1) | async-done | bytes 3145760 | tf_op jit(solution)/shard_map/all_to_all | solution.py:464
  148.0 1.7 copy-done.1
  149.6 15.3 %filter_early.1 = bf16[32,3,2,8,1024]{4,3,2,1,0:T(8,128)(2,1)} custom-call(bf16[32,2,3,8,1024]{4,3,2,1,0:T(8,128)(2,1)} %copy-done.1, f32[16,1024]{1,0:T(8,128)} %proto_ref.1, bf16[8,128,256]{2,1,0:T(8,128)(2,1)} %constant.17.clone.refs_1_.high_ref, bf16[8,128,256]{2,1,0:T(8,128)(2,1)} %constant.18.clone.refs_2_.low_ref), custom_call_target="tpu_custom_call" | custom-call | flops 17999998976 | bytes 6291456 | tf_op jit(solution)/shard_map/filter_early/pallas_call | solution.py:338
  164.9 4.2 %all-to-all-start.2 = ((bf16[32,3,2,8,1024]{4,3,2,1,0:T(8,128)(2,1)}), bf16[32,3,2,8,1024]{4,3,2,1,0:T(8,128)(2,1)S(1)}, u32[]{:S(2)}, u32[]{:S(2)}) async-start(bf16[32,3,2,8,1024]{4,3,2,1,0:T(8,128)(2,1)} %filter_early.1), calls=%async_computation.2 | async-start | bytes 6291456 | tf_op jit(solution)/shard_map/all_to_all | solution.py:464
  169.2 13.5 %collective-permute-done.3.a1 = bf16[32,3,8,1024]{3,2,1,0:T(8,128)(2,1)} collective-permute-done((bf16[32,3,8,1024]{3,2,1,0:T(8,128)(2,1)}, bf16[32,3,8,1024]{3,2,1,0:T(8,128)(2,1)}, u32[]{:S(2)}, u32[]{:S(2)}) %collective-permute-start.3) | collective-permute-done | bytes 1572896 | tf_op jit(solution)/shard_map/ppermute | solution.py:469
  182.6 0.0 collective-permute-done.4.a2
  182.6 0.6 collective-permute-done.5.a3
  183.2 18.3 %filter_late.1 = bf16[32,3,2,8,1024]{4,3,2,1,0:T(8,128)(2,1)} custom-call(s32[4,4]{1,0:T(4,128)} %block_ref.5, s32[4]{0:T(128)} %count_ref.7, s32[2]{0:T(128)} %pad_add_fusion.place_ref, bf16[32,4,3,8,1024]{4,3,2,1,0:T(8,128)(2,1)} %all-to-all-done.a0, bf16[32,3,8,1024]{3,2,1,0:T(8,128)(2,1)} %collective-permute-done.3.a1, ...), custom_call_target="tpu_custom_call" | custom-call | flops 17999998976 | bytes 6291456 | tf_op jit(solution)/shard_map/filter_late/pallas_call | solution.py:354
  201.6 9.2 %all-to-all-done.2.early_ref = bf16[32,3,2,8,1024]{4,3,2,1,0:T(8,128)(2,1)S(1)} async-done(((bf16[32,3,2,8,1024]{4,3,2,1,0:T(8,128)(2,1)}), bf16[32,3,2,8,1024]{4,3,2,1,0:T(8,128)(2,1)S(1)}, u32[]{:S(2)}, u32[]{:S(2)}) %all-to-all-start.2) | async-done | bytes 3145760 | tf_op jit(solution)/shard_map/all_to_all | solution.py:464
  210.7 44.6 %all_to_all.20.late_ref = bf16[32,3,2,8,1024]{4,3,2,1,0:T(8,128)(2,1)} all-to-all(bf16[32,3,2,8,1024]{4,3,2,1,0:T(8,128)(2,1)} %filter_late.1), channel_id=1, replica_groups=mesh['tm'=32,'chan'=4] {'tm'}, dimensions={0} | all-to-all | bytes 6291456 | tf_op jit(solution)/shard_map/all_to_all | solution.py:464
  255.4 0.0 copy-done
  255.4 4.8 %unpack.1 = bf16[3,1,4,2,1024,128]{5,4,3,2,1,0:T(8,128)(2,1)} custom-call(s32[4,4]{1,0:T(4,128)} %start_ref.1, s32[4,4]{1,0:T(4,128)} %frames_ref.1, s32[4]{0:T(128)} %count_ref.7, s32[2]{0:T(128)} %pad_add_fusion.place_ref, bf16[32,3,2,8,1024]{4,3,2,1,0:T(8,128)(2,1)} %copy-done, bf16[32,3,2,8,1024]{4,3,2,1,0:T(8,128)(2,1)} %all_to_all.20.late_ref), custom_call_target="tpu_custom_call" | custom-call | tf_op jit(solution)/shard_map/unpack/pallas_call | solution.py:440
  (2 shorter events, 0.0 us)
Async XLA Ops:
  9.4 89.5 %all-to-all-start = ((bf16[32,4,3,8,1024]{4,3,2,1,0:T(8,128)(2,1)}), bf16[32,4,3,8,1024]{4,3,2,1,0:T(8,128)(2,1)}, u32[]{:S(2)}, u32[]{:S(2)}) async-start(bf16[32,4,3,8,1024]{4,3,2,1,0:T(8,128)(2,1)} %get-tuple-element.18), calls=%async_computation | async-start | bytes 12582912 | tf_op jit(solution)/shard_map/all_to_all | solution.py:464
  17.9 39.7 %collective-permute-start = (bf16[2,3,1024,128]{3,2,1,0:T(8,128)(2,1)}, bf16[2,3,1024,128]{3,2,1,0:T(8,128)(2,1)S(1)}, u32[]{:S(2)}, u32[]{:S(2)}) collective-permute-start(bf16[2,3,1024,128]{3,2,1,0:T(8,128)(2,1)} %get-tuple-element.20), channel_id=1, source_target_pairs={{0,1},{1,2},{2,3},{3,0},{4,5},{5,6},{6,7},{7,4},{8,9},{9,10},{10,1... | collective-permute-start | bytes 4718600 | tf_op jit(solution)/shard_map/ppermute | solution.py:469
  18.0 74.5 %collective-permute-start.1 = (bf16[2,3,1024,128]{3,2,1,0:T(8,128)(2,1)}, bf16[2,3,1024,128]{3,2,1,0:T(8,128)(2,1)S(1)}, u32[]{:S(2)}, u32[]{:S(2)}) collective-permute-start(bf16[2,3,1024,128]{3,2,1,0:T(8,128)(2,1)} %get-tuple-element.21), channel_id=1, source_target_pairs={{0,2},{1,3},{2,0},{3,1},{4,6},{5,7},{6,4},{7,5},{8,10},{9,11},{10,... | collective-permute-start | bytes 4718600 | tf_op jit(solution)/shard_map/ppermute | solution.py:469
  24.2 68.4 %collective-permute-start.2 = (bf16[2,3,1024,128]{3,2,1,0:T(8,128)(2,1)}, bf16[2,3,1024,128]{3,2,1,0:T(8,128)(2,1)}, u32[]{:S(2)}, u32[]{:S(2)}) collective-permute-start(bf16[2,3,1024,128]{3,2,1,0:T(8,128)(2,1)} %get-tuple-element.22), channel_id=1, source_target_pairs={{0,3},{1,0},{2,1},{3,2},{4,7},{5,4},{6,5},{7,6},{8,11},{9,8},{10,9... | collective-permute-start | bytes 4718600 | tf_op jit(solution)/shard_map/ppermute | solution.py:469
  57.7 34.9 %copy-start.2 = (bf16[2,3,1024,128]{3,2,1,0:T(8,128)(2,1)}, bf16[2,3,1024,128]{3,2,1,0:T(8,128)(2,1)S(1)}, u32[]{:S(2)}) copy-start(bf16[2,3,1024,128]{3,2,1,0:T(8,128)(2,1)S(1)} %collective-permute-done.a1) | copy-start | bytes 4718596
  92.6 1.2 copy-start.3
  98.9 49.0 %all-to-all-start.1 = ((bf16[32,2,3,8,1024]{4,3,2,1,0:T(8,128)(2,1)}), bf16[32,2,3,8,1024]{4,3,2,1,0:T(8,128)(2,1)S(1)}, u32[]{:S(2)}, u32[]{:S(2)}) async-start(bf16[32,2,3,8,1024]{4,3,2,1,0:T(8,128)(2,1)} %choose.1), calls=%async_computation.1 | async-start | bytes 6291456 | tf_op jit(solution)/shard_map/all_to_all | solution.py:464
  110.8 71.8 %collective-permute-start.3 = (bf16[32,3,8,1024]{3,2,1,0:T(8,128)(2,1)}, bf16[32,3,8,1024]{3,2,1,0:T(8,128)(2,1)}, u32[]{:S(2)}, u32[]{:S(2)}) collective-permute-start(bf16[32,3,8,1024]{3,2,1,0:T(8,128)(2,1)} %get-tuple-element.33), channel_id=1, source_target_pairs={{0,1},{1,2},{2,3},{3,0},{4,5},{5,6},{6,7},{7,4},{8,9},{9,10},{10,1... | collective-permute-start | bytes 4718600 | tf_op jit(solution)/shard_map/ppermute | solution.py:469
  110.8 71.8 %collective-permute-start.4 = (bf16[32,3,8,1024]{3,2,1,0:T(8,128)(2,1)}, bf16[32,3,8,1024]{3,2,1,0:T(8,128)(2,1)}, u32[]{:S(2)}, u32[]{:S(2)}) collective-permute-start(bf16[32,3,8,1024]{3,2,1,0:T(8,128)(2,1)} %get-tuple-element.32), channel_id=1, source_target_pairs={{0,2},{1,3},{2,0},{3,1},{4,6},{5,7},{6,4},{7,5},{8,10},{9,11},{10,... | collective-permute-start | bytes 4718600 | tf_op jit(solution)/shard_map/ppermute | solution.py:469
  113.4 69.8 %collective-permute-start.5 = (bf16[32,3,8,1024]{3,2,1,0:T(8,128)(2,1)}, bf16[32,3,8,1024]{3,2,1,0:T(8,128)(2,1)}, u32[]{:S(2)}, u32[]{:S(2)}) collective-permute-start(bf16[32,3,8,1024]{3,2,1,0:T(8,128)(2,1)} %get-tuple-element.31), channel_id=1, source_target_pairs={{0,3},{1,0},{2,1},{3,2},{4,7},{5,4},{6,5},{7,6},{8,11},{9,8},{10,9... | collective-permute-start | bytes 4718600 | tf_op jit(solution)/shard_map/ppermute | solution.py:469
  148.0 1.7 copy-start.1
  164.9 45.8 %all-to-all-start.2 = ((bf16[32,3,2,8,1024]{4,3,2,1,0:T(8,128)(2,1)}), bf16[32,3,2,8,1024]{4,3,2,1,0:T(8,128)(2,1)S(1)}, u32[]{:S(2)}, u32[]{:S(2)}) async-start(bf16[32,3,2,8,1024]{4,3,2,1,0:T(8,128)(2,1)} %filter_early.1), calls=%async_computation.2 | async-start | bytes 6291456 | tf_op jit(solution)/shard_map/all_to_all | solution.py:464
  210.7 44.6 %copy-start = (bf16[32,3,2,8,1024]{4,3,2,1,0:T(8,128)(2,1)}, bf16[32,3,2,8,1024]{4,3,2,1,0:T(8,128)(2,1)S(1)}, u32[]{:S(2)}) copy-start(bf16[32,3,2,8,1024]{4,3,2,1,0:T(8,128)(2,1)S(1)} %all-to-all-done.2.early_ref) | copy-start | bytes 9437188

commit v5 on v4

--- a/solution.py
+++ b/solution.py
@@ -26,6 +26,7 @@
 LANES = 128
 FRAMES = 84
 GROUP = 21
+COST = pl.CostEstimate(flops=18_000_000_000, transcendentals=0, bytes_accessed=2 * MAXREQ * HOPS * 4 * NFINE * 2)
 
 
 def late_pick():
@@ -145,6 +146,10 @@
     )(req_block, req_count, place, coarse, pick)
 
 
+def in_hbm(array):
+    return pltpu.with_memory_space_constraint(array, pltpu.HBM)
+
+
 def arrival(slot, block_ref, count_ref, place_ref):
     owner = place_ref[0]
     slot = jnp.where(slot < count_ref[owner], slot, 0)
@@ -200,8 +205,9 @@
                 pltpu.SemaphoreType.DMA((MAXREQ // 2, HOPS_DEV)),
             ],
         ),
+        cost_estimate=pl.CostEstimate(flops=150_000_000_000, transcendentals=0, bytes_accessed=2**22),
         name="choose",
-    )(req_block, req_count, place, *arrived, pick)
+    )(req_block, req_count, place, *map(in_hbm, arrived), pick)
 
 
 def turn(value, sign):
@@ -272,8 +278,10 @@
 
 
 def early_kernel(x_ref, *refs):
+    pair = pl.program_id(0)
+
     def load(lanes):
-        return x_ref[:, 0, :, :, lanes].astype(jnp.float32).reshape(HOPS, ROWS, LANES)
+        return x_ref[:, pair, :, :, lanes].astype(jnp.float32).reshape(HOPS, ROWS, LANES)
 
     transform(load, *refs)
 
@@ -318,7 +326,6 @@
     ]
 
 
-COST = pl.CostEstimate(flops=18_000_000_000, transcendentals=0, bytes_accessed=2 * MAXREQ * HOPS * 4 * NFINE * 2)
 RESULT = jax.ShapeDtypeStruct((TM, HOPS_DEV, MAXREQ // 2, ROWS, NFINE), jnp.bfloat16)
 
 
@@ -340,14 +347,14 @@
         out_shape=RESULT,
         grid=(MAXREQ // 2,),
         in_specs=[
-            pl.BlockSpec((TM, 1, HOPS_DEV, ROWS, NFINE), lambda p: (0, p, 0, 0, 0)),
+            pl.BlockSpec(memory_space=pltpu.VMEM),
             *table_specs(),
         ],
         out_specs=result_spec(),
         scratch_shapes=work_space(),
         cost_estimate=COST,
         name="filter_early",
-    )(gathered, *tables)
+    )(pltpu.with_memory_space_constraint(gathered, pltpu.VMEM), *tables)
 
 
 def filter_late(arrived, tables, req_block, req_count, place):
@@ -367,7 +374,7 @@
         ),
         cost_estimate=COST,
         name="filter_late",
-    )(req_block, req_count, place, *arrived, *tables)
+    )(req_block, req_count, place, *map(in_hbm, arrived), *tables)
 
 
 def final_pick(slot):
@@ -457,7 +464,7 @@
             ],
         ),
         name="unpack",
-    )(req_start, req_frames, req_count, place, early, late)
+    )(req_start, req_frames, req_count, place, in_hbm(early), in_hbm(late))
 
 
 def over_tm(array):
@@ -466,7 +473,7 @@
 
 def along_chan(arrays):
     return [arrays[0]] + [
-        lax.ppermute(arrays[d], "chan", [(s, (s + d) % OWNERS) for s in range(OWNERS)])
+        lax.ppermute(in_hbm(arrays[d]), "chan", [(s, (s + d) % OWNERS) for s in range(OWNERS)])
         for d in range(1, OWNERS)
     ]
 

time: 264 us -> 261 us (0.989)
    all_to_all x3, waiting for transfers between devices: 43.1 us -> 51.2 us  [over_tm(): return lax.all_to_all(array, 'tm', split_axis=0, concat_axis=0, tiled=True)]
    ppermute x6, waiting for transfers between devices: 82.5 us -> 75.7 us  [along_chan(): lax.ppermute(in_hbm(arrays[d]), 'chan', [(s, (s + d) % OWNERS) for s in r...]
    ppermute x6, starting transfers between devices: 9.45 us -> 12.9 us  [along_chan(): lax.ppermute(in_hbm(arrays[d]), 'chan', [(s, (s + d) % OWNERS) for s in r...]
    all_to_all x3, starting transfers between devices: 20.1 us -> 16.8 us  [over_tm(): return lax.all_to_all(array, 'tm', split_axis=0, concat_axis=0, tiled=True)]
  transfers between devices with their start and end apart: 9 -> 9, of which waited for: 6 -> 7; matrix products, arithmetic and copies ran while one was open for 2% -> 2% of each run, Pallas kernels for 15% -> 15%
where the time goes in v5:
time: 261 us; the launch traced here: 258 us
  waiting for transfers between devices  127 us (49%)
  Pallas kernels  50.4 us (19%)
  blocking collectives  44.6 us (17%)
  starting transfers between devices  29.6 us (11%)
  local copies, waits for them, and re-layouts  5.77 us (2%)
    ppermute x6, waiting for transfers between devices, along_chan(): lax.ppermute(in_hbm(arrays[d]), 'chan', [(s, (s + d) % OWNERS) for s in r...  75.7 us
    all_to_all x3, waiting for transfers between devices, over_tm(): return lax.all_to_all(array, 'tm', split_axis=0, concat_axis=0, tiled=True)  51.2 us
    all_to_all x1, blocking collectives, over_tm(): return lax.all_to_all(array, 'tm', split_axis=0, concat_axis=0, tiled=True)  44.6 us
    pallas_call x1, Pallas kernels, filter_late(): pl.pallas_call(late_kernel, out_shape=RESULT, grid_spec=pltpu.PrefetchSca...  18.4 us
    all_to_all x3, starting transfers between devices, over_tm(): return lax.all_to_all(array, 'tm', split_axis=0, concat_axis=0, tiled=True)  16.8 us
    pallas_call x1, Pallas kernels, filter_early(): pl.pallas_call(early_kernel, out_shape=RESULT, grid=(MAXREQ // 2,), in_sp...  14.7 us
    ppermute x6, starting transfers between devices, along_chan(): lax.ppermute(in_hbm(arrays[d]), 'chan', [(s, (s + d) % OWNERS) for s in r...  12.9 us
    pallas_call x1, Pallas kernels, pack(): pl.pallas_call(pack_kernel, out_shape=[jax.ShapeDtypeStruct((TM, OWNERS,...  6.27 us
  transfers between devices with their start and end apart: 9, of which 7 were waited for; matrix products, arithmetic and copies ran while one was open for 2% of the time, Pallas kernels for 15%

profile of v5, /device:TPU:0, one launch (start us, length us, event | category | flops | bytes accessed | tf_op | source)
XLA Modules:
  0.0 258.1 jit_solution(6416708734016266964)
XLA Ops:
  0.0 0.6 pad_add_fusion.place_ref
  0.6 6.3 %pack.1 = (bf16[32,4,3,8,1024]{4,3,2,1,0:T(8,128)(2,1)}, bf16[2,3,1024,128]{3,2,1,0:T(8,128)(2,1)}, bf16[2,3,1024,128]{3,2,1,0:T(8,128)(2,1)}, bf16[2,3,1024,128...) custom-call(s32[4,4]{1,0:T(4,128)} %block_ref.5, s32[4]{0:T(128)} %count_ref.7, s32[2]{0:T(128)} %pad_add_fusion.place_ref, ...), custom_call_target="tpu_custom_call" | custom-call | tf_op jit(solution)/shard_map/pack/pallas_call | solution.py:128
  6.8 2.2 collective-permute-start
  9.0 6.0 %collective-permute-start.1 = (bf16[2,3,1024,128]{3,2,1,0:T(8,128)(2,1)}, bf16[2,3,1024,128]{3,2,1,0:T(8,128)(2,1)S(1)}, u32[]{:S(2)}, u32[]{:S(2)}) collective-permute-start(bf16[2,3,1024,128]{3,2,1,0:T(8,128)(2,1)} %get-tuple-element.21), channel_id=1, source_target_pairs={{0,2},{1,3},{2,0},{3,1},{4,6},{5,7},{6,4},{7,5},{8,10},{9,11},{10,... | collective-permute-start | bytes 4718600 | tf_op jit(solution)/shard_map/ppermute | solution.py:476
  15.0 0.1 collective-permute-start.2
  15.1 8.4 %all-to-all-start = ((bf16[32,4,3,8,1024]{4,3,2,1,0:T(8,128)(2,1)}), bf16[32,4,3,8,1024]{4,3,2,1,0:T(8,128)(2,1)}, u32[]{:S(2)}, u32[]{:S(2)}) async-start(bf16[32,4,3,8,1024]{4,3,2,1,0:T(8,128)(2,1)} %get-tuple-element.18), calls=%async_computation | async-start | bytes 12582912 | tf_op jit(solution)/shard_map/all_to_all | solution.py:471
  23.6 24.6 %collective-permute-done.a1 = bf16[2,3,1024,128]{3,2,1,0:T(8,128)(2,1)S(1)} collective-permute-done((bf16[2,3,1024,128]{3,2,1,0:T(8,128)(2,1)}, bf16[2,3,1024,128]{3,2,1,0:T(8,128)(2,1)S(1)}, u32[]{:S(2)}, u32[]{:S(2)}) %collective-permute-start) | collective-permute-done | bytes 1572896 | tf_op jit(solution)/shard_map/ppermute | solution.py:476
  48.2 0.0 copy-start.1
  48.2 34.9 %collective-permute-done.1.a2 = bf16[2,3,1024,128]{3,2,1,0:T(8,128)(2,1)S(1)} collective-permute-done((bf16[2,3,1024,128]{3,2,1,0:T(8,128)(2,1)}, bf16[2,3,1024,128]{3,2,1,0:T(8,128)(2,1)S(1)}, u32[]{:S(2)}, u32[]{:S(2)}) %collective-permute-start.1) | collective-permute-done | bytes 1572896 | tf_op jit(solution)/shard_map/ppermute | solution.py:476
  83.0 0.0 copy-start.2
  83.0 0.0 collective-permute-done.2.a3
  83.0 0.0 copy-done.1
  83.0 1.1 copy-done.2
  84.2 5.6 %choose.1 = bf16[32,2,3,8,1024]{4,3,2,1,0:T(8,128)(2,1)} custom-call(s32[4,4]{1,0:T(4,128)} %block_ref.5, s32[4]{0:T(128)} %count_ref.7, s32[2]{0:T(128)} %pad_add_fusion.place_ref, bf16[2,3,1024,128]{3,2,1,0:T(8,128)(2,1)} %get-tuple-element.19.a0, bf16[2,3,1024,128]{3,2,1,0:T(8,128)(2,1)} %copy-done.1, bf16[2,3,1024,128]{3,2,1,0:T(8,128)(2,1)} %copy-done.2, ...), custom_call_target="tpu_custom_call" | custom-call | flops 149999992832 | bytes 4194304 | tf_op jit(solution)/shard_map/choose/pallas_call | solution.py:193
  89.8 11.7 %all-to-all-done.a0 = bf16[32,4,3,8,1024]{4,3,2,1,0:T(8,128)(2,1)} async-done(((bf16[32,4,3,8,1024]{4,3,2,1,0:T(8,128)(2,1)}), bf16[32,4,3,8,1024]{4,3,2,1,0:T(8,128)(2,1)}, u32[]{:S(2)}, u32[]{:S(2)}) %all-to-all-start) | async-done | bytes 6291488 | tf_op jit(solution)/shard_map/all_to_all | solution.py:471
  101.4 4.1 %all-to-all-start.1 = ((bf16[32,2,3,8,1024]{4,3,2,1,0:T(8,128)(2,1)}), bf16[32,2,3,8,1024]{4,3,2,1,0:T(8,128)(2,1)S(1)}, u32[]{:S(2)}, u32[]{:S(2)}) async-start(bf16[32,2,3,8,1024]{4,3,2,1,0:T(8,128)(2,1)} %choose.1), calls=%async_computation.1 | async-start | bytes 6291456 | tf_op jit(solution)/shard_map/all_to_all | solution.py:471
  105.5 4.6 %slice_bitcast_fusion = (bf16[32,3,8,1024]{3,2,1,0:T(8,128)(2,1)}, bf16[32,3,8,1024]{3,2,1,0:T(8,128)(2,1)}, bf16[32,3,8,1024]{3,2,1,0:T(8,128)(2,1)}) fusion(bf16[32,4,3,8,1024]{4,3,2,1,0:T(8,128)(2,1)} %all-to-all-done.a0), kind=kLoop, calls=%fused_computation | loop fusion | bytes 9437184 | tf_op jit(solution)/shard_map/squeeze | solution.py:490
  110.1 1.9 collective-permute-start.3
  112.1 0.0 collective-permute-start.4
  112.1 2.7 %collective-permute-start.5 = (bf16[32,3,8,1024]{3,2,1,0:T(8,128)(2,1)}, bf16[32,3,8,1024]{3,2,1,0:T(8,128)(2,1)}, u32[]{:S(2)}, u32[]{:S(2)}) collective-permute-start(bf16[32,3,8,1024]{3,2,1,0:T(8,128)(2,1)} %get-tuple-element.31), channel_id=1, source_target_pairs={{0,3},{1,0},{2,1},{3,2},{4,7},{5,4},{6,5},{7,6},{8,11},{9,8},{10,9... | collective-permute-start | bytes 4718600 | tf_op jit(solution)/shard_map/ppermute | solution.py:476
  114.7 32.5 %all-to-all-done.1.x_ref = bf16[32,2,3,8,1024]{4,3,2,1,0:T(8,128)(2,1)S(1)} async-done(((bf16[32,2,3,8,1024]{4,3,2,1,0:T(8,128)(2,1)}), bf16[32,2,3,8,1024]{4,3,2,1,0:T(8,128)(2,1)S(1)}, u32[]{:S(2)}, u32[]{:S(2)}) %all-to-all-start.1) | async-done | bytes 3145760 | tf_op jit(solution)/shard_map/all_to_all | solution.py:471
  147.3 14.7 %filter_early.1 = bf16[32,3,2,8,1024]{4,3,2,1,0:T(8,128)(2,1)} custom-call(bf16[32,2,3,8,1024]{4,3,2,1,0:T(8,128)(2,1)S(1)} %all-to-all-done.1.x_ref, f32[16,1024]{1,0:T(8,128)} %proto_ref.1, bf16[8,128,256]{2,1,0:T(8,128)(2,1)} %constant.17.clone.refs_1_.high_ref, bf16[8,128,256]{2,1,0:T(8,128)(2,1)} %constant.18.clone.refs_2_.low_ref), custom_call_target="tpu_custom_call" | custom-call | flops 17999998976 | bytes 6291456 | tf_op jit(solution)/shard_map/filter_early/pallas_call | solution.py:345
  162.0 4.2 %all-to-all-start.2 = ((bf16[32,3,2,8,1024]{4,3,2,1,0:T(8,128)(2,1)}), bf16[32,3,2,8,1024]{4,3,2,1,0:T(8,128)(2,1)S(1)}, u32[]{:S(2)}, u32[]{:S(2)}) async-start(bf16[32,3,2,8,1024]{4,3,2,1,0:T(8,128)(2,1)} %filter_early.1), calls=%async_computation.2 | async-start | bytes 6291456 | tf_op jit(solution)/shard_map/all_to_all | solution.py:471
  166.3 15.6 %collective-permute-done.3.a1 = bf16[32,3,8,1024]{3,2,1,0:T(8,128)(2,1)} collective-permute-done((bf16[32,3,8,1024]{3,2,1,0:T(8,128)(2,1)}, bf16[32,3,8,1024]{3,2,1,0:T(8,128)(2,1)}, u32[]{:S(2)}, u32[]{:S(2)}) %collective-permute-start.3) | collective-permute-done | bytes 1572896 | tf_op jit(solution)/shard_map/ppermute | solution.py:476
  181.8 0.0 collective-permute-done.4.a2
  181.8 0.6 collective-permute-done.5.a3
  182.5 18.4 %filter_late.1 = bf16[32,3,2,8,1024]{4,3,2,1,0:T(8,128)(2,1)} custom-call(s32[4,4]{1,0:T(4,128)} %block_ref.5, s32[4]{0:T(128)} %count_ref.7, s32[2]{0:T(128)} %pad_add_fusion.place_ref, bf16[32,4,3,8,1024]{4,3,2,1,0:T(8,128)(2,1)} %all-to-all-done.a0, bf16[32,3,8,1024]{3,2,1,0:T(8,128)(2,1)} %collective-permute-done.3.a1, ...), custom_call_target="tpu_custom_call" | custom-call | flops 17999998976 | bytes 6291456 | tf_op jit(solution)/shard_map/filter_late/pallas_call | solution.py:361
  200.8 7.0 %all-to-all-done.2.early_ref = bf16[32,3,2,8,1024]{4,3,2,1,0:T(8,128)(2,1)S(1)} async-done(((bf16[32,3,2,8,1024]{4,3,2,1,0:T(8,128)(2,1)}), bf16[32,3,2,8,1024]{4,3,2,1,0:T(8,128)(2,1)S(1)}, u32[]{:S(2)}, u32[]{:S(2)}) %all-to-all-start.2) | async-done | bytes 3145760 | tf_op jit(solution)/shard_map/all_to_all | solution.py:471
  207.9 0.0 copy-start
  207.9 44.6 %all_to_all.20.late_ref = bf16[32,3,2,8,1024]{4,3,2,1,0:T(8,128)(2,1)} all-to-all(bf16[32,3,2,8,1024]{4,3,2,1,0:T(8,128)(2,1)} %filter_late.1), channel_id=1, replica_groups=mesh['tm'=32,'chan'=4] {'tm'}, dimensions={0} | all-to-all | bytes 6291456 | tf_op jit(solution)/shard_map/all_to_all | solution.py:471
  252.5 0.0 copy-done
  252.5 5.4 %unpack.1 = bf16[3,1,4,2,1024,128]{5,4,3,2,1,0:T(8,128)(2,1)} custom-call(s32[4,4]{1,0:T(4,128)} %start_ref.1, s32[4,4]{1,0:T(4,128)} %frames_ref.1, s32[4]{0:T(128)} %count_ref.7, s32[2]{0:T(128)} %pad_add_fusion.place_ref, bf16[32,3,2,8,1024]{4,3,2,1,0:T(8,128)(2,1)} %copy-done, bf16[32,3,2,8,1024]{4,3,2,1,0:T(8,128)(2,1)} %all_to_all.20.late_ref), custom_call_target="tpu_custom_call" | custom-call | tf_op jit(solution)/shard_map/unpack/pallas_call | solution.py:447
Async XLA Ops:
  6.8 41.3 %collective-permute-start = (bf16[2,3,1024,128]{3,2,1,0:T(8,128)(2,1)}, bf16[2,3,1024,128]{3,2,1,0:T(8,128)(2,1)S(1)}, u32[]{:S(2)}, u32[]{:S(2)}) collective-permute-start(bf16[2,3,1024,128]{3,2,1,0:T(8,128)(2,1)} %get-tuple-element.20), channel_id=1, source_target_pairs={{0,1},{1,2},{2,3},{3,0},{4,5},{5,6},{6,7},{7,4},{8,9},{9,10},{10,1... | collective-permute-start | bytes 4718600 | tf_op jit(solution)/shard_map/ppermute | solution.py:476
  9.0 74.0 %collective-permute-start.1 = (bf16[2,3,1024,128]{3,2,1,0:T(8,128)(2,1)}, bf16[2,3,1024,128]{3,2,1,0:T(8,128)(2,1)S(1)}, u32[]{:S(2)}, u32[]{:S(2)}) collective-permute-start(bf16[2,3,1024,128]{3,2,1,0:T(8,128)(2,1)} %get-tuple-element.21), channel_id=1, source_target_pairs={{0,2},{1,3},{2,0},{3,1},{4,6},{5,7},{6,4},{7,5},{8,10},{9,11},{10,... | collective-permute-start | bytes 4718600 | tf_op jit(solution)/shard_map/ppermute | solution.py:476
  15.0 68.0 %collective-permute-start.2 = (bf16[2,3,1024,128]{3,2,1,0:T(8,128)(2,1)}, bf16[2,3,1024,128]{3,2,1,0:T(8,128)(2,1)}, u32[]{:S(2)}, u32[]{:S(2)}) collective-permute-start(bf16[2,3,1024,128]{3,2,1,0:T(8,128)(2,1)} %get-tuple-element.22), channel_id=1, source_target_pairs={{0,3},{1,0},{2,1},{3,2},{4,7},{5,4},{6,5},{7,6},{8,11},{9,8},{10,9... | collective-permute-start | bytes 4718600 | tf_op jit(solution)/shard_map/ppermute | solution.py:476
  15.1 86.3 %all-to-all-start = ((bf16[32,4,3,8,1024]{4,3,2,1,0:T(8,128)(2,1)}), bf16[32,4,3,8,1024]{4,3,2,1,0:T(8,128)(2,1)}, u32[]{:S(2)}, u32[]{:S(2)}) async-start(bf16[32,4,3,8,1024]{4,3,2,1,0:T(8,128)(2,1)} %get-tuple-element.18), calls=%async_computation | async-start | bytes 12582912 | tf_op jit(solution)/shard_map/all_to_all | solution.py:471
  48.2 34.9 %copy-start.1 = (bf16[2,3,1024,128]{3,2,1,0:T(8,128)(2,1)}, bf16[2,3,1024,128]{3,2,1,0:T(8,128)(2,1)S(1)}, u32[]{:S(2)}) copy-start(bf16[2,3,1024,128]{3,2,1,0:T(8,128)(2,1)S(1)} %collective-permute-done.a1) | copy-start | bytes 4718596
  83.0 1.1 copy-start.2
  101.4 45.8 %all-to-all-start.1 = ((bf16[32,2,3,8,1024]{4,3,2,1,0:T(8,128)(2,1)}), bf16[32,2,3,8,1024]{4,3,2,1,0:T(8,128)(2,1)S(1)}, u32[]{:S(2)}, u32[]{:S(2)}) async-start(bf16[32,2,3,8,1024]{4,3,2,1,0:T(8,128)(2,1)} %choose.1), calls=%async_computation.1 | async-start | bytes 6291456 | tf_op jit(solution)/shard_map/all_to_all | solution.py:471
  110.1 71.7 %collective-permute-start.3 = (bf16[32,3,8,1024]{3,2,1,0:T(8,128)(2,1)}, bf16[32,3,8,1024]{3,2,1,0:T(8,128)(2,1)}, u32[]{:S(2)}, u32[]{:S(2)}) collective-permute-start(bf16[32,3,8,1024]{3,2,1,0:T(8,128)(2,1)} %get-tuple-element.33), channel_id=1, source_target_pairs={{0,1},{1,2},{2,3},{3,0},{4,5},{5,6},{6,7},{7,4},{8,9},{9,10},{10,1... | collective-permute-start | bytes 4718600 | tf_op jit(solution)/shard_map/ppermute | solution.py:476
  112.1 69.8 %collective-permute-start.4 = (bf16[32,3,8,1024]{3,2,1,0:T(8,128)(2,1)}, bf16[32,3,8,1024]{3,2,1,0:T(8,128)(2,1)}, u32[]{:S(2)}, u32[]{:S(2)}) collective-permute-start(bf16[32,3,8,1024]{3,2,1,0:T(8,128)(2,1)} %get-tuple-element.32), channel_id=1, source_target_pairs={{0,2},{1,3},{2,0},{3,1},{4,6},{5,7},{6,4},{7,5},{8,10},{9,11},{10,... | collective-permute-start | bytes 4718600 | tf_op jit(solution)/shard_map/ppermute | solution.py:476
  112.1 70.4 %collective-permute-start.5 = (bf16[32,3,8,1024]{3,2,1,0:T(8,128)(2,1)}, bf16[32,3,8,1024]{3,2,1,0:T(8,128)(2,1)}, u32[]{:S(2)}, u32[]{:S(2)}) collective-permute-start(bf16[32,3,8,1024]{3,2,1,0:T(8,128)(2,1)} %get-tuple-element.31), channel_id=1, source_target_pairs={{0,3},{1,0},{2,1},{3,2},{4,7},{5,4},{6,5},{7,6},{8,11},{9,8},{10,9... | collective-permute-start | bytes 4718600 | tf_op jit(solution)/shard_map/ppermute | solution.py:476
  162.0 45.8 %all-to-all-start.2 = ((bf16[32,3,2,8,1024]{4,3,2,1,0:T(8,128)(2,1)}), bf16[32,3,2,8,1024]{4,3,2,1,0:T(8,128)(2,1)S(1)}, u32[]{:S(2)}, u32[]{:S(2)}) async-start(bf16[32,3,2,8,1024]{4,3,2,1,0:T(8,128)(2,1)} %filter_early.1), calls=%async_computation.2 | async-start | bytes 6291456 | tf_op jit(solution)/shard_map/all_to_all | solution.py:471
  207.9 44.6 %copy-start = (bf16[32,3,2,8,1024]{4,3,2,1,0:T(8,128)(2,1)}, bf16[32,3,2,8,1024]{4,3,2,1,0:T(8,128)(2,1)S(1)}, u32[]{:S(2)}) copy-start(bf16[32,3,2,8,1024]{4,3,2,1,0:T(8,128)(2,1)S(1)} %all-to-all-done.2.early_ref) | copy-start | bytes 9437188

commit v6 on v5

--- a/solution.py
+++ b/solution.py
@@ -25,7 +25,8 @@
 RADIX = 8
 LANES = 128
 FRAMES = 84
-GROUP = 21
+GROUP = 12
+UNROLLED = 42
 COST = pl.CostEstimate(flops=18_000_000_000, transcendentals=0, bytes_accessed=2 * MAXREQ * HOPS * 4 * NFINE * 2)
 
 
@@ -88,10 +89,6 @@
             pl.when(wanted[d][0][0])(lambda d=d: block_copy(d, 0).wait())
             continue
 
-        @pl.when(wanted[d][0][0] & jnp.logical_not(wanted[d][1][0]))
-        def _():
-            block_buf[d, 1] = jnp.zeros((2, HOPS_DEV * NFINE, BLOCKW), jnp.bfloat16)
-
         pl.when(wanted[d][1][0])(lambda d=d: block_copy(d, 1).wait())
         for rank in range(PAIR):
 
@@ -102,19 +99,24 @@
                 ).reshape(HOPS_DEV, NFINE, BLOCKW)
                 early_copy(d, rank).start()
 
-        @pl.when(wanted[d][0][0])
-        def _():
+        def turn_blocks(d, ranks):
             def one_hop(hop, carry):
                 rows = pl.ds(pl.multiple_of(hop * NFINE, NFINE), NFINE)
-                wide = jnp.concatenate([block_buf[d, i // 2, i % 2, rows] for i in range(2 * PAIR)], axis=1)
+                wide = jnp.concatenate([block_buf[d, i // 2, i % 2, rows] for i in range(2 * ranks)], axis=1)
                 turned = lax.dot_general(
-                    pick_ref[...], wide, (((1,), (1,)), ((), ())), preferred_element_type=jnp.float32
+                    pick_ref[:, : 2 * ranks * BLOCKW],
+                    wide,
+                    (((1,), (1,)), ((), ())),
+                    preferred_element_type=jnp.float32,
                 )
                 late_buf[d, :, hop] = turned.reshape(TM, ROWS, NFINE).astype(jnp.bfloat16)
                 return carry
 
             lax.fori_loop(0, HOPS_DEV, one_hop, 0)
             late_copy(d).start()
+
+        pl.when(wanted[d][1][0])(lambda d=d: turn_blocks(d, 2))
+        pl.when(wanted[d][0][0] & jnp.logical_not(wanted[d][1][0]))(lambda d=d: turn_blocks(d, 1))
 
     for d, r in order:
         pl.when(wanted[d][r][0])(lambda d=d, r=r: early_copy(d, r).wait())
@@ -146,6 +148,10 @@
     )(req_block, req_count, place, coarse, pick)
 
 
+def in_vmem(array):
+    return pltpu.with_memory_space_constraint(array, pltpu.VMEM)
+
+
 def in_hbm(array):
     return pltpu.with_memory_space_constraint(array, pltpu.HBM)
 
@@ -230,51 +236,54 @@
     return [pair for both in zip(even, odd) for pair in both]
 
 
-def transform(load, proto_ref, high_ref, low_ref, out_ref, wide_ref, fir_ref, split_ref):
+def transform(load, group_size, proto_ref, high_ref, low_ref, out_ref, wide_ref, fir_ref):
     sign = jnp.where(lax.broadcasted_iota(jnp.int32, (ROWS, LANES), 0) < ROWS // 2, 1.0, -1.0)
-    wide_ref[HOPS:, :, :] = jnp.zeros((FRAMES + TAPS - 1 - HOPS, ROWS, LANES), jnp.float32)
-    def taps(tile, carry):
-        lanes = pl.ds(pl.multiple_of(tile * LANES, LANES), LANES)
-        wide_ref[:HOPS] = load(lanes)
-        weights = [jnp.broadcast_to(proto_ref[tap, lanes].reshape(1, LANES), (ROWS, LANES)) for tap in range(TAPS)]
-
-        def fir(step, inner):
-            first = step * GROUP
-            samples = wide_ref[pl.ds(first, GROUP + TAPS - 1)]
-            total = samples[:GROUP] * weights[0]
-            for tap in range(1, TAPS):
-                total = total + samples[tap : tap + GROUP] * weights[tap]
-            fir_ref[pl.ds(first, GROUP), :, lanes] = total
-            return inner
-
-        return lax.fori_loop(0, FRAMES // GROUP, fir, carry)
-
-    lax.fori_loop(0, RADIX, taps, 0)
-
-    def butterflies(step, carry):
-        first = step * 2
-        parts = [fir_ref[pl.ds(first, 2), :, tile * LANES : (tile + 1) * LANES] for tile in range(RADIX)]
-        rows = pl.ds(pl.multiple_of(first * ROWS, 2 * ROWS), 2 * ROWS)
-        for m1, value in enumerate(dft8(parts, sign)):
-            value = value.reshape(2 * ROWS, LANES)
-            high = value.astype(jnp.bfloat16)
-            split_ref[m1, rows, :LANES] = high
-            split_ref[m1, rows, LANES : 2 * LANES] = (value - high.astype(jnp.float32)).astype(jnp.bfloat16)
-            split_ref[m1, rows, 2 * LANES :] = high
+    wide_ref[:, HOPS:] = jnp.zeros((RADIX, FRAMES + TAPS - 1 - HOPS, ROWS, LANES), jnp.float32)
+
+    def widen(tile, carry):
+        wide_ref[tile, :HOPS] = load(pl.ds(pl.multiple_of(tile * LANES, LANES), LANES))
         return carry
 
-    lax.fori_loop(0, FRAMES // 2, butterflies, 0)
-    for m1 in range(RADIX):
-        high = high_ref[m1]
-        product = jnp.dot(
-            split_ref[m1], jnp.concatenate([high, high, low_ref[m1]], axis=0), preferred_element_type=jnp.float32
-        )
-        cosines = product[:, :LANES].reshape(FRAMES, ROWS, LANES)
-        sines = product[:, LANES:].reshape(FRAMES, ROWS, LANES)
-        result = (cosines + turn(sines, sign)).astype(jnp.bfloat16)
-        out_ref[: FRAMES // HOPS_DEV, :, 0, :, m1 * LANES : (m1 + 1) * LANES] = result.reshape(
-            FRAMES // HOPS_DEV, HOPS_DEV, ROWS, LANES
-        )
+    lax.fori_loop(0, RADIX, widen, 0)
+
+    def one_group(group, carry):
+        first = group * group_size
+        for tile in range(RADIX):
+            lanes = slice(tile * LANES, (tile + 1) * LANES)
+            total = None
+            for tap in range(TAPS):
+                weights = jnp.broadcast_to(proto_ref[tap, lanes].reshape(1, LANES), (ROWS, LANES))
+                part = wide_ref[tile, pl.ds(first + tap, group_size)] * weights
+                total = part if total is None else total + part
+            fir_ref[group, tile] = total
+        for frame in range(0, group_size, 2):
+            parts = [fir_ref[group, tile, frame : frame + 2] for tile in range(RADIX)]
+            for m1, value in enumerate(dft8(parts, sign)):
+                fir_ref[group, m1, frame : frame + 2] = value
+        for m1 in range(RADIX):
+            value = fir_ref[group, m1].reshape(group_size * ROWS, LANES)
+            top = value.astype(jnp.bfloat16)
+            rest = (value - top.astype(jnp.float32)).astype(jnp.bfloat16)
+            high = high_ref[m1]
+            product = jnp.dot(
+                jnp.concatenate([top, rest, top], axis=1),
+                jnp.concatenate([high, high, low_ref[m1]], axis=0),
+                preferred_element_type=jnp.float32,
+            )
+            cosines = product[:, :LANES].reshape(group_size, ROWS, LANES)
+            sines = product[:, LANES:].reshape(group_size, ROWS, LANES)
+            result = (cosines + turn(sines, sign)).astype(jnp.bfloat16)
+            devices = group_size // HOPS_DEV
+            out_ref[pl.ds(group * devices, devices), :, 0, :, m1 * LANES : (m1 + 1) * LANES] = result.reshape(
+                devices, HOPS_DEV, ROWS, LANES
+            )
+        return carry
+
+    if group_size == UNROLLED:
+        for group in range(FRAMES // group_size):
+            one_group(group, 0)
+    else:
+        lax.fori_loop(0, FRAMES // group_size, one_group, 0)
 
 
 def early_kernel(x_ref, *refs):
@@ -283,10 +292,10 @@
     def load(lanes):
         return x_ref[:, pair, :, :, lanes].astype(jnp.float32).reshape(HOPS, ROWS, LANES)
 
-    transform(load, *refs)
-
-
-def late_kernel(block_ref, count_ref, place_ref, a0, a1, a2, a3, proto_ref, high_ref, low_ref, out_ref, wide_ref, fir_ref, split_ref, held_ref, sem):
+    transform(load, UNROLLED, *refs)
+
+
+def late_kernel(block_ref, count_ref, place_ref, a0, a1, a2, a3, proto_ref, high_ref, low_ref, out_ref, wide_ref, fir_ref, held_ref, sem):
     pair = pl.program_id(0)
 
     @pl.when(pair == 0)
@@ -315,7 +324,7 @@
         second = jnp.where(second_rank == 1, second, pltpu.roll(second, SHARE, 1))
         return jnp.where(is_second, second, first)
 
-    transform(load, proto_ref, high_ref, low_ref, out_ref, wide_ref, fir_ref, split_ref)
+    transform(load, GROUP, proto_ref, high_ref, low_ref, out_ref, wide_ref, fir_ref)
 
 
 def table_specs():
@@ -333,11 +342,10 @@
     return pl.BlockSpec((TM, HOPS_DEV, 1, ROWS, NFINE), lambda p, *refs: (0, 0, p, 0, 0))
 
 
-def work_space():
+def work_space(group_size):
     return [
-        pltpu.VMEM((FRAMES + TAPS - 1, ROWS, LANES), jnp.float32),
-        pltpu.VMEM((FRAMES, ROWS, NFINE), jnp.float32),
-        pltpu.VMEM((RADIX, FRAMES * ROWS, 3 * LANES), jnp.bfloat16),
+        pltpu.VMEM((RADIX, FRAMES + TAPS - 1, ROWS, LANES), jnp.float32),
+        pltpu.VMEM((FRAMES // group_size, RADIX, group_size, ROWS, LANES), jnp.float32),
     ]
 
 
@@ -351,10 +359,10 @@
             *table_specs(),
         ],
         out_specs=result_spec(),
-        scratch_shapes=work_space(),
+        scratch_shapes=work_space(UNROLLED),
         cost_estimate=COST,
         name="filter_early",
-    )(pltpu.with_memory_space_constraint(gathered, pltpu.VMEM), *tables)
+    )(in_vmem(gathered), *tables)
 
 
 def filter_late(arrived, tables, req_block, req_count, place):
@@ -366,105 +374,129 @@
             grid=(MAXREQ // 2,),
             in_specs=[pl.BlockSpec(memory_space=pl.ANY)] * OWNERS + table_specs(),
             out_specs=result_spec(),
-            scratch_shapes=work_space()
+            scratch_shapes=work_space(GROUP)
             + [
                 pltpu.VMEM((MAXREQ, TM, HOPS_DEV, ROWS, NFINE), jnp.bfloat16),
                 pltpu.SemaphoreType.DMA((MAXREQ,)),
             ],
         ),
         cost_estimate=COST,
+        compiler_params=pltpu.CompilerParams(vmem_limit_bytes=56 * 2**20),
         name="filter_late",
     )(req_block, req_count, place, *map(in_hbm, arrived), *tables)
 
 
-def final_pick(slot):
-    shape = (2 * TM * ROWS, 2 * BLOCKW)
+def final_pick():
+    shape = (TM * ROWS, 2 * BLOCKW)
     row, column = (lax.broadcasted_iota(jnp.int32, shape, dim) for dim in range(2))
-    place = (row // ROWS) * SHARE + row % SHARE + BLOCKW * ((row // 4) % 2)
-    return jnp.where((place == column) & ((row // 2) % 2 == slot), 1.0, 0.0).astype(jnp.bfloat16)
-
-
-def unpack_kernel(start_ref, frames_ref, count_ref, place_ref, early_ref, late_ref, out_ref, back_buf, rows_ref, turned_ref, pick_ref, sem):
+    place = (row // ROWS) * SHARE + row % SHARE + HALF * ((row // 4) % 2) + BLOCKW * ((row // 2) % 2)
+    return jnp.where(place == column, 1.0, 0.0).astype(jnp.bfloat16)
+
+
+def is_active(hop, slot, start_ref, frames_ref, count_ref, place_ref):
     owner = place_ref[0]
+    frame = place_ref[1] * HOPS_DEV + hop
+    begin = start_ref[owner, slot]
+    return (slot < count_ref[owner]) & (frame >= begin) & (frame < begin + frames_ref[owner, slot])
+
+
+def turn_back(back, pick_ref, turned_ref):
+    rows = back.astype(jnp.float32).reshape(TM * ROWS, NFINE).astype(jnp.bfloat16)
+    columns = lax.dot_general(rows, pick_ref[...], (((0,), (0,)), ((), ())), preferred_element_type=jnp.float32)
+    for m1 in range(RADIX):
+        for slot in range(2):
+            turned_ref[slot, pl.ds(m1, LANES, stride=RADIX), :] = columns[
+                m1 * LANES : (m1 + 1) * LANES, slot * BLOCKW : (slot + 1) * BLOCKW
+            ]
+
+
+def unpack_early_kernel(start_ref, frames_ref, count_ref, place_ref, early_ref, out_ref, turned_ref, pick_ref):
+    refs = start_ref, frames_ref, count_ref, place_ref
     step = pl.program_id(0)
-
-    def is_active(hop, slot):
-        frame = place_ref[1] * HOPS_DEV + hop
-        begin = start_ref[owner, slot]
-        return (slot < count_ref[owner]) & (frame >= begin) & (frame < begin + frames_ref[owner, slot])
-
-    def back_copies(hop, pair):
-        at = hop * (MAXREQ // 2) + pair
-        return [
-            pltpu.make_async_copy(ref.at[:, hop, pair], back_buf.at[at, half], sem.at[at, half])
-            for half, ref in enumerate((early_ref, late_ref))
-        ]
+    hop, pair = step // (MAXREQ // 2), step % (MAXREQ // 2)
 
     @pl.when(step == 0)
     def _():
-        for hop in range(HOPS_DEV):
-            for pair in range(MAXREQ // 2):
-
-                @pl.when(is_active(hop, 2 * pair) | is_active(hop, 2 * pair + 1))
-                def _():
-                    for copy in back_copies(hop, pair):
-                        copy.start()
-
-        for which in range(2):
-            pick_ref[which] = final_pick(which)
-
+        pick_ref[...] = final_pick()
+
+    @pl.when(is_active(hop, 2 * pair, *refs) | is_active(hop, 2 * pair + 1, *refs))
+    def _():
+        turn_back(early_ref[:, 0, 0], pick_ref, turned_ref)
+        out_ref[0] = turned_ref[...].astype(jnp.bfloat16)
+
+
+def unpack_kernel(start_ref, frames_ref, count_ref, place_ref, part_ref, late_ref, out_ref, turned_ref, pick_ref):
+    refs = start_ref, frames_ref, count_ref, place_ref
+    step = pl.program_id(0)
     hop, pair = step // (MAXREQ // 2), step % (MAXREQ // 2)
-    active = [is_active(hop, 2 * pair + which) for which in range(2)]
-
-    @pl.when(active[0] | active[1])
+
+    @pl.when(step == 0)
     def _():
-        for copy in back_copies(hop, pair):
-            copy.wait()
-        rows_ref[...] = back_buf[step].astype(jnp.float32).reshape(2 * TM * ROWS, NFINE).astype(jnp.bfloat16)
+        pick_ref[...] = final_pick()
+
+    @pl.when(is_active(hop, 2 * pair, *refs) | is_active(hop, 2 * pair + 1, *refs))
+    def _():
+        turn_back(late_ref[:, hop, pair], pick_ref, turned_ref)
 
     for which in range(2):
-
-        @pl.when(active[which])
+        active = is_active(hop, 2 * pair + which, *refs)
+
+        @pl.when(active)
         def _():
-            columns = lax.dot_general(
-                rows_ref[...], pick_ref[which], (((0,), (0,)), ((), ())), preferred_element_type=jnp.float32
-            )
-            for m1 in range(RADIX):
-                for part in range(2):
-                    turned_ref[part, pl.ds(m1, LANES, stride=RADIX), :] = columns[
-                        m1 * LANES : (m1 + 1) * LANES, part * BLOCKW : (part + 1) * BLOCKW
-                    ]
-            out_ref[0, 0, which] = turned_ref[...].astype(jnp.bfloat16)
-
-        @pl.when(jnp.logical_not(active[which]))
+            early = part_ref[0, which]
+            late = turned_ref[which].astype(jnp.bfloat16)
+            out_ref[0, 0, which, 0] = jnp.concatenate([early[:, :HALF], late[:, :HALF]], axis=1)
+            out_ref[0, 0, which, 1] = jnp.concatenate([early[:, HALF:], late[:, HALF:]], axis=1)
+
+        @pl.when(jnp.logical_not(active))
         def _():
             out_ref[0, 0, which] = jnp.zeros((2, NFINE, BLOCKW), jnp.bfloat16)
 
 
-def unpack(early, late, req_start, req_frames, req_count, place):
-    anywhere = pl.BlockSpec(memory_space=pl.ANY)
-    steps = HOPS_DEV * MAXREQ // 2
+STEPS = HOPS_DEV * MAXREQ // 2
+
+
+def unpack_early(early, req_start, req_frames, req_count, place):
+    return pl.pallas_call(
+        unpack_early_kernel,
+        out_shape=jax.ShapeDtypeStruct((STEPS, 2, NFINE, BLOCKW), jnp.bfloat16),
+        grid_spec=pltpu.PrefetchScalarGridSpec(
+            num_scalar_prefetch=4,
+            grid=(STEPS,),
+            in_specs=[pl.BlockSpec((TM, 1, 1, ROWS, NFINE), lambda i, *refs: (0, i // (MAXREQ // 2), i % (MAXREQ // 2), 0, 0))],
+            out_specs=pl.BlockSpec((1, 2, NFINE, BLOCKW), lambda i, *refs: (i, 0, 0, 0)),
+            scratch_shapes=[
+                pltpu.VMEM((2, NFINE, BLOCKW), jnp.float32),
+                pltpu.VMEM((TM * ROWS, 2 * BLOCKW), jnp.bfloat16),
+            ],
+        ),
+        cost_estimate=COST,
+        compiler_params=pltpu.CompilerParams(vmem_limit_bytes=52 * 2**20),
+        name="unpack_early",
+    )(req_start, req_frames, req_count, place, in_hbm(early))
+
+
+def unpack(part, late, req_start, req_frames, req_count, place):
+    resident = pl.BlockSpec(memory_space=pltpu.VMEM)
     return pl.pallas_call(
         unpack_kernel,
         out_shape=jax.ShapeDtypeStruct((HOPS_DEV, 1, MAXREQ, 2, NFINE, BLOCKW), jnp.bfloat16),
         grid_spec=pltpu.PrefetchScalarGridSpec(
             num_scalar_prefetch=4,
-            grid=(steps,),
-            in_specs=[anywhere, anywhere],
+            grid=(STEPS,),
+            in_specs=[pl.BlockSpec((1, 2, NFINE, BLOCKW), lambda i, *refs: (i, 0, 0, 0)), resident],
             out_specs=pl.BlockSpec(
                 (1, 1, 2, 2, NFINE, BLOCKW),
                 lambda i, *refs: (i // (MAXREQ // 2), 0, i % (MAXREQ // 2), 0, 0, 0),
             ),
             scratch_shapes=[
-                pltpu.VMEM((steps, 2, TM, ROWS, NFINE), jnp.bfloat16),
-                pltpu.VMEM((2 * TM * ROWS, NFINE), jnp.bfloat16),
                 pltpu.VMEM((2, NFINE, BLOCKW), jnp.float32),
-                pltpu.VMEM((2, 2 * TM * ROWS, 2 * BLOCKW), jnp.bfloat16),
-                pltpu.SemaphoreType.DMA((steps, 2)),
+                pltpu.VMEM((TM * ROWS, 2 * BLOCKW), jnp.bfloat16),
             ],
         ),
+        compiler_params=pltpu.CompilerParams(vmem_limit_bytes=52 * 2**20),
         name="unpack",
-    )(req_start, req_frames, req_count, place, in_hbm(early), in_hbm(late))
+    )(req_start, req_frames, req_count, place, in_hbm(part), in_vmem(late))
 
 
 def over_tm(array):
@@ -490,9 +522,11 @@
     late = along_chan([late] + [late[:, d] for d in range(1, OWNERS)])
     early = filter_early(early, tables)
     _, *late = lax.optimization_barrier((early, *late))
-    early, late = lax.optimization_barrier((over_tm(early), filter_late(late, tables, req_block, req_count, place)))
+    early = over_tm(early)
+    _, late = lax.optimization_barrier((early, filter_late(late, tables, req_block, req_count, place)))
     late = over_tm(late)
-    return unpack(early, late, req_start, req_frames, req_count, place)
+    part = unpack_early(early, req_start, req_frames, req_count, place)
+    return unpack(part, late, req_start, req_frames, req_count, place)
 
 
 def solution(mesh):

time: 261 us -> 261 us (level); the launches traced: 258 us -> 261 us
  blocking collectives: 44.6 us -> 0 us
  waiting for transfers between devices: 127 us -> 165 us
  Pallas kernels: 50.4 us -> 58 us
    all_to_all x1 -> x0, blocking collectives: 44.6 us -> none  [over_tm(): return lax.all_to_all(array, 'tm', split_axis=0, concat_axis=0, tiled=True)]
    all_to_all x3 -> x4, waiting for transfers between devices: 51.2 us -> 88.9 us  [over_tm(): return lax.all_to_all(array, 'tm', split_axis=0, concat_axis=0, tiled=True)]
    pallas_call x0 -> x1, Pallas kernels: none -> 5.9 us  [unpack_early(): pl.pallas_call(unpack_early_kernel, out_shape=jax.ShapeDtypeStruct((STEPS...]
    all_to_all x3 -> x4, starting transfers between devices: 16.8 us -> 20.6 us  [over_tm(): return lax.all_to_all(array, 'tm', split_axis=0, concat_axis=0, tiled=True)]
    ppermute x6, starting transfers between devices: 12.9 us -> 9.89 us  [along_chan(): lax.ppermute(in_hbm(arrays[d]), 'chan', [(s, (s + d) % OWNERS) for s in r...]
  transfers between devices with their start and end apart: 9 -> 10, of which waited for: 7 -> 9; matrix products, arithmetic and copies ran while one was open for 2% -> 2% of each run, Pallas kernels for 15% -> 16%
where the time goes in v6:
time: 261 us
  waiting for transfers between devices  165 us (63%)
  Pallas kernels  58 us (22%)
  starting transfers between devices  30.5 us (12%)
  local copies, waits for them, and re-layouts  6.59 us (3%)
    all_to_all x4, waiting for transfers between devices, over_tm(): return lax.all_to_all(array, 'tm', split_axis=0, concat_axis=0, tiled=True)  88.9 us
    ppermute x6, waiting for transfers between devices, along_chan(): lax.ppermute(in_hbm(arrays[d]), 'chan', [(s, (s + d) % OWNERS) for s in r...  76 us
    all_to_all x4, starting transfers between devices, over_tm(): return lax.all_to_all(array, 'tm', split_axis=0, concat_axis=0, tiled=True)  20.6 us
    pallas_call x1, Pallas kernels, filter_late(): pl.pallas_call(late_kernel, out_shape=RESULT, grid_spec=pltpu.PrefetchSca...  18.8 us
    pallas_call x1, Pallas kernels, filter_early(): pl.pallas_call(early_kernel, out_shape=RESULT, grid=(MAXREQ // 2,), in_sp...  12.4 us
    ppermute x6, starting transfers between devices, along_chan(): lax.ppermute(in_hbm(arrays[d]), 'chan', [(s, (s + d) % OWNERS) for s in r...  9.89 us
    pallas_call x1, Pallas kernels, pack(): pl.pallas_call(pack_kernel, out_shape=[jax.ShapeDtypeStruct((TM, OWNERS,...  8.8 us
    pallas_call x1, Pallas kernels, unpack(): pl.pallas_call(unpack_kernel, out_shape=jax.ShapeDtypeStruct((HOPS_DEV, 1...  6.85 us
  transfers between devices with their start and end apart: 10, of which 9 were waited for; matrix products, arithmetic and copies ran while one was open for 2% of the time, Pallas kernels for 16%

profile of v6, /device:TPU:0, one launch (start us, length us, event | category | flops | bytes accessed | tf_op | source)
XLA Modules:
  0.0 260.7 jit_solution(16422072036109955597)
XLA Ops:
  0.0 0.6 pad_add_fusion.place_ref
  0.6 8.8 %pack.1 = (bf16[32,4,3,8,1024]{4,3,2,1,0:T(8,128)(2,1)}, bf16[2,3,1024,128]{3,2,1,0:T(8,128)(2,1)}, bf16[2,3,1024,128]{3,2,1,0:T(8,128)(2,1)}, bf16[2,3,1024,128...) custom-call(s32[4,4]{1,0:T(4,128)} %block_ref.5, s32[4]{0:T(128)} %count_ref.9, s32[2]{0:T(128)} %pad_add_fusion.place_ref, ...), custom_call_target="tpu_custom_call" | custom-call | tf_op jit(solution)/shard_map/pack/pallas_call | solution.py:130
  9.4 3.7 %collective-permute-start = (bf16[2,3,1024,128]{3,2,1,0:T(8,128)(2,1)}, bf16[2,3,1024,128]{3,2,1,0:T(8,128)(2,1)S(1)}, u32[]{:S(2)}, u32[]{:S(2)}) collective-permute-start(bf16[2,3,1024,128]{3,2,1,0:T(8,128)(2,1)} %get-tuple-element.19), channel_id=1, source_target_pairs={{0,1},{1,2},{2,3},{3,0},{4,5},{5,6},{6,7},{7,4},{8,9},{9,10},{10,1... | collective-permute-start | bytes 4718600 | tf_op jit(solution)/shard_map/ppermute | solution.py:508
  13.2 0.0 collective-permute-start.1
  13.2 2.8 %collective-permute-start.2 = (bf16[2,3,1024,128]{3,2,1,0:T(8,128)(2,1)}, bf16[2,3,1024,128]{3,2,1,0:T(8,128)(2,1)}, u32[]{:S(2)}, u32[]{:S(2)}) collective-permute-start(bf16[2,3,1024,128]{3,2,1,0:T(8,128)(2,1)} %get-tuple-element.21), channel_id=1, source_target_pairs={{0,3},{1,0},{2,1},{3,2},{4,7},{5,4},{6,5},{7,6},{8,11},{9,8},{10,9... | collective-permute-start | bytes 4718600 | tf_op jit(solution)/shard_map/ppermute | solution.py:508
  15.9 8.4 %all-to-all-start = ((bf16[32,4,3,8,1024]{4,3,2,1,0:T(8,128)(2,1)}), bf16[32,4,3,8,1024]{4,3,2,1,0:T(8,128)(2,1)}, u32[]{:S(2)}, u32[]{:S(2)}) async-start(bf16[32,4,3,8,1024]{4,3,2,1,0:T(8,128)(2,1)} %get-tuple-element.17), calls=%async_computation | async-start | bytes 12582912 | tf_op jit(solution)/shard_map/all_to_all | solution.py:503
  24.4 23.9 %collective-permute-done.a1 = bf16[2,3,1024,128]{3,2,1,0:T(8,128)(2,1)S(1)} collective-permute-done((bf16[2,3,1024,128]{3,2,1,0:T(8,128)(2,1)}, bf16[2,3,1024,128]{3,2,1,0:T(8,128)(2,1)S(1)}, u32[]{:S(2)}, u32[]{:S(2)}) %collective-permute-start) | collective-permute-done | bytes 1572896 | tf_op jit(solution)/shard_map/ppermute | solution.py:508
  48.3 32.5 %collective-permute-done.1.a2 = bf16[2,3,1024,128]{3,2,1,0:T(8,128)(2,1)S(1)} collective-permute-done((bf16[2,3,1024,128]{3,2,1,0:T(8,128)(2,1)}, bf16[2,3,1024,128]{3,2,1,0:T(8,128)(2,1)S(1)}, u32[]{:S(2)}, u32[]{:S(2)}) %collective-permute-start.1) | collective-permute-done | bytes 1572896 | tf_op jit(solution)/shard_map/ppermute | solution.py:508
  80.8 0.9 collective-permute-done.2.a3
  81.7 0.3 copy-done.6
  82.0 5.2 %choose.1 = bf16[32,2,3,8,1024]{4,3,2,1,0:T(8,128)(2,1)} custom-call(s32[4,4]{1,0:T(4,128)} %block_ref.5, s32[4]{0:T(128)} %count_ref.9, s32[2]{0:T(128)} %pad_add_fusion.place_ref, bf16[2,3,1024,128]{3,2,1,0:T(8,128)(2,1)} %get-tuple-element.18.a0, bf16[2,3,1024,128]{3,2,1,0:T(8,128)(2,1)} %copy-done.5, bf16[2,3,1024,128]{3,2,1,0:T(8,128)(2,1)} %copy-done.6, ...), custom_call_target="tpu_custom_call" | custom-call | flops 149999992832 | bytes 4194304 | tf_op jit(solution)/shard_map/choose/pallas_call | solution.py:199
  87.2 15.1 %all-to-all-done.a0 = bf16[32,4,3,8,1024]{4,3,2,1,0:T(8,128)(2,1)} async-done(((bf16[32,4,3,8,1024]{4,3,2,1,0:T(8,128)(2,1)}), bf16[32,4,3,8,1024]{4,3,2,1,0:T(8,128)(2,1)}, u32[]{:S(2)}, u32[]{:S(2)}) %all-to-all-start) | async-done | bytes 6291488 | tf_op jit(solution)/shard_map/all_to_all | solution.py:503
  102.3 4.1 %all-to-all-start.1 = ((bf16[32,2,3,8,1024]{4,3,2,1,0:T(8,128)(2,1)}), bf16[32,2,3,8,1024]{4,3,2,1,0:T(8,128)(2,1)S(1)}, u32[]{:S(2)}, u32[]{:S(2)}) async-start(bf16[32,2,3,8,1024]{4,3,2,1,0:T(8,128)(2,1)} %choose.1), calls=%async_computation.1 | async-start | bytes 6291456 | tf_op jit(solution)/shard_map/all_to_all | solution.py:503
  106.3 4.6 %slice_bitcast_fusion = (bf16[32,3,8,1024]{3,2,1,0:T(8,128)(2,1)}, bf16[32,3,8,1024]{3,2,1,0:T(8,128)(2,1)}, bf16[32,3,8,1024]{3,2,1,0:T(8,128)(2,1)}) fusion(bf16[32,4,3,8,1024]{4,3,2,1,0:T(8,128)(2,1)} %all-to-all-done.a0), kind=kLoop, calls=%fused_computation | loop fusion | bytes 9437184 | tf_op jit(solution)/shard_map/squeeze | solution.py:522
  111.0 2.8 %collective-permute-start.4 = (bf16[32,3,8,1024]{3,2,1,0:T(8,128)(2,1)}, bf16[32,3,8,1024]{3,2,1,0:T(8,128)(2,1)}, u32[]{:S(2)}, u32[]{:S(2)}) collective-permute-start(bf16[32,3,8,1024]{3,2,1,0:T(8,128)(2,1)} %get-tuple-element.30), channel_id=1, source_target_pairs={{0,2},{1,3},{2,0},{3,1},{4,6},{5,7},{6,4},{7,5},{8,10},{9,11},{10,... | collective-permute-start | bytes 4718600 | tf_op jit(solution)/shard_map/ppermute | solution.py:508
  113.8 0.6 collective-permute-start.5
  114.4 33.7 %all-to-all-done.1.x_ref = bf16[32,2,3,8,1024]{4,3,2,1,0:T(8,128)(2,1)S(1)} async-done(((bf16[32,2,3,8,1024]{4,3,2,1,0:T(8,128)(2,1)}), bf16[32,2,3,8,1024]{4,3,2,1,0:T(8,128)(2,1)S(1)}, u32[]{:S(2)}, u32[]{:S(2)}) %all-to-all-start.1) | async-done | bytes 3145760 | tf_op jit(solution)/shard_map/all_to_all | solution.py:503
  148.1 12.4 %filter_early.1 = bf16[32,3,2,8,1024]{4,3,2,1,0:T(8,128)(2,1)} custom-call(bf16[32,2,3,8,1024]{4,3,2,1,0:T(8,128)(2,1)S(1)} %all-to-all-done.1.x_ref, f32[16,1024]{1,0:T(8,128)} %proto_ref.1, bf16[8,128,256]{2,1,0:T(8,128)(2,1)} %constant.17.clone.refs_1_.high_ref, bf16[8,128,256]{2,1,0:T(8,128)(2,1)} %constant.18.clone.refs_2_.low_ref), custom_call_target="tpu_custom_call" | custom-call | flops 17999998976 | bytes 6291456 | tf_op jit(solution)/shard_map/filter_early/pallas_call | solution.py:353
  160.5 4.1 %all-to-all-start.2 = ((bf16[32,3,2,8,1024]{4,3,2,1,0:T(8,128)(2,1)}), bf16[32,3,2,8,1024]{4,3,2,1,0:T(8,128)(2,1)S(1)}, u32[]{:S(2)}, u32[]{:S(2)}) async-start(bf16[32,3,2,8,1024]{4,3,2,1,0:T(8,128)(2,1)} %filter_early.1), calls=%async_computation.2 | async-start | bytes 6291456 | tf_op jit(solution)/shard_map/all_to_all | solution.py:503
  164.6 18.1 %collective-permute-done.3.a1 = bf16[32,3,8,1024]{3,2,1,0:T(8,128)(2,1)} collective-permute-done((bf16[32,3,8,1024]{3,2,1,0:T(8,128)(2,1)}, bf16[32,3,8,1024]{3,2,1,0:T(8,128)(2,1)}, u32[]{:S(2)}, u32[]{:S(2)}) %collective-permute-start.3) | collective-permute-done | bytes 1572896 | tf_op jit(solution)/shard_map/ppermute | solution.py:508
  182.7 0.0 collective-permute-done.4.a2
  182.7 0.6 collective-permute-done.5.a3
  183.3 18.8 %filter_late.1 = bf16[32,3,2,8,1024]{4,3,2,1,0:T(8,128)(2,1)} custom-call(s32[4,4]{1,0:T(4,128)} %block_ref.5, s32[4]{0:T(128)} %count_ref.9, s32[2]{0:T(128)} %pad_add_fusion.place_ref, bf16[32,4,3,8,1024]{4,3,2,1,0:T(8,128)(2,1)} %all-to-all-done.a0, bf16[32,3,8,1024]{3,2,1,0:T(8,128)(2,1)} %collective-permute-done.3.a1, ...), custom_call_target="tpu_custom_call" | custom-call | flops 17999998976 | bytes 6291456 | tf_op jit(solution)/shard_map/filter_late/pallas_call | solution.py:369
  202.1 0.0 copy-start
  202.1 0.0 copy-start.1
  202.1 0.0 copy-start.2
  202.1 4.2 %all-to-all-done.2.early_ref = bf16[32,3,2,8,1024]{4,3,2,1,0:T(8,128)(2,1)S(1)} async-done(((bf16[32,3,2,8,1024]{4,3,2,1,0:T(8,128)(2,1)}), bf16[32,3,2,8,1024]{4,3,2,1,0:T(8,128)(2,1)S(1)}, u32[]{:S(2)}, u32[]{:S(2)}) %all-to-all-start.2) | async-done | bytes 3145760 | tf_op jit(solution)/shard_map/all_to_all | solution.py:503
  206.4 1.7 copy-done.4
  208.0 4.1 %all-to-all-start.3 = ((bf16[32,3,2,8,1024]{4,3,2,1,0:T(8,128)(2,1)}), bf16[32,3,2,8,1024]{4,3,2,1,0:T(8,128)(2,1)S(1)}, u32[]{:S(2)}, u32[]{:S(2)}) async-start(bf16[32,3,2,8,1024]{4,3,2,1,0:T(8,128)(2,1)} %filter_late.1), calls=%async_computation.3 | async-start | bytes 6291456 | tf_op jit(solution)/shard_map/all_to_all | solution.py:503
  212.1 5.9 %unpack_early.1.part_ref = bf16[6,2,1024,128]{3,2,1,0:T(8,128)(2,1)} custom-call(s32[4,4]{1,0:T(4,128)S(1)} %copy-done, s32[4,4]{1,0:T(4,128)S(1)} %copy-done.1, s32[4]{0:T(128)S(1)} %copy-done.2, s32[2]{0:T(128)S(1)} %copy-done.3, bf16[32,3,2,8,1024]{4,3,2,1,0:T(8,128)(2,1)} %copy-done.4), custom_call_target="tpu_custom_call" | custom-call | flops 17999998976 | bytes 6291456 | tf_op jit(solution)/shard_map/unpack_early/pallas_call | solution.py:460
  218.0 35.8 %all-to-all-done.3.late_ref = bf16[32,3,2,8,1024]{4,3,2,1,0:T(8,128)(2,1)S(1)} async-done(((bf16[32,3,2,8,1024]{4,3,2,1,0:T(8,128)(2,1)}), bf16[32,3,2,8,1024]{4,3,2,1,0:T(8,128)(2,1)S(1)}, u32[]{:S(2)}, u32[]{:S(2)}) %all-to-all-start.3) | async-done | bytes 3145760 | tf_op jit(solution)/shard_map/all_to_all | solution.py:503
  253.9 6.9 %unpack.1 = bf16[3,1,4,2,1024,128]{5,4,3,2,1,0:T(8,128)(2,1)} custom-call(s32[4,4]{1,0:T(4,128)} %start_ref.3, s32[4,4]{1,0:T(4,128)} %frames_ref.3, s32[4]{0:T(128)} %count_ref.9, s32[2]{0:T(128)} %pad_add_fusion.place_ref, bf16[6,2,1024,128]{3,2,1,0:T(8,128)(2,1)} %unpack_early.1.part_ref, bf16[32,3,2,8,1024]{4,3,2,1,0:T(8,128)(2,1)S(1)} %all-to-all-done.3.late_ref), custom_call_target="tpu_custom_call" | custom-call | tf_op jit(solution)/shard_map/unpack/pallas_call | solution.py:481
  (10 shorter events, 0.0 us)
Async XLA Ops:
  9.4 38.9 %collective-permute-start = (bf16[2,3,1024,128]{3,2,1,0:T(8,128)(2,1)}, bf16[2,3,1024,128]{3,2,1,0:T(8,128)(2,1)S(1)}, u32[]{:S(2)}, u32[]{:S(2)}) collective-permute-start(bf16[2,3,1024,128]{3,2,1,0:T(8,128)(2,1)} %get-tuple-element.19), channel_id=1, source_target_pairs={{0,1},{1,2},{2,3},{3,0},{4,5},{5,6},{6,7},{7,4},{8,9},{9,10},{10,1... | collective-permute-start | bytes 4718600 | tf_op jit(solution)/shard_map/ppermute | solution.py:508
  13.2 67.7 %collective-permute-start.1 = (bf16[2,3,1024,128]{3,2,1,0:T(8,128)(2,1)}, bf16[2,3,1024,128]{3,2,1,0:T(8,128)(2,1)S(1)}, u32[]{:S(2)}, u32[]{:S(2)}) collective-permute-start(bf16[2,3,1024,128]{3,2,1,0:T(8,128)(2,1)} %get-tuple-element.20), channel_id=1, source_target_pairs={{0,2},{1,3},{2,0},{3,1},{4,6},{5,7},{6,4},{7,5},{8,10},{9,11},{10,... | collective-permute-start | bytes 4718600 | tf_op jit(solution)/shard_map/ppermute | solution.py:508
  13.2 68.5 %collective-permute-start.2 = (bf16[2,3,1024,128]{3,2,1,0:T(8,128)(2,1)}, bf16[2,3,1024,128]{3,2,1,0:T(8,128)(2,1)}, u32[]{:S(2)}, u32[]{:S(2)}) collective-permute-start(bf16[2,3,1024,128]{3,2,1,0:T(8,128)(2,1)} %get-tuple-element.21), channel_id=1, source_target_pairs={{0,3},{1,0},{2,1},{3,2},{4,7},{5,4},{6,5},{7,6},{8,11},{9,8},{10,9... | collective-permute-start | bytes 4718600 | tf_op jit(solution)/shard_map/ppermute | solution.py:508
  15.9 86.3 %all-to-all-start = ((bf16[32,4,3,8,1024]{4,3,2,1,0:T(8,128)(2,1)}), bf16[32,4,3,8,1024]{4,3,2,1,0:T(8,128)(2,1)}, u32[]{:S(2)}, u32[]{:S(2)}) async-start(bf16[32,4,3,8,1024]{4,3,2,1,0:T(8,128)(2,1)} %get-tuple-element.17), calls=%async_computation | async-start | bytes 12582912 | tf_op jit(solution)/shard_map/all_to_all | solution.py:503
  48.3 33.4 %copy-start.5 = (bf16[2,3,1024,128]{3,2,1,0:T(8,128)(2,1)}, bf16[2,3,1024,128]{3,2,1,0:T(8,128)(2,1)S(1)}, u32[]{:S(2)}) copy-start(bf16[2,3,1024,128]{3,2,1,0:T(8,128)(2,1)S(1)} %collective-permute-done.a1) | copy-start | bytes 4718596
  80.8 1.2 copy-start.6
  102.3 45.8 %all-to-all-start.1 = ((bf16[32,2,3,8,1024]{4,3,2,1,0:T(8,128)(2,1)}), bf16[32,2,3,8,1024]{4,3,2,1,0:T(8,128)(2,1)S(1)}, u32[]{:S(2)}, u32[]{:S(2)}) async-start(bf16[32,2,3,8,1024]{4,3,2,1,0:T(8,128)(2,1)} %choose.1), calls=%async_computation.1 | async-start | bytes 6291456 | tf_op jit(solution)/shard_map/all_to_all | solution.py:503
  111.0 71.7 %collective-permute-start.3 = (bf16[32,3,8,1024]{3,2,1,0:T(8,128)(2,1)}, bf16[32,3,8,1024]{3,2,1,0:T(8,128)(2,1)}, u32[]{:S(2)}, u32[]{:S(2)}) collective-permute-start(bf16[32,3,8,1024]{3,2,1,0:T(8,128)(2,1)} %get-tuple-element.31), channel_id=1, source_target_pairs={{0,1},{1,2},{2,3},{3,0},{4,5},{5,6},{6,7},{7,4},{8,9},{9,10},{10,1... | collective-permute-start | bytes 4718600 | tf_op jit(solution)/shard_map/ppermute | solution.py:508
  111.0 71.7 %collective-permute-start.4 = (bf16[32,3,8,1024]{3,2,1,0:T(8,128)(2,1)}, bf16[32,3,8,1024]{3,2,1,0:T(8,128)(2,1)}, u32[]{:S(2)}, u32[]{:S(2)}) collective-permute-start(bf16[32,3,8,1024]{3,2,1,0:T(8,128)(2,1)} %get-tuple-element.30), channel_id=1, source_target_pairs={{0,2},{1,3},{2,0},{3,1},{4,6},{5,7},{6,4},{7,5},{8,10},{9,11},{10,... | collective-permute-start | bytes 4718600 | tf_op jit(solution)/shard_map/ppermute | solution.py:508
  113.8 69.5 %collective-permute-start.5 = (bf16[32,3,8,1024]{3,2,1,0:T(8,128)(2,1)}, bf16[32,3,8,1024]{3,2,1,0:T(8,128)(2,1)}, u32[]{:S(2)}, u32[]{:S(2)}) collective-permute-start(bf16[32,3,8,1024]{3,2,1,0:T(8,128)(2,1)} %get-tuple-element.29), channel_id=1, source_target_pairs={{0,3},{1,0},{2,1},{3,2},{4,7},{5,4},{6,5},{7,6},{8,11},{9,8},{10,9... | collective-permute-start | bytes 4718600 | tf_op jit(solution)/shard_map/ppermute | solution.py:508
  160.5 45.8 %all-to-all-start.2 = ((bf16[32,3,2,8,1024]{4,3,2,1,0:T(8,128)(2,1)}), bf16[32,3,2,8,1024]{4,3,2,1,0:T(8,128)(2,1)S(1)}, u32[]{:S(2)}, u32[]{:S(2)}) async-start(bf16[32,3,2,8,1024]{4,3,2,1,0:T(8,128)(2,1)} %filter_early.1), calls=%async_computation.2 | async-start | bytes 6291456 | tf_op jit(solution)/shard_map/all_to_all | solution.py:503
  202.1 10.0 %copy-start = (s32[4,4]{1,0:T(4,128)S(1)}, s32[4,4]{1,0:T(4,128)}, u32[]{:S(2)}) copy-start(s32[4,4]{1,0:T(4,128)} %start_ref.3) | copy-start | bytes 196
  202.1 10.0 %copy-start.1 = (s32[4,4]{1,0:T(4,128)S(1)}, s32[4,4]{1,0:T(4,128)}, u32[]{:S(2)}) copy-start(s32[4,4]{1,0:T(4,128)} %frames_ref.3) | copy-start | bytes 196
  202.1 10.0 %copy-start.2 = (s32[4]{0:T(128)S(1)}, s32[4]{0:T(128)}, u32[]{:S(2)}) copy-start(s32[4]{0:T(128)} %count_ref.9) | copy-start | bytes 52
  202.1 10.0 %copy-start.3 = (s32[2]{0:T(128)S(1)}, s32[2]{0:T(128)}, u32[]{:S(2)}) copy-start(s32[2]{0:T(128)} %pad_add_fusion.place_ref) | copy-start | bytes 28
  206.4 1.7 copy-start.4
  208.0 45.8 %all-to-all-start.3 = ((bf16[32,3,2,8,1024]{4,3,2,1,0:T(8,128)(2,1)}), bf16[32,3,2,8,1024]{4,3,2,1,0:T(8,128)(2,1)S(1)}, u32[]{:S(2)}, u32[]{:S(2)}) async-start(bf16[32,3,2,8,1024]{4,3,2,1,0:T(8,128)(2,1)} %filter_late.1), calls=%async_computation.3 | async-start | bytes 6291456 | tf_op jit(solution)/shard_map/all_to_all | solution.py:503
